TPU v7x, 32 devices: a whole 2x2x4 slice. The times are simulated.
32 devices in a mesh: ctx: 16 (over z, y, x), wa: 2 (over core).
Axes of the slice: x: 2, y: 2, z: 4, core: 2. Of those that a mesh axis runs over, the one named last changes fastest.
Arguments:
- tokens: bfloat16 [32768, 768], P(('ctx', 'wa')), may hold values from -6 to 6
- seq_ids: int32 [256], replicated, may hold values from 0 to 1, as said below
- w_qkv: bfloat16 [2, 768, 2304], P(None, ('ctx', 'wa')), may hold values from -0.21875 to 0.21875
- w_out: bfloat16 [2, 768, 768], P(None, ('ctx', 'wa')), may hold values from -1.75 to 1.75
- w_up: bfloat16 [2, 768, 3072], P(None, ('ctx', 'wa')), may hold values from -0.21875 to 0.21875
- w_down: bfloat16 [2, 3072, 768], P(None, ('ctx', 'wa')), may hold values from -0.109375 to 0.109375
- biases: bfloat16 [2, 6, 768], P(None, None, ('ctx', 'wa')), may hold values from -1.1953125 to 1.1953125
- up_bias: bfloat16 [2, 3072], P(None, ('ctx', 'wa')), may hold values from -1.1953125 to 1.1953125
- norm_gains: bfloat16 [2, 2, 768], P(None, None, ('ctx', 'wa')), may hold values from 0.5 to 1.5
- pos_table: bfloat16 [128, 768], P(None, ('ctx', 'wa')), may hold values from -3 to 3
- cotangent: bfloat16 [32768, 768], P(('ctx', 'wa')), may hold values from -6 to 6
Outputs:
- layer_out: bfloat16 [32768, 768], P(('ctx', 'wa'))
- grad_tokens: bfloat16 [32768, 768], P(('ctx', 'wa'))
- grad_w_qkv: float32 [2, 768, 2304], P(None, ('ctx', 'wa'))
- grad_w_out: float32 [2, 768, 768], P(None, ('ctx', 'wa'))
- grad_w_up: float32 [2, 768, 3072], P(None, ('ctx', 'wa'))
- grad_w_down: float32 [2, 3072, 768], P(None, ('ctx', 'wa'))
- grad_biases: float32 [2, 6, 768], P(None, None, ('ctx', 'wa'))
- grad_up_bias: float32 [2, 3072], P(None, ('ctx', 'wa'))
- grad_norm_gains: float32 [2, 2, 768], P(None, None, ('ctx', 'wa'))
- grad_pos_table: float32 [128, 768], P(None, ('ctx', 'wa'))
Inputs may be any that keep to these rules, and one draw needn't show every extreme that they name: `seq_ids`: every sequence holds exactly 128 segments, spread over the segment slots in any order.
All inputs are finite; a program needn't handle non-finite values.
Results may differ from a plain program's by a relative error of at most 0.023.
Values may be sent and summed in bfloat16 or wider, within the bound.
No kernel may reach another device: no remote copies, remote signals or barrier semaphores. Data moves between devices by JAX's collectives and lax.ppermute only.
A program may use at most 256 MiB of HBM per device.

v0:
```python
from functools import partial

import jax
import jax.numpy as jnp
from jax import lax
from jax.sharding import PartitionSpec as P

HDIM = 64
SEG = 128


def layer_norm(values, weight, offset):
    center = values - jnp.mean(values, axis=-1, keepdims=True)
    spread = jnp.mean(center * center, axis=-1, keepdims=True)
    return center * lax.rsqrt(spread + 1e-05) * weight + offset


def gelu_exact(values):
    return 0.5 * values * (1.0 + lax.erf(values * 0.7071067811865476))


def column_sums(values):
    return jnp.sum(values.astype(jnp.float32), axis=0)


def segment_layout(queries):
    groups = queries.shape[0] // SEG
    head_count = queries.shape[1] // HDIM
    return (groups, SEG, head_count, HDIM)


def segment_scores(queries, key_rows):
    blocked = segment_layout(queries)
    return jnp.einsum(
        "gqhd,gkhd->ghqk",
        queries.reshape(blocked),
        key_rows.reshape(blocked),
        preferred_element_type=jnp.float32,
    ) * HDIM ** (-0.5)


def segment_forward(queries, key_rows, value_rows):
    blocked = segment_layout(queries)
    scores = segment_scores(queries, key_rows)
    row_peak = jnp.max(scores, axis=-1, keepdims=True)
    raised = jnp.exp(scores - row_peak)
    totals = jnp.sum(raised, axis=-1, keepdims=True)
    probability = (raised / totals).astype(jnp.bfloat16)
    context = jnp.einsum(
        "ghqk,gkhd->gqhd",
        probability,
        value_rows.reshape(blocked),
        preferred_element_type=jnp.float32,
    )
    return (context.reshape(queries.shape), row_peak + jnp.log(totals))


def segment_backward(grad_context, queries, key_rows, value_rows, attend_state):
    blocked = segment_layout(queries)
    probability = jnp.exp(segment_scores(queries, key_rows) - attend_state)
    grad_prob = jnp.einsum(
        "gqhd,gkhd->ghqk",
        grad_context.reshape(blocked),
        value_rows.reshape(blocked),
        preferred_element_type=jnp.float32,
    )
    grad_scores = (
        probability * (grad_prob - jnp.sum(grad_prob * probability, axis=-1, keepdims=True))
    ).astype(jnp.bfloat16)
    grad_q = jnp.einsum(
        "ghqk,gkhd->gqhd",
        grad_scores,
        key_rows.reshape(blocked),
        preferred_element_type=jnp.float32,
    ) * HDIM ** (-0.5)
    grad_k = jnp.einsum(
        "ghqk,gqhd->gkhd", grad_scores, queries.reshape(blocked), preferred_element_type=jnp.float32
    ) * HDIM ** (-0.5)
    grad_v = jnp.einsum(
        "ghqk,gqhd->gkhd",
        probability.astype(jnp.bfloat16),
        grad_context.reshape(blocked),
        preferred_element_type=jnp.float32,
    )
    return (
        grad_q.reshape(queries.shape),
        grad_k.reshape(queries.shape),
        grad_v.reshape(queries.shape),
    )


def split_heads(values):
    return values.reshape(values.shape[0], values.shape[1] // HDIM, HDIM)


def cross_scores(queries, all_keys, allowed):
    scores = jnp.einsum(
        "qhd,khd->hqk",
        split_heads(queries),
        split_heads(all_keys),
        preferred_element_type=jnp.float32,
    ) * HDIM ** (-0.5)
    return jnp.where(allowed[None], scores, -1e30)


def cross_forward(queries, key_rows, value_rows, local_ids, seq_ids):
    all_keys, all_values = (
        lax.all_gather(key_rows, ("ctx", "wa"), axis=0, tiled=True),
        lax.all_gather(value_rows, ("ctx", "wa"), axis=0, tiled=True),
    )
    allowed = local_ids[:, None] == seq_ids[None, :]
    scores = cross_scores(queries, all_keys, allowed)
    row_peak = jnp.max(scores, axis=-1, keepdims=True)
    raised = jnp.exp(scores - row_peak)
    totals = jnp.sum(raised, axis=-1, keepdims=True)
    probability = (raised / totals).astype(jnp.bfloat16)
    context = jnp.einsum(
        "hqk,khd->qhd", probability, split_heads(all_values), preferred_element_type=jnp.float32
    )
    return (context.reshape(queries.shape), (row_peak + jnp.log(totals), all_keys, all_values))


def cross_backward(grad_context, queries, key_rows, value_rows, attend_state, local_ids, seq_ids):
    saved_lse, all_keys, all_values = attend_state
    allowed = local_ids[:, None] == seq_ids[None, :]
    probability = jnp.exp(cross_scores(queries, all_keys, allowed) - saved_lse)
    grad_prob = jnp.einsum(
        "qhd,khd->hqk",
        split_heads(grad_context),
        split_heads(all_values),
        preferred_element_type=jnp.float32,
    )
    prob_dot = jnp.sum(grad_prob * probability, axis=-1, keepdims=True)
    grad_scores = (probability * (grad_prob - prob_dot)).astype(jnp.bfloat16)
    grad_q = jnp.einsum(
        "hqk,khd->qhd", grad_scores, split_heads(all_keys), preferred_element_type=jnp.float32
    ) * HDIM ** (-0.5)
    part_k = jnp.einsum(
        "hqk,qhd->khd", grad_scores, split_heads(queries), preferred_element_type=jnp.float32
    ) * HDIM ** (-0.5)
    part_v = jnp.einsum(
        "hqk,qhd->khd",
        probability.astype(jnp.bfloat16),
        split_heads(grad_context),
        preferred_element_type=jnp.float32,
    )
    grad_k, grad_v = (
        lax.psum_scatter(
            part_k.reshape(part_k.shape[0], -1), ("ctx", "wa"), scatter_dimension=0, tiled=True
        ),
        lax.psum_scatter(
            part_v.reshape(part_v.shape[0], -1), ("ctx", "wa"), scatter_dimension=0, tiled=True
        ),
    )
    return (grad_q.reshape(queries.shape), grad_k, grad_v)


def block_forward(hidden, weights, attend):
    w_qkv, w_out, w_up, w_down, biases, up_bias, norm_gains = weights
    model_width = w_out.shape[0]
    hidden_low = hidden.astype(jnp.bfloat16)
    projected = jnp.dot(hidden_low, w_qkv, preferred_element_type=jnp.float32)
    queries = (projected[:, :model_width] + biases[0]).astype(jnp.bfloat16)
    key_rows = projected[:, model_width : 2 * model_width].astype(jnp.bfloat16)
    value_rows = (projected[:, 2 * model_width :] + biases[1]).astype(jnp.bfloat16)
    context, attend_state = attend(queries, key_rows, value_rows)
    context_low = context.astype(jnp.bfloat16)
    attn_out = jnp.dot(context_low, w_out, preferred_element_type=jnp.float32) + biases[2]
    normed, first_norm = jax.vjp(
        layer_norm,
        hidden + attn_out,
        norm_gains[0].astype(jnp.float32),
        biases[3].astype(jnp.float32),
    )
    normed_low = normed.astype(jnp.bfloat16)
    before = jnp.dot(normed_low, w_up, preferred_element_type=jnp.float32) + up_bias
    active, gelu_back = jax.vjp(gelu_exact, before)
    active_low = active.astype(jnp.bfloat16)
    ffn_out = jnp.dot(active_low, w_down, preferred_element_type=jnp.float32) + biases[4]
    result, second_norm = jax.vjp(
        layer_norm,
        normed + ffn_out,
        norm_gains[1].astype(jnp.float32),
        biases[5].astype(jnp.float32),
    )
    stored = (
        hidden_low,
        queries,
        key_rows,
        value_rows,
        attend_state,
        context_low,
        normed_low,
        active_low,
        first_norm,
        gelu_back,
        second_norm,
    )
    return (result, stored)


def block_backward(grad_result, stored, weights, attend_back):
    w_qkv, w_out, w_up, w_down, biases, up_bias, norm_gains = weights
    (
        hidden_low,
        queries,
        key_rows,
        value_rows,
        attend_state,
        context_low,
        normed_low,
        active_low,
        first_norm,
        gelu_back,
        second_norm,
    ) = stored
    model_width = w_out.shape[0]
    grad_second, gain_second, shift_second = second_norm(grad_result)
    grad_ffn = grad_second.astype(jnp.bfloat16)
    grad_wdown = jnp.einsum("ti,to->io", active_low, grad_ffn, preferred_element_type=jnp.float32)
    grad_active = jnp.dot(grad_ffn, w_down.T, preferred_element_type=jnp.float32)
    (grad_before,) = gelu_back(grad_active)
    grad_before_low = grad_before.astype(jnp.bfloat16)
    grad_wup = jnp.einsum(
        "ti,to->io", normed_low, grad_before_low, preferred_element_type=jnp.float32
    )
    grad_normed = grad_second + jnp.dot(grad_before_low, w_up.T, preferred_element_type=jnp.float32)
    grad_first, gain_first, shift_first = first_norm(grad_normed)
    grad_attn = grad_first.astype(jnp.bfloat16)
    grad_wout = jnp.einsum("ti,to->io", context_low, grad_attn, preferred_element_type=jnp.float32)
    grad_context = jnp.dot(grad_attn, w_out.T, preferred_element_type=jnp.float32).astype(
        jnp.bfloat16
    )
    grad_q, grad_k, grad_v = attend_back(grad_context, queries, key_rows, value_rows, attend_state)
    grad_qkv = jnp.concatenate([grad_q, grad_k, grad_v], axis=1).astype(jnp.bfloat16)
    grad_wqkv = jnp.einsum("ti,to->io", hidden_low, grad_qkv, preferred_element_type=jnp.float32)
    grad_hidden = grad_first + jnp.dot(grad_qkv, w_qkv.T, preferred_element_type=jnp.float32)
    grad_bias = jnp.stack(
        [
            column_sums(grad_qkv[:, :model_width]),
            column_sums(grad_qkv[:, 2 * model_width :]),
            column_sums(grad_attn),
            shift_first,
            column_sums(grad_ffn),
            shift_second,
        ]
    )
    grad_gain = jnp.stack([gain_first, gain_second])
    return (
        (
            grad_wqkv,
            grad_wout,
            grad_wup,
            grad_wdown,
            grad_bias,
            column_sums(grad_before_low),
            grad_gain,
        ),
        grad_hidden,
    )


def place_table(row_ids, row_slots, seq_ids, table_rows):
    all_slots = jnp.arange(seq_ids.shape[0], dtype=jnp.int32)
    earlier = (seq_ids[None, :] == row_ids[:, None]) & (all_slots[None, :] < row_slots[:, None])
    places = jnp.sum(earlier.astype(jnp.int32), axis=1)
    return (places[:, None] == table_rows[None, :]).astype(jnp.float32)


def shards(
    tokens, seq_ids, w_qkv, w_out, w_up, w_down, biases, up_bias, norm_gains, pos_table, cotangent
):
    rows_here = tokens.shape[0]
    segs_here = rows_here // SEG
    model_width = tokens.shape[1]
    first_seg = lax.axis_index(("ctx", "wa")) * segs_here
    local_ids = lax.dynamic_slice_in_dim(seq_ids, first_seg, segs_here)
    table_rows = jnp.arange(pos_table.shape[0], dtype=jnp.int32)
    local_slots = first_seg + jnp.arange(segs_here, dtype=jnp.int32)
    onehot = place_table(local_ids, local_slots, seq_ids, table_rows)
    first_weights = (
        lax.all_gather(w_qkv[0], ("ctx", "wa"), axis=0, tiled=True),
        lax.all_gather(w_out[0], ("ctx", "wa"), axis=0, tiled=True),
        lax.all_gather(w_up[0], ("ctx", "wa"), axis=0, tiled=True),
        lax.all_gather(w_down[0], ("ctx", "wa"), axis=0, tiled=True),
        lax.all_gather(biases[0], ("ctx", "wa"), axis=1, tiled=True),
        lax.all_gather(up_bias[0], ("ctx", "wa"), axis=0, tiled=True),
        lax.all_gather(norm_gains[0], ("ctx", "wa"), axis=1, tiled=True),
    )
    segment_out, segment_stored = block_forward(
        tokens.astype(jnp.float32), first_weights, segment_forward
    )
    second_weights = (
        lax.all_gather(w_qkv[1], ("ctx", "wa"), axis=0, tiled=True),
        lax.all_gather(w_out[1], ("ctx", "wa"), axis=0, tiled=True),
        lax.all_gather(w_up[1], ("ctx", "wa"), axis=0, tiled=True),
        lax.all_gather(w_down[1], ("ctx", "wa"), axis=0, tiled=True),
        lax.all_gather(biases[1], ("ctx", "wa"), axis=1, tiled=True),
        lax.all_gather(up_bias[1], ("ctx", "wa"), axis=0, tiled=True),
        lax.all_gather(norm_gains[1], ("ctx", "wa"), axis=1, tiled=True),
        lax.all_gather(pos_table, ("ctx", "wa"), axis=1, tiled=True),
    )
    blocked_out = segment_out.reshape(segs_here, SEG, model_width)
    cross_in = blocked_out[:, 0, :] + jnp.dot(
        onehot, second_weights[7].astype(jnp.float32), precision=lax.Precision.HIGHEST
    )
    grad_out = cotangent.astype(jnp.float32).reshape(segs_here, SEG, model_width)
    cross_out, cross_stored = block_forward(
        cross_in, second_weights[:7], partial(cross_forward, local_ids=local_ids, seq_ids=seq_ids)
    )
    layer_out = (
        blocked_out.at[:, 0, :].set(cross_out).reshape(rows_here, model_width).astype(jnp.bfloat16)
    )
    first_back = (
        lax.all_gather(w_qkv[0], ("ctx", "wa"), axis=0, tiled=True),
        lax.all_gather(w_out[0], ("ctx", "wa"), axis=0, tiled=True),
        lax.all_gather(w_up[0], ("ctx", "wa"), axis=0, tiled=True),
        lax.all_gather(w_down[0], ("ctx", "wa"), axis=0, tiled=True),
        lax.all_gather(biases[0], ("ctx", "wa"), axis=1, tiled=True),
        lax.all_gather(up_bias[0], ("ctx", "wa"), axis=0, tiled=True),
        lax.all_gather(norm_gains[0], ("ctx", "wa"), axis=1, tiled=True),
    )
    second_back = (
        lax.all_gather(w_qkv[1], ("ctx", "wa"), axis=0, tiled=True),
        lax.all_gather(w_out[1], ("ctx", "wa"), axis=0, tiled=True),
        lax.all_gather(w_up[1], ("ctx", "wa"), axis=0, tiled=True),
        lax.all_gather(w_down[1], ("ctx", "wa"), axis=0, tiled=True),
        lax.all_gather(biases[1], ("ctx", "wa"), axis=1, tiled=True),
        lax.all_gather(up_bias[1], ("ctx", "wa"), axis=0, tiled=True),
        lax.all_gather(norm_gains[1], ("ctx", "wa"), axis=1, tiled=True),
    )
    second_grads, grad_cross_in = block_backward(
        grad_out[:, 0, :],
        cross_stored,
        second_back,
        partial(cross_backward, local_ids=local_ids, seq_ids=seq_ids),
    )
    grad_places = jnp.dot(onehot.T, grad_cross_in, precision=lax.Precision.HIGHEST)
    summed = (
        lax.psum_scatter(second_grads[0], ("ctx", "wa"), scatter_dimension=0, tiled=True),
        lax.psum_scatter(second_grads[1], ("ctx", "wa"), scatter_dimension=0, tiled=True),
        lax.psum_scatter(second_grads[2], ("ctx", "wa"), scatter_dimension=0, tiled=True),
        lax.psum_scatter(second_grads[3], ("ctx", "wa"), scatter_dimension=0, tiled=True),
        lax.psum_scatter(second_grads[4].T, ("ctx", "wa"), scatter_dimension=0, tiled=True),
        lax.psum_scatter(second_grads[5], ("ctx", "wa"), scatter_dimension=0, tiled=True),
        lax.psum_scatter(second_grads[6].T, ("ctx", "wa"), scatter_dimension=0, tiled=True),
        lax.psum_scatter(grad_places.T, ("ctx", "wa"), scatter_dimension=0, tiled=True),
    )
    second_shares = (
        summed[0],
        summed[1],
        summed[2],
        summed[3],
        summed[4].T,
        summed[5],
        summed[6].T,
        summed[7].T,
    )
    grad_segment = grad_out.at[:, 0, :].set(grad_cross_in).reshape(rows_here, model_width)
    first_grads, grad_hidden = block_backward(
        grad_segment, segment_stored, first_back, segment_backward
    )
    first_summed = (
        lax.psum_scatter(first_grads[0], ("ctx", "wa"), scatter_dimension=0, tiled=True),
        lax.psum_scatter(first_grads[1], ("ctx", "wa"), scatter_dimension=0, tiled=True),
        lax.psum_scatter(first_grads[2], ("ctx", "wa"), scatter_dimension=0, tiled=True),
        lax.psum_scatter(first_grads[3], ("ctx", "wa"), scatter_dimension=0, tiled=True),
        lax.psum_scatter(first_grads[4].T, ("ctx", "wa"), scatter_dimension=0, tiled=True),
        lax.psum_scatter(first_grads[5], ("ctx", "wa"), scatter_dimension=0, tiled=True),
        lax.psum_scatter(first_grads[6].T, ("ctx", "wa"), scatter_dimension=0, tiled=True),
    )
    first_shares = (
        first_summed[0],
        first_summed[1],
        first_summed[2],
        first_summed[3],
        first_summed[4].T,
        first_summed[5],
        first_summed[6].T,
    )
    return (
        layer_out,
        grad_hidden.astype(jnp.bfloat16),
        jnp.stack([first_shares[0], second_shares[0]]),
        jnp.stack([first_shares[1], second_shares[1]]),
        jnp.stack([first_shares[2], second_shares[2]]),
        jnp.stack([first_shares[3], second_shares[3]]),
        jnp.stack([first_shares[4], second_shares[4]]),
        jnp.stack([first_shares[5], second_shares[5]]),
        jnp.stack([first_shares[6], second_shares[6]]),
        second_shares[7],
    )


def solution(mesh):
    in_specs = (
        P(("ctx", "wa"), None),
        P(),
        P(None, ("ctx", "wa"), None),
        P(None, ("ctx", "wa"), None),
        P(None, ("ctx", "wa"), None),
        P(None, ("ctx", "wa"), None),
        P(None, None, ("ctx", "wa")),
        P(None, ("ctx", "wa")),
        P(None, None, ("ctx", "wa")),
        P(None, ("ctx", "wa")),
        P(("ctx", "wa"), None),
    )
    out_specs = (
        P(("ctx", "wa"), None),
        P(("ctx", "wa"), None),
        P(None, ("ctx", "wa"), None),
        P(None, ("ctx", "wa"), None),
        P(None, ("ctx", "wa"), None),
        P(None, ("ctx", "wa"), None),
        P(None, None, ("ctx", "wa")),
        P(None, ("ctx", "wa")),
        P(None, None, ("ctx", "wa")),
        P(None, ("ctx", "wa")),
    )
    return jax.shard_map(shards, mesh=mesh, in_specs=in_specs, out_specs=out_specs, check_vma=False)
```

profile of v0, /device:TPU:0, one launch (start us, length us, event | category | flops | bytes accessed | tf_op | source)
XLA Modules:
  0.0 2038.0 jit_solution(10453540245337547517)
XLA Ops:
  17.6 44.8 %all-gather.1 = bf16[1,6,768]{1,0,2:T(2,128)(2,1)S(1)} all-gather(bf16[1,6,24]{1,0,2:T(2,128)(2,1)S(1)} %copy.184), channel_id=3, replica_groups=mesh['ctx'=16,'wa'=2] {'ctx','wa'}, dimensions={2}, use_global_device_ids=true | all-gather | bytes 9504 | tf_op jit(solution)/shard_map/all_gather | solution.py:286
  62.4 13.5 fusion.107
  76.4 37.1 %all-reduce.10 = (bf16[3072]{0:T(1024)(128)(2,1)S(1)}, bf16[3072]{0:T(1024)(128)(2,1)S(1)}) all-reduce(bf16[3072]{0:T(1024)(128)(2,1)S(1)} %dynamic-update-slice.6, bf16[3072]{0:T(1024)(128)(2,1)S(1)} %dynamic-update-slice.7), channel_id=7, replica_groups=mesh['ctx'=16,'wa'=2] {'ctx','wa'}, use_global_device_ids=true, to_apply=%add | all-reduce | flops 6144 | bytes 24576
  113.7 41.8 %all-gather.3 = bf16[1,2,768]{1,0,2:T(2,128)(2,1)S(1)} all-gather(bf16[1,2,24]{1,0,2:T(2,128)(2,1)S(1)} %copy.185), channel_id=5, replica_groups=mesh['ctx'=16,'wa'=2] {'ctx','wa'}, dimensions={2}, use_global_device_ids=true | all-gather | bytes 3168 | tf_op jit(solution)/shard_map/all_gather | solution.py:288
  155.5 4.6 fusion.108
  161.1 37.7 %all_gather.66 = bf16[128,768]{0,1:T(8,128)(2,1)S(1)} all-gather(bf16[128,24]{0,1:T(8,128)(2,1)S(1)} %copy-done.79), channel_id=1, replica_groups=mesh['ctx'=16,'wa'=2] {'ctx','wa'}, dimensions={1}, use_global_device_ids=true | all-gather | bytes 202752 | tf_op jit(solution)/shard_map/all_gather | solution.py:301
  198.9 39.2 %all-gather.8 = bf16[1,6,768]{1,0,2:T(2,128)(2,1)S(1)} all-gather(bf16[1,6,24]{1,0,2:T(2,128)(2,1)S(1)} %copy.187), channel_id=10, replica_groups=mesh['ctx'=16,'wa'=2] {'ctx','wa'}, dimensions={2}, use_global_device_ids=true | all-gather | bytes 9504 | tf_op jit(solution)/shard_map/all_gather | solution.py:298
  238.2 14.0 fusion.99
  252.9 38.7 %all-gather.10 = bf16[1,2,768]{1,0,2:T(2,128)(2,1)S(1)} all-gather(bf16[1,2,24]{1,0,2:T(2,128)(2,1)S(1)} %copy.188), channel_id=12, replica_groups=mesh['ctx'=16,'wa'=2] {'ctx','wa'}, dimensions={2}, use_global_device_ids=true | all-gather | bytes 3168 | tf_op jit(solution)/shard_map/all_gather | solution.py:300
  291.6 4.6 fusion.100
  297.7 5.8 fusion.23
  307.3 1.8 copy.192
  310.8 1.8 copy.193
  312.7 3.2 copy.126
  323.2 2.4 copy.133
  325.6 3.9 fusion.167
  330.0 12.8 multiply_convert_fusion
  342.8 9.0 fusion.168
  355.5 2.6 fusion.19
  358.1 39.4 %all_gather.70 = bf16[256,768]{1,0:T(8,128)(2,1)S(1)} all-gather(bf16[8,768]{1,0:T(8,128)(2,1)S(1)} %slice.315), channel_id=1, replica_groups=mesh['ctx'=16,'wa'=2] {'ctx','wa'}, dimensions={0}, use_global_device_ids=true | all-gather | bytes 405504 | tf_op jit(solution)/shard_map/all_gather | solution.py:108
  397.8 38.5 %all_gather.69 = bf16[256,768]{1,0:T(8,128)(2,1)S(1)} all-gather(bf16[8,768]{1,0:T(8,128)(2,1)S(1)} %get-tuple-element.137), channel_id=1, replica_groups=mesh['ctx'=16,'wa'=2] {'ctx','wa'}, dimensions={0}, use_global_device_ids=true | all-gather | bytes 405504 | tf_op jit(solution)/shard_map/all_gather | solution.py:109
  439.3 10.1 all-gather.35.cloned.1.call-done
  449.4 3.2 fusion.25
  452.6 62.9 %all-gather.37.cloned.1.call-done = bf16[1,3072,768]{2,1,0:T(8,128)(2,1)} async-done(((bf16[1,96,768]{2,1,0:T(8,128)(2,1)}), bf16[1,3072,768]{2,1,0:T(8,128)(2,1)}) %all-gather.37.cloned.1.call-update) | async-done | bytes 4718608 | tf_op jit(solution)/shard_map/all_gather | solution.py:297
  515.5 3.3 fusion.171
  521.2 1.9 convert_reduce_fusion.5
  523.1 2.1 multiply_reduce_fusion.9
  539.1 84.5 %reduce-scatter.22.cloned.1.call-done = f32[8,768]{1,0:T(8,128)} async-done(((f32[256,768]{1,0:T(8,128)}), f32[8,768]{1,0:T(8,128)}) %reduce-scatter.22.cloned.1.call-update) | async-done | bytes 24592 | tf_op jit(solution)/shard_map/reduce_scatter | solution.py:148
  624.3 98.8 %reduce-scatter.24.cloned.1.call-done = f32[8,768]{1,0:T(8,128)} async-done(((f32[256,768]{1,0:T(8,128)}), f32[8,768]{1,0:T(8,128)}) %reduce-scatter.24.cloned.1.call-update) | async-done | bytes 24592 | tf_op jit(solution)/shard_map/reduce_scatter | solution.py:151
  723.9 3.0 fusion.76
  727.2 4.6 fusion.32
  731.9 2.0 fusion.158
  734.7 15.3 convert_reduce_fusion
  750.1 6.1 multiply_reduce_fusion.2
  759.8 2.6 convolution_convert_fusion
  762.4 2.7 copy.151
  767.0 5.2 fusion.53
  772.2 2.4 multiply_reduce_fusion
  777.1 2.0 multiply_convert_fusion.1
  779.1 3.5 fusion.51
  787.6 1.9 fusion.172
  789.6 5.0 fusion.47
  794.8 3.7 fusion.52
  801.7 2.1 copy-done.35
  803.8 5.8 convolution_bitcast_fusion
  809.7 8.1 copy.172
  818.5 4.0 fusion.133
  823.4 5.1 fusion.153
  829.9 10.2 fusion.173
  840.9 5.2 fusion.150
  848.0 10.7 fusion.154
  863.4 9.5 add_convert_fusion.1
  872.8 36.7 %all-reduce.13.cloned.1.call-done = (f32[768,6]{0,1:T(8,128)}, f32[768,6]{0,1:T(8,128)}, f32[3072]{0:T(1024)}, f32[3072]{0:T(1024)}, f32[768,2]{0,1:T(2,128)}, /*index=5*/f32[768,2]{0,1:T(2,128)}) async-done(((f32[768,6]{0,1:T(8,128)}, f32[768,6]{0,1:T(8,128)}, f32[3072]{0:T(1024)}, f32[3072]{0:T(1024)}, f32[768,2]{0,1:T(2,128)}, /*index=5*/f32[768,2]{0,1:T(2,128)}), (f32[768,6]{0,1:T(8,128)}, ...) | async-done | bytes 73744
  913.7 101.4 %reduce-scatter.28.cloned.1.call-done = f32[24,768]{1,0:T(8,128)} async-done(((f32[768,768]{1,0:T(8,128)}), f32[24,768]{1,0:T(8,128)}) %reduce-scatter.28.cloned.1.call-update) | async-done | bytes 73744 | tf_op jit(solution)/shard_map/reduce_scatter | solution.py:341
  1015.1 104.1 %reduce-scatter.26.cloned.1.call-done = f32[24,768]{1,0:T(8,128)} async-done(((f32[768,768]{1,0:T(8,128)}), f32[24,768]{1,0:T(8,128)}) %reduce-scatter.26.cloned.1.call-update) | async-done | bytes 73744 | tf_op jit(solution)/shard_map/reduce_scatter | solution.py:365
  1120.8 122.1 %reduce-scatter.38.cloned.1.call-done = f32[24,2304]{1,0:T(8,128)} async-done(((f32[768,2304]{1,0:T(8,128)}), f32[24,2304]{1,0:T(8,128)}) %reduce-scatter.38.cloned.1.call-update) | async-done | bytes 221200
  1244.6 123.0 %reduce-scatter.40.cloned.1.call-done = f32[24,2304]{1,0:T(8,128)} async-done(((f32[768,2304]{1,0:T(8,128)}), f32[24,2304]{1,0:T(8,128)}) %reduce-scatter.40.cloned.1.call-update) | async-done | bytes 221200
  1370.1 138.1 %reduce-scatter.36.cloned.1.call-done = f32[96,768]{1,0:T(8,128)} async-done(((f32[3072,768]{1,0:T(8,128)}), f32[96,768]{1,0:T(8,128)}) %reduce-scatter.36.cloned.1.call-update) | async-done | bytes 294928 | tf_op jit(solution)/shard_map/reduce_scatter | solution.py:343
  1508.1 141.3 %reduce-scatter.34.cloned.1.call-done = f32[96,768]{1,0:T(8,128)} async-done(((f32[3072,768]{1,0:T(8,128)}), f32[96,768]{1,0:T(8,128)}) %reduce-scatter.34.cloned.1.call-update) | async-done | bytes 294928 | tf_op jit(solution)/shard_map/reduce_scatter | solution.py:367
  1649.5 1.9 pad_maximum_fusion.1
  1651.4 138.5 %reduce-scatter.32.cloned.1.call-done = f32[24,3072]{1,0:T(8,128)} async-done(((f32[768,3072]{1,0:T(8,128)}), f32[24,3072]{1,0:T(8,128)}) %reduce-scatter.32.cloned.1.call-update) | async-done | bytes 294928 | tf_op jit(solution)/shard_map/reduce_scatter | solution.py:342
  1789.9 141.4 %reduce-scatter.30.cloned.1.call-done = f32[24,3072]{1,0:T(8,128)} async-done(((f32[768,3072]{1,0:T(8,128)}), f32[24,3072]{1,0:T(8,128)}) %reduce-scatter.30.cloned.1.call-update) | async-done | bytes 294928 | tf_op jit(solution)/shard_map/reduce_scatter | solution.py:366
  1931.2 1.9 pad_maximum_fusion
  1933.2 97.5 %reduce-scatter.42.cloned.1.call-done = f32[24,128]{1,0:T(8,128)} async-done(((f32[768,128]{1,0:T(8,128)}), f32[24,128]{1,0:T(8,128)}) %reduce-scatter.42.cloned.1.call-update) | async-done | bytes 12304
  (382 shorter events, 88.8 us)
Async XLA Ops:
  7.2 68.7 %copy-start.84 = (bf16[2,96]{1,0:T(2,128)(2,1)S(1)}, bf16[2,96]{1,0:T(2,128)(2,1)}, u32[]{:S(2)}) copy-start(bf16[2,96]{1,0:T(2,128)(2,1)} %param.22) | copy-start | bytes 1156
  7.2 106.4 %copy-start.85 = (bf16[2,2,24]{2,1,0:T(2,128)(2,1)S(1)}, bf16[2,2,24]{2,1,0:T(2,128)(2,1)}, u32[]{:S(2)}) copy-start(bf16[2,2,24]{2,1,0:T(2,128)(2,1)} %param.23) | copy-start | bytes 580
  7.2 290.5 %all-gather.23.cloned.1.call-start = ((), (), s32[]{:S(2)}) async-start(), calls=%async_computation.19 | async-start | bytes 3649536 | tf_op jit(solution)/shard_map/all_gather | solution.py:282
  8.9 151.3 %copy-start.82 = (s32[256]{0:T(256)S(1)}, s32[256]{0:T(256)}, u32[]{:S(2)}) copy-start(s32[256]{0:T(256)} %param.16) | copy-start | bytes 3076
  8.9 152.2 %copy-start.79 = (bf16[128,24]{0,1:T(8,128)(2,1)S(1)}, bf16[128,24]{0,1:T(8,128)(2,1)}, u32[]{:S(2)}) copy-start(bf16[128,24]{0,1:T(8,128)(2,1)} %param.24) | copy-start | bytes 18436
  8.9 316.6 %all-gather.25.cloned.1.call-start = ((), (), s32[]{:S(2)}) async-start(), calls=%async_computation.20 | async-start | bytes 1216512 | tf_op jit(solution)/shard_map/all_gather | solution.py:283
  10.4 319.6 %all-gather.27.cloned.1.call-start = ((), (), s32[]{:S(2)}) async-start(), calls=%async_computation.21 | async-start | bytes 4866048 | tf_op jit(solution)/shard_map/all_gather | solution.py:284
  12.2 330.6 %all-gather.29.cloned.1.call-start = ((), (), s32[]{:S(2)}) async-start(), calls=%async_computation.22 | async-start | bytes 4866048 | tf_op jit(solution)/shard_map/all_gather | solution.py:285
  14.0 341.5 %all-gather.31.cloned.1.call-start = ((), (), s32[]{:S(2)}) async-start(), calls=%async_computation.23 | async-start | bytes 3649536 | tf_op jit(solution)/shard_map/all_gather | solution.py:294
  14.6 422.8 %all-gather.33.cloned.1.call-start = ((), (), s32[]{:S(2)}) async-start(), calls=%async_computation.24 | async-start | bytes 1216512 | tf_op jit(solution)/shard_map/all_gather | solution.py:295
  15.2 434.2 %all-gather.35.cloned.1.call-start = ((), (), s32[]{:S(2)}) async-start(), calls=%async_computation.25 | async-start | bytes 4866048 | tf_op jit(solution)/shard_map/all_gather | solution.py:296
  15.9 499.5 %all-gather.37.cloned.1.call-start = ((), (), s32[]{:S(2)}) async-start(), calls=%async_computation.26 | async-start | bytes 4866048 | tf_op jit(solution)/shard_map/all_gather | solution.py:297
  16.7 606.9 %reduce-scatter.22.cloned.1.call-start = ((), (), s32[]{:S(2)}) async-start(), calls=%async_computation.11 | async-start | bytes 811008 | tf_op jit(solution)/shard_map/reduce_scatter | solution.py:148
  75.9 266.9 %copy-start.54 = (f32[768]{0:T(1024)}, f32[768]{0:T(1024)S(1)}, u32[]{:S(2)}) copy-start(f32[768]{0:T(1024)S(1)} %get-tuple-element.91) | copy-start | bytes 9220
  75.9 221.8 %copy-start.86 = (bf16[1024,768]{1,0:T(8,128)(2,1)S(1)}, bf16[1024,768]{1,0:T(8,128)(2,1)}, u32[]{:S(2)}) copy-start(bf16[1024,768]{1,0:T(8,128)(2,1)} %param.15) | copy-start | bytes 4718596
  113.6 216.4 %copy-start.75 = (f32[3072]{0:T(1024)}, f32[3072]{0:T(1024)S(1)}, u32[]{:S(2)}) copy-start(f32[3072]{0:T(1024)S(1)} %convert_element_type.226) | copy-start | bytes 36868
  160.2 182.7 %copy-start.49 = (f32[768]{0:T(1024)}, f32[768]{0:T(1024)S(1)}, u32[]{:S(2)}) copy-start(f32[768]{0:T(1024)S(1)} %get-tuple-element.88) | copy-start | bytes 9220
  160.2 192.3 %copy-start.56 = (f32[768]{0:T(1024)}, f32[768]{0:T(1024)S(1)}, u32[]{:S(2)}) copy-start(f32[768]{0:T(1024)S(1)} %get-tuple-element.87) | copy-start | bytes 9220
  161.1 194.2 %copy-start.80 = (s32[8]{0:T(128)}, s32[8]{0:T(128)S(1)}, u32[]{:S(2)}) copy-start(s32[8]{0:T(128)S(1)} %convert_reduce_fusion.10) | copy-start | bytes 100
  309.1 8.6 copy-start.11
  312.7 5.0 copy-start.12
  329.4 13.4 copy-start.5
  330.0 12.9 copy-start.62
  353.5 44.2 %copy-start.72 = (f32[768]{0:T(1024)S(1)}, f32[768]{0:T(1024)}, u32[]{:S(2)}) copy-start(f32[768]{0:T(1024)} %get-tuple-element.85) | copy-start | bytes 9220
  353.5 44.2 %copy-start.73 = (f32[768]{0:T(1024)S(1)}, f32[768]{0:T(1024)}, u32[]{:S(2)}) copy-start(f32[768]{0:T(1024)} %get-tuple-element.86) | copy-start | bytes 9220
  355.5 81.9 %copy-start.33 = (f32[8,768]{1,0:T(8,128)}, f32[8,768]{1,0:T(8,128)S(1)}, u32[]{:S(2)}) copy-start(f32[8,768]{1,0:T(8,128)S(1)} %convolution_add_fusion) | copy-start | bytes 73732
  355.5 81.0 %copy-start.78 = (pred[8,256]{1,0:T(8,128)(4,1)S(1)}, pred[8,256]{1,0:T(8,128)(4,1)}, u32[]{:S(2)}) copy-start(pred[8,256]{1,0:T(8,128)(4,1)} %broadcast_compare_fusion) | copy-start | bytes 6148
  355.5 81.9 %copy-start.71 = (f32[768]{0:T(1024)S(1)}, f32[768]{0:T(1024)}, u32[]{:S(2)}) copy-start(f32[768]{0:T(1024)} %get-tuple-element.84) | copy-start | bytes 9220
  358.1 91.3 %copy-start.60 = (f32[3072]{0:T(1024)S(1)}, f32[3072]{0:T(1024)}, u32[]{:S(2)}) copy-start(f32[3072]{0:T(1024)} %convert_element_type.227) | copy-start | bytes 36868
  437.2 78.2 %copy-start.70 = (f32[768]{0:T(1024)S(1)}, f32[768]{0:T(1024)}, u32[]{:S(2)}) copy-start(f32[768]{0:T(1024)} %get-tuple-element.82) | copy-start | bytes 9220
  437.4 81.4 %copy-start.43 = (bf16[8,768]{1,0:T(8,128)(2,1)}, bf16[8,768]{1,0:T(8,128)(2,1)S(1)}, u32[]{:S(2)}) copy-start(bf16[8,768]{1,0:T(8,128)(2,1)S(1)} %convert_element_type.195) | copy-start | bytes 36868
  439.1 86.1 %copy-start.29 = (f32[8,768]{1,0:T(8,128)}, f32[8,768]{1,0:T(8,128)S(1)}, u32[]{:S(2)}) copy-start(f32[8,768]{1,0:T(8,128)S(1)} %get-tuple-element.156) | copy-start | bytes 73732
  439.1 86.1 %copy-start.66 = (f32[8]{0:T(128)}, f32[8]{0:T(128)S(1)}, u32[]{:S(2)}) copy-start(f32[8]{0:T(128)S(1)} %broadcast_multiply_fusion.3) | copy-start | bytes 100
  439.3 85.9 %copy-start.68 = (f32[8]{0:T(128)}, f32[8]{0:T(128)S(1)}, u32[]{:S(2)}) copy-start(f32[8]{0:T(128)S(1)} %fusion.144) | copy-start | bytes 100
  449.4 73.7 %slice-start.2 = ((s8[4718592]{0:T(1024)(128)(4,1)}), s8[524288]{0:T(1024)(128)(4,1)S(1)}, s32[]{:S(2)}) async-start(s8[4718592]{0:T(1024)(128)(4,1)} %bitcast.269), calls=%async_computation.33 | async-start | bytes 1048576
  452.6 70.6 %copy-start.24 = (f32[8,3072]{1,0:T(8,128)}, f32[8,3072]{1,0:T(8,128)S(1)}, u32[]{:S(2)}) copy-start(f32[8,3072]{1,0:T(8,128)S(1)} %fusion.25) | copy-start | bytes 294916
  452.6 66.4 %copy-start.42 = (f32[8,1,768]{2,1,0:T(1,128)S(1)}, f32[8,1,768]{2,1,0:T(1,128)}, u32[]{:S(2)}) copy-start(f32[8,1,768]{2,1,0:T(1,128)} %slice.248) | copy-start | bytes 73732
  452.6 66.5 %copy-start.61 = (f32[768]{0:T(1024)S(1)}, f32[768]{0:T(1024)}, u32[]{:S(2)}) copy-start(f32[768]{0:T(1024)} %get-tuple-element.79) | copy-start | bytes 9220
  452.6 67.1 %copy-start.74 = (f32[768]{0:T(1024)S(1)}, f32[768]{0:T(1024)}, u32[]{:S(2)}) copy-start(f32[768]{0:T(1024)} %get-tuple-element.81) | copy-start | bytes 9220
  515.5 5.7 copy-start.10
  515.5 7.7 slice-start.3
  529.1 194.0 %reduce-scatter.24.cloned.1.call-start = ((), (), s32[]{:S(2)}) async-start(), calls=%async_computation.12 | async-start | bytes 811008 | tf_op jit(solution)/shard_map/reduce_scatter | solution.py:151
  530.8 378.8 %all-reduce.13.cloned.1.call-start = ((), (), s32[]{:S(2)}) async-start(), calls=%async_computation.30 | async-start | bytes 172032
  727.2 4.7 copy-start.1
  734.0 16.1 slice-start.4
  734.3 15.7 copy-start.26
  734.7 15.3 copy-start.6
  734.7 15.3 copy-start.50
  734.7 15.3 slice-start.5
  750.0 6.1 copy-start.20
  750.1 6.1 copy-start.63
  762.4 9.8 slice-start
  767.0 5.2 slice-start.1
  767.0 5.2 copy-start.22
  787.5 227.6 %reduce-scatter.28.cloned.1.call-start = ((), (), s32[]{:S(2)}) async-start(), calls=%async_computation.14 | async-start | bytes 2433024 | tf_op jit(solution)/shard_map/reduce_scatter | solution.py:341
  789.5 329.7 %reduce-scatter.26.cloned.1.call-start = ((), (), s32[]{:S(2)}) async-start(), calls=%async_computation.13 | async-start | bytes 2433024 | tf_op jit(solution)/shard_map/reduce_scatter | solution.py:365
  789.5 5.3 copy-start.9
  794.6 448.4 %reduce-scatter.38.cloned.1.call-start = ((), (), s32[]{:S(2)}) async-start(), calls=%async_computation.27 | async-start | bytes 7299072
  817.8 549.8 %reduce-scatter.40.cloned.1.call-start = ((), (), s32[]{:S(2)}) async-start(), calls=%async_computation.28 | async-start | bytes 7299072
  822.5 685.6 %reduce-scatter.36.cloned.1.call-start = ((), (), s32[]{:S(2)}) async-start(), calls=%async_computation.18 | async-start | bytes 9732096 | tf_op jit(solution)/shard_map/reduce_scatter | solution.py:343
  828.5 821.0 %reduce-scatter.34.cloned.1.call-start = ((), (), s32[]{:S(2)}) async-start(), calls=%async_computation.17 | async-start | bytes 9732096 | tf_op jit(solution)/shard_map/reduce_scatter | solution.py:367
  840.1 949.7 %reduce-scatter.32.cloned.1.call-start = ((), (), s32[]{:S(2)}) async-start(), calls=%async_computation.16 | async-start | bytes 9732096 | tf_op jit(solution)/shard_map/reduce_scatter | solution.py:342
  846.2 1085.1 %reduce-scatter.30.cloned.1.call-start = ((), (), s32[]{:S(2)}) async-start(), calls=%async_computation.15 | async-start | bytes 9732096 | tf_op jit(solution)/shard_map/reduce_scatter | solution.py:366
  858.8 1171.9 %reduce-scatter.42.cloned.1.call-start = ((), (), s32[]{:S(2)}) async-start(), calls=%async_computation.29 | async-start | bytes 405504
  (53 other events, 123.5 us)
Sparse Core Ops, SparseCore 0:
  11.5 63.3 all-gather.22
  77.8 52.9 all-gather.24
  134.3 63.7 all-gather.26
  201.4 63.9 all-gather.28
  268.1 58.5 all-gather.30
  329.4 53.0 all-gather.32
  386.0 63.3 all-gather.34
  452.9 62.5 all-gather.36
  529.3 94.2 reduce-scatter.21
  628.6 94.5 reduce-scatter.23
  787.6 121.9 all-reduce.12
  914.7 100.3 reduce-scatter.27
  1021.2 97.9 reduce-scatter.25
  1124.8 118.1 reduce-scatter.37
  1249.4 118.1 reduce-scatter.39
  1373.4 134.7 reduce-scatter.35
  1514.9 134.5 reduce-scatter.33
  1655.2 134.6 reduce-scatter.31
  1796.8 134.4 reduce-scatter.29
  1936.6 94.0 reduce-scatter.41
where the time goes:
time: 2050 us; the launch traced here: 2040 us
  waiting for transfers between devices  1400 us (68%)
  blocking collectives  317 us (15%)
  matrix products  152 us (7%)
  local copies, waits for them, and re-layouts  75.2 us (4%)
  other arithmetic  73 us (4%)
    unnamed x24, waiting for transfers between devices  382 us
    reduce_scatter x1, waiting for transfers between devices, shards(): lax.psum_scatter(first_grads[2], ('ctx', 'wa'), scatter_dimension=0, tile...  141 us
    reduce_scatter x1, waiting for transfers between devices, shards(): lax.psum_scatter(first_grads[3], ('ctx', 'wa'), scatter_dimension=0, tile...  141 us
    reduce_scatter x1, waiting for transfers between devices, shards(): lax.psum_scatter(second_grads[2], ('ctx', 'wa'), scatter_dimension=0, til...  139 us
    reduce_scatter x1, waiting for transfers between devices, shards(): lax.psum_scatter(second_grads[3], ('ctx', 'wa'), scatter_dimension=0, til...  138 us
    reduce_scatter x1, waiting for transfers between devices, shards(): lax.psum_scatter(first_grads[1], ('ctx', 'wa'), scatter_dimension=0, tile...  104 us
    reduce_scatter x1, waiting for transfers between devices, shards(): lax.psum_scatter(second_grads[1], ('ctx', 'wa'), scatter_dimension=0, til...  101 us
    reduce_scatter x1, waiting for transfers between devices, cross_backward(): lax.psum_scatter(part_v.reshape(part_v.shape[0], -1), ('ctx', 'wa'), scat...  98.8 us
  transfers between devices with their start and end apart: 20, of which 14 were waited for; matrix products, arithmetic and copies ran while one was open for 10% of the time, Pallas kernels for 0%

commit v1 on v0

v1 whole, which is shorter than its diff:
```python
from functools import partial

import jax
import jax.numpy as jnp
from jax import lax
from jax.experimental import pallas as pl
from jax.experimental.pallas import tpu as pltpu
from jax.sharding import PartitionSpec as P

HDIM = 64
SEG = 128
TP = 4
AXES = ("ctx", "wa")
F32 = jnp.float32
BF16 = jnp.bfloat16
SCALE = HDIM ** (-0.5)


def dot(a, b, dims=((1,), (0,))):
    return lax.dot_general(a, b, (dims, ((), ())), preferred_element_type=F32)


def normalize(values):
    center = values - jnp.mean(values, axis=-1, keepdims=True)
    spread = jnp.mean(center * center, axis=-1, keepdims=True)
    inverse = lax.rsqrt(spread + 1e-05)
    return center * inverse, inverse


def normalize_back(grad, normal, inverse):
    return inverse * (
        grad
        - jnp.mean(grad, axis=-1, keepdims=True)
        - normal * jnp.mean(grad * normal, axis=-1, keepdims=True)
    )


def gelu_pair(values):
    phi = 0.5 * (1.0 + lax.erf(values * 0.7071067811865476))
    density = jnp.exp(-0.5 * values * values) * 0.3989422804014327
    return values * phi, phi + values * density


class Net:
    def __init__(self, count):
        self.count = count
        self.bits = count.bit_length() - 1
        self.me = lax.axis_index(AXES)

    def bit(self, b):
        return (self.me >> b) & 1

    def hop(self, value, b):
        return lax.ppermute(value, AXES, [(i, i ^ (1 << b)) for i in range(self.count)])

    def grow(self, value, b, axis):
        other = self.hop(value, b)
        return jnp.where(
            self.bit(b) == 0,
            jnp.concatenate([value, other], axis),
            jnp.concatenate([other, value], axis),
        )

    def pick(self, value, which, axis):
        return lax.dynamic_slice_in_dim(value, which, 1, axis)

    def halve(self, value, b, axis, dtype):
        other = self.hop(self.pick(value, 1 - self.bit(b), axis), b)
        keep = self.pick(value, self.bit(b), axis)
        return (keep.astype(F32) + other.astype(F32)).astype(dtype)

    def trade(self, value, b, axis):
        other = self.hop(self.pick(value, 1 - self.bit(b), axis), b)
        keep = self.pick(value, self.bit(b), axis)
        return jnp.where(
            self.bit(b) == 0,
            jnp.concatenate([keep, other], axis),
            jnp.concatenate([other, keep], axis),
        )

    def total(self, value, bit_list):
        for b in bit_list:
            value = value + self.hop(value, b)
        return value


def place_blocks(net, parts, rows, width):
    arrays = [part[0] for part in parts]

    def body(me_ref, *refs):
        sources, target, sem = refs[: len(parts)], refs[len(parts)], refs[len(parts) + 1]
        me = me_ref[0]
        copies = []
        for source, (array, masks, col) in zip(sources, parts):
            for j, mask in enumerate(masks):
                copies.append(
                    pltpu.make_async_copy(
                        source.at[j],
                        target.at[me ^ mask, :, pl.ds(col, array.shape[2])],
                        sem,
                    )
                )
        for copy in copies:
            copy.start()
        pltpu.make_async_copy(target, target, sem).wait()

    return pl.pallas_call(
        body,
        out_shape=jax.ShapeDtypeStruct((net.count, rows, width), BF16),
        in_specs=[pl.BlockSpec(memory_space=pltpu.SMEM)]
        + [pl.BlockSpec(memory_space=pl.ANY)] * len(parts),
        out_specs=pl.BlockSpec(memory_space=pl.ANY),
        scratch_shapes=[pltpu.SemaphoreType.DMA],
        name="place_blocks",
    )(net.me.reshape(1), *arrays)


def link_orders(net):
    high = [net.bits - 1, net.bits - 2]
    mid = list(range(1, net.bits - 2))
    return high + mid, high + mid[::-1]


def gather_rows(net, shard):
    rows, width = shard.shape
    if rows % 8:
        return lax.all_gather(shard, AXES, axis=0, tiled=True)
    cut = (width // 256) * 128
    parts = []
    for order, col, end in zip(link_orders(net), (0, cut), (cut, width)):
        have, masks = shard[None, :, col:end], [0]
        for b in order[:-1]:
            have = jnp.concatenate([have, net.hop(have, b)], 0)
            masks = masks + [m ^ (1 << b) for m in masks]
        last = order[-1]
        late = net.hop(have, last)
        late_masks = [m ^ (1 << last) for m in masks]
        parts.append((have, masks, col))
        parts.append((net.hop(have, 0), [m ^ 1 for m in masks], col))
        parts.append((late, late_masks, col))
        parts.append((net.hop(late, 0), [m ^ 1 for m in late_masks], col))
    return place_blocks(net, parts, rows, width).reshape(net.count * rows, width)


def scatter_rows(net, grad):
    width = grad.shape[1]
    rows = grad.shape[0] // net.count
    cube = grad.reshape((2,) * net.bits + (rows, width))
    cube = net.halve(cube, 0, net.bits - 1, BF16)
    cut = (width // 256) * 128
    out = []
    for order, col, end in zip(link_orders(net), (0, cut), (cut, width)):
        half = cube[..., col:end]
        for step, b in enumerate(order[::-1]):
            last = step == len(order) - 1
            half = net.halve(half, b, net.bits - 1 - b, F32 if last else BF16)
        out.append(half.reshape(rows, end - col))
    return jnp.concatenate(out, 1)


def head_probability(qkv_ref, head, heads):
    width = heads * HDIM
    queries = qkv_ref[:, head * HDIM : (head + 1) * HDIM]
    keys = qkv_ref[:, width + head * HDIM : width + (head + 1) * HDIM]
    values = qkv_ref[:, 2 * width + head * HDIM : 2 * width + (head + 1) * HDIM]
    scores = dot(queries, keys, ((1,), (1,))) * SCALE
    raised = jnp.exp(scores - jnp.max(scores, axis=-1, keepdims=True))
    chance = raised / jnp.sum(raised, axis=-1, keepdims=True)
    return queries, keys, values, chance


def attend_forward_body(heads, qkv_ref, out_ref):
    for pair in range(heads // 2):
        both = []
        for head in (2 * pair, 2 * pair + 1):
            _, _, values, chance = head_probability(qkv_ref, head, heads)
            both.append(dot(chance.astype(BF16), values))
        out_ref[:, pair * 128 : (pair + 1) * 128] = jnp.concatenate(both, 1).astype(BF16)


def attend_backward_body(heads, qkv_ref, grad_ref, out_ref, sums_ref):
    width = heads * HDIM
    for pair in range(heads // 2):
        got = ([], [], [])
        for head in (2 * pair, 2 * pair + 1):
            queries, keys, values, chance = head_probability(qkv_ref, head, heads)
            grad = grad_ref[:, head * HDIM : (head + 1) * HDIM]
            slope = dot(grad, values, ((1,), (1,)))
            slope = slope - jnp.sum(slope * chance, axis=-1, keepdims=True)
            tilt = (chance * slope).astype(BF16)
            got[0].append(dot(tilt, keys) * SCALE)
            got[1].append(dot(tilt, queries, ((0,), (0,))) * SCALE)
            got[2].append(dot(chance.astype(BF16), grad, ((0,), (0,))))
        for part in range(3):
            low = jnp.concatenate(got[part], 1).astype(BF16)
            at = part * width + pair * 128
            out_ref[:, at : at + 128] = low
            sums_ref[0, :, at : at + 128] = jnp.sum(low.astype(F32), axis=0, keepdims=True)


def segment_attend(qkv):
    rows, width = qkv.shape[0], qkv.shape[1] // 3
    return pl.pallas_call(
        partial(attend_forward_body, width // HDIM),
        out_shape=jax.ShapeDtypeStruct((rows, width), BF16),
        grid=(rows // SEG,),
        in_specs=[pl.BlockSpec((SEG, 3 * width), lambda i: (i, 0))],
        out_specs=pl.BlockSpec((SEG, width), lambda i: (i, 0)),
        name="segment_attend",
    )(qkv)


def segment_attend_back(qkv, grad):
    rows, width = grad.shape
    return pl.pallas_call(
        partial(attend_backward_body, width // HDIM),
        out_shape=(
            jax.ShapeDtypeStruct((rows, 3 * width), BF16),
            jax.ShapeDtypeStruct((rows // SEG, 1, 3 * width), F32),
        ),
        grid=(rows // SEG,),
        in_specs=[
            pl.BlockSpec((SEG, 3 * width), lambda i: (i, 0)),
            pl.BlockSpec((SEG, width), lambda i: (i, 0)),
        ],
        out_specs=(
            pl.BlockSpec((SEG, 3 * width), lambda i: (i, 0)),
            pl.BlockSpec((1, 1, 3 * width), lambda i: (i, 0, 0)),
        ),
        name="segment_attend_back",
    )(qkv, grad)


def tail_forward(hidden, context, w_out, w_up, w_down, biases, up_bias, gains):
    mixed = hidden.astype(F32) + dot(context, w_out) + biases[2]
    normal1, inverse1 = normalize(mixed)
    normed = normal1 * gains[0] + biases[3]
    normed_low = normed.astype(BF16)
    active, slope = gelu_pair(dot(normed_low, w_up) + up_bias)
    active = active.astype(BF16)
    slope = slope.astype(BF16)
    second = normed + dot(active, w_down) + biases[4]
    normal2, inverse2 = normalize(second)
    result = normal2 * gains[1] + biases[5]
    return result, (normal1, inverse1, normed_low, active, slope, normal2, inverse2)


def tail_backward(grad, kept, w_out, w_up, w_down, gains):
    normal1, inverse1, _, _, slope, normal2, inverse2 = kept
    gain2, shift2 = jnp.sum(grad * normal2, axis=0), jnp.sum(grad, axis=0)
    grad_second = normalize_back(grad * gains[1], normal2, inverse2)
    grad_ffn = grad_second.astype(BF16)
    grad_before = (dot(grad_ffn, w_down, ((1,), (1,))) * slope.astype(F32)).astype(BF16)
    grad_normed = grad_second + dot(grad_before, w_up, ((1,), (1,)))
    gain1, shift1 = jnp.sum(grad_normed * normal1, axis=0), jnp.sum(grad_normed, axis=0)
    grad_mixed = normalize_back(grad_normed * gains[0], normal1, inverse1)
    grad_attn = grad_mixed.astype(BF16)
    grad_context = dot(grad_attn, w_out, ((1,), (1,))).astype(BF16)
    sums = (gain1, shift1, gain2, shift2)
    return grad_ffn, grad_before, grad_mixed, grad_attn, grad_context, sums


def column_sums(values):
    return jnp.sum(values.astype(F32), axis=0)


def cross_weights(net, w_qkv, w_out, w_up, w_down):
    rows, width = w_out.shape
    hi, lo = net.bits - 1, net.bits - 2
    plane = net.bits - 2
    part = width // TP
    hidden = w_up.shape[1] // TP
    cols = jnp.concatenate(
        [
            w_qkv.reshape(rows, 3, TP, part).transpose(2, 0, 1, 3).reshape(TP, rows, 3 * part),
            w_up.reshape(rows, TP, hidden).transpose(1, 0, 2),
        ],
        2,
    )
    cols = cols.reshape(2, 2, rows, 3 * part + hidden)
    cols = net.trade(net.trade(cols, hi, 0), lo, 1)
    cols = cols.reshape((TP,) + (1,) * plane + (rows, 3 * part + hidden))
    deep = jnp.concatenate([w_out, w_down], 0)
    deep = deep.reshape((1,) * plane + deep.shape)
    up = list(range(1, plane))
    for b in up + [0]:
        cols = net.grow(cols, b, plane - b)
    for b in up[::-1] + [0]:
        deep = net.grow(deep, b, plane - 1 - b)
    cols = cols.reshape(width, 3 * part + hidden)
    deep = deep.reshape(net.count // TP, -1, width)
    return (
        cols[:, : 3 * part],
        deep[:, :rows].reshape(part, width),
        cols[:, 3 * part :],
        deep[:, rows:].reshape(hidden, width),
    )


def cross_weight_grads(net, grad_qkv, grad_out, grad_up, grad_down):
    hi, lo = net.bits - 1, net.bits - 2
    plane = net.bits - 2
    planes = net.count // TP
    width = grad_qkv.shape[0]
    part = grad_out.shape[0]
    hidden = grad_down.shape[0]
    rows = width // net.count
    cols = jnp.concatenate([grad_qkv, grad_up], 1)
    cols = cols.reshape((TP,) + (2,) * plane + (rows, 3 * part + hidden))
    deep = jnp.concatenate(
        [grad_out.reshape(planes, rows, width), grad_down.reshape(planes, -1, width)], 1
    )
    deep = deep.reshape((2,) * plane + deep.shape[1:])
    up = list(range(1, plane))
    for b in [0] + up[::-1]:
        cols = net.halve(cols, b, plane - b, BF16)
    for step, b in enumerate([0] + up):
        deep = net.halve(deep, b, plane - 1 - b, F32 if step == plane - 1 else BF16)
    cols = cols.reshape(2, 2, rows, 3 * part + hidden)
    cols = net.trade(net.trade(cols, hi, 0), lo, 1).astype(F32)
    cols = cols.reshape(TP, rows, 3 * part + hidden)
    deep = deep.reshape(-1, width)
    return (
        cols[:, :, : 3 * part].reshape(TP, rows, 3, part).transpose(1, 2, 0, 3).reshape(rows, -1),
        deep[:rows],
        cols[:, :, 3 * part :].transpose(1, 0, 2).reshape(rows, -1),
        deep[rows:],
    )


def split_heads(values):
    return values.reshape(values.shape[0], values.shape[1] // HDIM, HDIM)


def cross_encoder(net, cross_in, grad_out, weights, biases, up_bias, gains, seq_ids):
    w_qkv, w_out, w_up, w_down = weights
    own, width = cross_in.shape
    part, hidden = w_out.shape[0], w_down.shape[0]
    planes = net.count // TP
    plane = net.bits - 2
    hi, lo = net.bits - 1, net.bits - 2
    member = net.me >> lo
    here = net.me & (planes - 1)
    up = list(range(1, plane))

    def share(values):
        return net.grow(net.grow(values, lo, 0), hi, 0)

    def mine(values):
        return lax.dynamic_slice_in_dim(values, member * own, own, 0)

    def slab(vector, size):
        return lax.dynamic_slice_in_dim(vector, member * size, size, 0)

    grad_all = share(grad_out).astype(F32)
    hidden_all = share(cross_in)
    hidden_low = hidden_all.astype(BF16)
    projected = dot(hidden_low, w_qkv)
    queries = (projected[:, :part] + slab(biases[0], part)).astype(BF16)
    key_rows = projected[:, part : 2 * part].astype(BF16)
    value_rows = (projected[:, 2 * part :] + slab(biases[1], part)).astype(BF16)
    both = jnp.concatenate([key_rows, value_rows], 1)
    count = both.shape[0]
    both = both.reshape((1,) * plane + both.shape)
    for b in [0] + up:
        both = net.grow(both, b, plane - 1 - b)
    both = both.reshape(planes * count, 2 * part)
    all_keys, all_values = split_heads(both[:, :part]), split_heads(both[:, part:])
    slots = seq_ids.reshape(TP, planes, own)
    key_ids = slots.transpose(1, 0, 2).reshape(-1)
    row_ids = lax.dynamic_slice_in_dim(slots, here, 1, 1).reshape(-1)
    allowed = row_ids[:, None] == key_ids[None, :]
    heads_q = split_heads(queries)
    scores = jnp.einsum("qhd,khd->hqk", heads_q, all_keys, preferred_element_type=F32) * SCALE
    scores = jnp.where(allowed[None], scores, -1e30)
    raised = jnp.exp(scores - jnp.max(scores, axis=-1, keepdims=True))
    chance = raised / jnp.sum(raised, axis=-1, keepdims=True)
    chance_low = chance.astype(BF16)
    context = jnp.einsum("hqk,khd->qhd", chance_low, all_values, preferred_element_type=F32)
    context = context.reshape(count, part).astype(BF16)
    mixed = hidden_all + net.total(dot(context, w_out), (lo, hi)) + biases[2]
    normal1, inverse1 = normalize(mixed)
    normed = normal1 * gains[0] + biases[3]
    normed_low = normed.astype(BF16)
    active, slope = gelu_pair(dot(normed_low, w_up) + slab(up_bias, hidden))
    active = active.astype(BF16)
    second = normed + net.total(dot(active, w_down), (lo, hi)) + biases[4]
    normal2, inverse2 = normalize(second)
    result = mine(normal2 * gains[1] + biases[5])

    grad_second = normalize_back(grad_all * gains[1], normal2, inverse2)
    grad_ffn = grad_second.astype(BF16)
    grad_before = (dot(grad_ffn, w_down, ((1,), (1,))) * slope).astype(BF16)
    grad_down = dot(active, grad_ffn, ((0,), (0,))).astype(BF16)
    grad_up = dot(normed_low, grad_before, ((0,), (0,))).astype(BF16)
    grad_normed = grad_second + net.total(dot(grad_before, w_up, ((1,), (1,))), (lo, hi))
    grad_mixed = normalize_back(grad_normed * gains[0], normal1, inverse1)
    grad_attn = grad_mixed.astype(BF16)
    grad_wout = dot(context, grad_attn, ((0,), (0,))).astype(BF16)
    grad_context = split_heads(dot(grad_attn, w_out, ((1,), (1,))).astype(BF16))
    slopes = jnp.einsum("qhd,khd->hqk", grad_context, all_values, preferred_element_type=F32)
    slopes = slopes - jnp.sum(slopes * chance, axis=-1, keepdims=True)
    tilt = (chance * slopes).astype(BF16)
    grad_q = jnp.einsum("hqk,khd->qhd", tilt, all_keys, preferred_element_type=F32) * SCALE
    part_k = jnp.einsum("hqk,qhd->khd", tilt, heads_q, preferred_element_type=F32) * SCALE
    part_v = jnp.einsum("hqk,qhd->khd", chance_low, grad_context, preferred_element_type=F32)
    both = jnp.concatenate([part_k.reshape(-1, part), part_v.reshape(-1, part)], 1)
    both = both.reshape((2,) * plane + (count, 2 * part))
    for b in [0] + up[::-1]:
        both = net.halve(both, b, plane - 1 - b, F32)
    both = both.reshape(count, 2 * part)
    grad_qkv = jnp.concatenate([grad_q.reshape(count, part), both], 1).astype(BF16)
    grad_wqkv = dot(hidden_low, grad_qkv, ((0,), (0,))).astype(BF16)
    back = dot(grad_qkv, w_qkv, ((1,), (1,))).reshape(2, 2, own, width)
    back = net.halve(net.halve(back, hi, 0, F32), lo, 1, F32).reshape(own, width)
    grad_in = mine(grad_mixed) + back

    def spread(vector, size):
        return lax.dynamic_update_slice_in_dim(jnp.zeros((size * TP,), F32), vector, member * size, 0)

    grad_own = mine(grad_all)
    normed_own = mine(grad_normed)
    bias_rows = jnp.stack(
        [
            spread(column_sums(grad_qkv[:, :part]), part),
            spread(column_sums(grad_qkv[:, 2 * part :]), part),
            column_sums(mine(grad_attn)),
            column_sums(normed_own),
            column_sums(mine(grad_ffn)),
            column_sums(grad_own),
        ]
    )
    gain_rows = jnp.stack(
        [column_sums(normed_own * mine(normal1)), column_sums(grad_own * mine(normal2))]
    )
    up_row = spread(column_sums(grad_before), hidden)
    return (
        result,
        grad_in,
        (grad_wqkv, grad_wout, grad_up, grad_down),
        (bias_rows, up_row, gain_rows),
    )


def pack_small(count, bias_rows, up_row, gain_rows):
    flat = jnp.concatenate(
        [
            bias_rows.reshape(6, count, -1).transpose(1, 0, 2).reshape(count, -1),
            up_row.reshape(count, -1),
            gain_rows.reshape(2, count, -1).transpose(1, 0, 2).reshape(count, -1),
        ],
        1,
    )
    return flat


def unpack_small(flat, share, hidden):
    lead = flat.shape[:-1]
    return (
        flat[..., : 6 * share].reshape(lead + (6, share)),
        flat[..., 6 * share : 6 * share + hidden],
        flat[..., 6 * share + hidden :].reshape(lead + (2, share)),
    )


def scatter_small(net, flat):
    cube = flat.reshape((2,) * net.bits + flat.shape[1:])
    for b in range(net.bits):
        cube = net.halve(cube, b, net.bits - 1 - b, F32)
    return cube.reshape(flat.shape[1:])


def gather_small(net, flat):
    cube = flat.reshape((1,) * net.bits + flat.shape)
    for b in list(range(1, net.bits)) + [0]:
        cube = net.grow(cube, b, net.bits - 1 - b)
    return cube.reshape((net.count,) + flat.shape)


def places_of(local_ids, local_slots, seq_ids, table_rows):
    all_slots = jnp.arange(seq_ids.shape[0], dtype=jnp.int32)
    earlier = (seq_ids[None, :] == local_ids[:, None]) & (all_slots[None, :] < local_slots[:, None])
    places = jnp.sum(earlier.astype(jnp.int32), axis=1)
    return places[:, None] == table_rows[None, :]


def shards(
    count, tokens, seq_ids, w_qkv, w_out, w_up, w_down, biases, up_bias, norm_gains, pos_table, cotangent
):
    net = Net(count)
    rows_here, width = tokens.shape
    segs_here = rows_here // SEG
    share, hidden = biases.shape[2], up_bias.shape[1]
    first_seg = net.me * segs_here
    local_ids = lax.dynamic_slice_in_dim(seq_ids, first_seg, segs_here)
    table_rows = jnp.arange(pos_table.shape[0], dtype=jnp.int32)
    local_slots = first_seg + jnp.arange(segs_here, dtype=jnp.int32)
    onehot = places_of(local_ids, local_slots, seq_ids, table_rows)

    small = jnp.concatenate(
        [
            pos_table.T.reshape(-1),
            *[
                jnp.concatenate([biases[e].reshape(-1), up_bias[e], norm_gains[e].reshape(-1)])
                for e in (0, 1)
            ],
        ]
    )
    table_size = pos_table.size
    small = jnp.pad(small, (0, -small.size % 128)).reshape(-1, 128)
    small = gather_small(net, small).reshape(count, -1)
    table = small[:, :table_size].reshape(width, pos_table.shape[0])
    each = 8 * share + hidden
    params = []
    for e in (0, 1):
        piece = small[:, table_size + e * each : table_size + (e + 1) * each].astype(F32)
        b, u, g = unpack_small(piece, share, hidden)
        params.append(
            (
                b.transpose(1, 0, 2).reshape(6, width),
                u.reshape(-1),
                g.transpose(1, 0, 2).reshape(2, width),
            )
        )
    biases0, up_bias0, gains0 = params[0]

    w_qkv0 = gather_rows(net, w_qkv[0])
    w_out0 = gather_rows(net, w_out[0])
    w_up0 = gather_rows(net, w_up[0])
    w_down0 = gather_rows(net, w_down[0])
    weights1 = cross_weights(net, w_qkv[1], w_out[1], w_up[1], w_down[1])

    projected = dot(tokens, w_qkv0)
    shift = jnp.concatenate([biases0[0], jnp.zeros((width,), F32), biases0[1]])
    qkv = (projected + shift).astype(BF16)
    context = segment_attend(qkv)
    result0, kept = tail_forward(tokens, context, w_out0, w_up0, w_down0, biases0, up_bias0, gains0)
    blocked = result0.reshape(segs_here, SEG, width)
    cross_in = blocked[:, 0, :] + dot(onehot.astype(BF16), table, ((1,), (1,)))
    grad_rows = cotangent.reshape(segs_here, SEG, width)
    result1, grad_cross, grads1, small1 = cross_encoder(
        net, cross_in, grad_rows[:, 0, :], weights1, *params[1], seq_ids
    )
    layer_out = blocked.at[:, 0, :].set(result1).reshape(rows_here, width).astype(BF16)

    shares1 = cross_weight_grads(net, *grads1)
    grad_places = lax.dot_general(
        grad_cross,
        onehot.astype(F32),
        (((0,), (0,)), ((), ())),
        precision=lax.Precision.HIGHEST,
        preferred_element_type=F32,
    ).reshape(count, -1)
    packed1 = scatter_small(net, jnp.concatenate([grad_places, pack_small(count, *small1)], 1))

    grad_segment = grad_rows.astype(F32).at[:, 0, :].set(grad_cross).reshape(rows_here, width)
    grad_ffn, grad_before, grad_mixed, grad_attn, grad_context, sums = tail_backward(
        grad_segment, kept, w_out0, w_up0, w_down0, gains0
    )
    _, _, normed_low, active, _, _, _ = kept
    grad_down0 = scatter_rows(net, dot(active, grad_ffn, ((0,), (0,))).astype(BF16))
    grad_up0 = scatter_rows(net, dot(normed_low, grad_before, ((0,), (0,))).astype(BF16))
    grad_out0 = scatter_rows(net, dot(context, grad_attn, ((0,), (0,))).astype(BF16))
    grad_qkv, qkv_sums = segment_attend_back(qkv, grad_context)
    qkv_sums = jnp.sum(qkv_sums, axis=(0, 1))
    grad_qkv0 = scatter_rows(net, dot(tokens, grad_qkv, ((0,), (0,))).astype(BF16))
    grad_tokens = (grad_mixed + dot(grad_qkv, w_qkv0, ((1,), (1,)))).astype(BF16)
    gain1, shift1, gain2, shift2 = sums
    packed0 = scatter_small(
        net,
        pack_small(
            count,
            jnp.stack(
                [
                    qkv_sums[:width],
                    qkv_sums[2 * width :],
                    column_sums(grad_attn),
                    shift1,
                    column_sums(grad_ffn),
                    shift2,
                ]
            ),
            column_sums(grad_before),
            jnp.stack([gain1, gain2]),
        ),
    )
    small0 = unpack_small(packed0, share, hidden)
    small1 = unpack_small(packed1[table_size:], share, hidden)
    return (
        layer_out,
        grad_tokens,
        jnp.stack([grad_qkv0, shares1[0]]),
        jnp.stack([grad_out0, shares1[1]]),
        jnp.stack([grad_up0, shares1[2]]),
        jnp.stack([grad_down0, shares1[3]]),
        jnp.stack([small0[0], small1[0]]),
        jnp.stack([small0[1], small1[1]]),
        jnp.stack([small0[2], small1[2]]),
        packed1[:table_size].reshape(share, -1).T,
    )


def solution(mesh):
    count = mesh.shape["ctx"] * mesh.shape["wa"]
    in_specs = (
        P(AXES, None),
        P(),
        P(None, AXES, None),
        P(None, AXES, None),
        P(None, AXES, None),
        P(None, AXES, None),
        P(None, None, AXES),
        P(None, AXES),
        P(None, None, AXES),
        P(None, AXES),
        P(AXES, None),
    )
    out_specs = (
        P(AXES, None),
        P(AXES, None),
        P(None, AXES, None),
        P(None, AXES, None),
        P(None, AXES, None),
        P(None, AXES, None),
        P(None, None, AXES),
        P(None, AXES),
        P(None, None, AXES),
        P(None, AXES),
    )
    return jax.shard_map(
        partial(shards, count), mesh=mesh, in_specs=in_specs, out_specs=out_specs, check_vma=False
    )
```

time: 2050 us -> 1170 us (0.57)
  waiting for transfers between devices: 1400 us -> 152 us
  Pallas kernels: 0 us -> 518 us
  blocking collectives: 317 us -> 0 us
  starting transfers between devices: 1.28 us -> 141 us
  local copies, waits for them, and re-layouts: 75.2 us -> 134 us
  matrix products: 152 us -> 116 us
    reduce_scatter x8 -> x0, waiting for transfers between devices: 948 us -> none  [the longest x1 141 us: shards(): lax.psum_scatter(first_grads[2], ('ctx', 'wa'), scatter_dimension=0, tile...]
    pallas_call x0 -> x6, Pallas kernels: none -> 518 us  [the longest x4 433 us: place_blocks(): pl.pallas_call(body, out_shape=jax.ShapeDtypeStruct((net.count, rows, wid...]
    unnamed x24 -> x0, waiting for transfers between devices: 382 us -> none
    all_gather x7 -> x0, blocking collectives: 280 us -> none  [the longest x1 44.8 us: shards(): lax.all_gather(biases[0], ('ctx', 'wa'), axis=1, tiled=True)]
    ppermute x0 -> x133, waiting for transfers between devices: none -> 152 us  [hop(): lax.ppermute(value, AXES, [(i, i ^ 1 << b) for i in range(self.count)])]
    ppermute x0 -> x133, starting transfers between devices: none -> 141 us  [hop(): lax.ppermute(value, AXES, [(i, i ^ 1 << b) for i in range(self.count)])]
    all_gather x8 -> x0, waiting for transfers between devices: 73 us -> none  [the longest x1 62.9 us: shards(): lax.all_gather(w_down[1], ('ctx', 'wa'), axis=0, tiled=True)]
    unnamed x1 -> x0, blocking collectives: 37.1 us -> none
  transfers between devices with their start and end apart: 20 -> 133, of which waited for: 14 -> 52; matrix products, arithmetic and copies ran while one was open for 10% -> 25% of each run, Pallas kernels for 0% -> 45%
where the time goes in v1:
time: 1170 us; the launch traced here: 1150 us
  Pallas kernels  518 us (44%)
  waiting for transfers between devices  152 us (13%)
  starting transfers between devices  141 us (12%)
  local copies, waits for them, and re-layouts  134 us (11%)
  matrix products  116 us (10%)
  other arithmetic  91.3 us (8%)
    pallas_call x4, Pallas kernels, place_blocks(): pl.pallas_call(body, out_shape=jax.ShapeDtypeStruct((net.count, rows, wid...  433 us
    ppermute x133, waiting for transfers between devices, hop(): lax.ppermute(value, AXES, [(i, i ^ 1 << b) for i in range(self.count)])  152 us
    ppermute x133, starting transfers between devices, hop(): lax.ppermute(value, AXES, [(i, i ^ 1 << b) for i in range(self.count)])  141 us
    dot_general x25, matrix products, dot(): return lax.dot_general(a, b, (dims, ((), ())), preferred_element_type=F32)  106 us
    pallas_call x1, Pallas kernels, segment_attend_back(): pl.pallas_call(partial(attend_backward_body, width // HDIM), out_shape=(j...  48.4 us
    pallas_call x1, Pallas kernels, segment_attend(): pl.pallas_call(partial(attend_forward_body, width // HDIM), out_shape=jax...  36 us
  transfers between devices with their start and end apart: 133, of which 52 were waited for; matrix products, arithmetic and copies ran while one was open for 25% of the time, Pallas kernels for 45%

profile of v1, /device:TPU:0, one launch (start us, length us, event | category | flops | bytes accessed | tf_op | source)
XLA Modules:
  0.0 1154.9 jit_solution(13823887929565424030)
XLA Ops:
  4.0 3.0 collective-permute-start.12
  8.0 2.7 collective-permute-start.6
  11.8 2.7 collective-permute-start.17
  19.3 2.6 collective-permute-start.35
  30.1 2.7 collective-permute-start.41
  38.8 3.2 collective-permute-done.24
  42.1 2.7 collective-permute-start.55
  48.9 2.8 collective-permute-done.15
  81.7 3.8 collective-permute-done.2
  91.4 36.8 %place_blocks.5 = bf16[32,24,768]{2,1,0:T(8,128)(2,1)} custom-call(s32[1]{0:T(128)} %bitcast.me_ref, bf16[8,24,384]{2,1,0:T(8,128)(2,1)} %copy-done.26, bf16[8,24,384]{2,1,0:T(8,128)(2,1)} %collective-permute-done.20.refs_1_, bf16[8,24,384]{2,1,0:T(8,128)(2,1)} %collective-permute-done.21.refs_2_, bf16[8,24,384]{2,1,0:T(8,128)(2,1)} %copy-done.52, ...), custom_call_target="tpu_custom_call" | custom-call | tf_op jit(solution)/shard_map/place_blocks/pallas_call | solution.py:107
  136.3 3.8 collective-permute-done.10.refs_6_
  140.1 3.1 collective-permute-done.4.refs_2_
  146.0 6.8 collective-permute-done.58
  158.6 108.3 %place_blocks.4 = bf16[32,24,2304]{2,1,0:T(8,128)(2,1)} custom-call(s32[1]{0:T(128)} %bitcast.me_ref, bf16[8,24,1152]{2,1,0:T(8,128)(2,1)} %copy-done.13, bf16[8,24,1152]{2,1,0:T(8,128)(2,1)} %copy-done.36, bf16[8,24,1152]{2,1,0:T(8,128)(2,1)} %copy-done.35, bf16[8,24,1152]{2,1,0:T(8,128)(2,1)} %copy-done.39, bf16[8,24,1152]{2,1,0:T(8,128)(2,1)} %copy-done.12, ...), custom_call_target="tpu_custom_call" | custom-call | tf_op jit(solution)/shard_map/place_blocks/pallas_call | solution.py:107
  266.9 8.5 fusion.6.qkv_ref
  275.4 36.0 %segment_attend.1 = bf16[1024,768]{1,0:T(8,128)(2,1)} custom-call(bf16[1024,2304]{1,0:T(8,128)(2,1)} %fusion.6.qkv_ref), custom_call_target="tpu_custom_call" | custom-call | tf_op jit(solution)/shard_map/segment_attend/pallas_call | solution.py:203
  311.4 3.8 fusion.112
  318.4 13.4 %collective-permute-done.51.refs_6_ = bf16[8,96,384]{2,1,0:T(8,128)(2,1)} collective-permute-done((bf16[8,96,384]{2,1,0:T(8,128)(2,1)}, bf16[8,96,384]{2,1,0:T(8,128)(2,1)}, u32[]{:S(2)}, u32[]{:S(2)}) %collective-permute-start.51) | collective-permute-done | bytes 589856 | tf_op jit(solution)/shard_map/ppermute | solution.py:54
  332.4 144.1 %place_blocks.6 = bf16[32,24,3072]{2,1,0:T(8,128)(2,1)} custom-call(s32[1]{0:T(128)} %bitcast.me_ref, bf16[8,24,1536]{2,1,0:T(8,128)(2,1)} %pad_maximum_fusion.1.refs_0_, bf16[8,24,1536]{2,1,0:T(8,128)(2,1)} %collective-permute-done.32.refs_1_, bf16[8,24,1536]{2,1,0:T(8,128)(2,1)} %collective-permute-done.33.refs_2_, ...), custom_call_target="tpu_custom_call" | custom-call | tf_op jit(solution)/shard_map/place_blocks/pallas_call | solution.py:107
  476.5 12.3 %multiply_convert_fusion.1 = (bf16[1024,3072]{1,0:T(8,128)(2,1)}, f32[1024,3072]{1,0:T(8,128)}) fusion(f32[3072]{0:T(1024)S(1)} %add.592, bf16[768,3072]{1,0:T(8,128)(2,1)} %bitcast.277, f32[1024,768]{1,0:T(8,128)S(1)} %get-tuple-element.170, f32[768]{0:T(1024)S(1)} %add.589, f32[768]{0:T(1024)S(1)} %mul.325, f32[1024]{0:T(1024)S(1)} %add_rsqrt_fusion.1, ...), kind=kOutput, calls=%fused_computation.9 | convolution fusion | flops 4854644736 | bytes 26765312 | tf_op jit(solution)/shard_map/dot_general | solution.py:20
  489.2 144.1 %place_blocks.7 = bf16[32,96,768]{2,1,0:T(8,128)(2,1)} custom-call(s32[1]{0:T(128)} %bitcast.me_ref, bf16[8,96,384]{2,1,0:T(8,128)(2,1)} %pad_maximum_fusion.3.refs_0_, bf16[8,96,384]{2,1,0:T(8,128)(2,1)} %collective-permute-done.44.refs_1_, bf16[8,96,384]{2,1,0:T(8,128)(2,1)} %collective-permute-done.45.refs_2_, ...), custom_call_target="tpu_custom_call" | custom-call | tf_op jit(solution)/shard_map/place_blocks/pallas_call | solution.py:107
  633.3 9.7 fusion.113
  650.3 2.8 maximum_select_fusion
  657.3 3.0 collective-permute-done.61
  710.2 3.4 convert_element_type.534
  736.3 2.7 collective-permute-done.72
  754.7 3.3 convert_element_type.532
  784.8 4.1 collective-permute-done.75
  803.2 2.7 pad_maximum_fusion
  805.9 4.2 copy.178
  827.0 3.0 fusion.95
  834.8 10.0 convolution_convert_fusion
  844.9 12.4 %convert_reduce_fusion = (f32[3072]{0:T(1024)}, bf16[1024,3072]{1,0:T(8,128)(2,1)S(1)}) fusion(f32[1024,3072]{1,0:T(8,128)} %get-tuple-element.172, f32[3072]{0:T(1024)S(1)} %copy-done.74, bf16[3072,768]{1,0:T(8,128)(2,1)S(1)} %bitcast.284, f32[1024,768]{1,0:T(8,128)S(1)} %get-tuple-element.87), kind=kOutput, calls=%fused_computation.7 | convolution fusion | flops 4879807488 | bytes 26763264 | tf_op jit(solution)/shard_map/dot_general | solution.py:20
  857.4 6.5 multiply_reduce_fusion
  863.9 8.2 convolution_convert_fusion.1
  873.9 2.6 convolution_convert_fusion.3.grad_ref
  876.4 48.4 %segment_attend_back.1 = (bf16[1024,2304]{1,0:T(8,128)(2,1)}, f32[8,1,2304]{2,1,0:T(1,128)}) custom-call(bf16[1024,2304]{1,0:T(8,128)(2,1)} %fusion.6.qkv_ref, bf16[1024,768]{1,0:T(8,128)(2,1)} %convolution_convert_fusion.3.grad_ref), custom_call_target="tpu_custom_call" | custom-call | tf_op jit(solution)/shard_map/segment_attend_back/pallas_call | solution.py:215
  924.9 8.7 convolution_convert_fusion.2
  933.6 5.0 add_convert_fusion.4
  960.3 2.9 convolution_convert_fusion.4
  964.4 3.3 constant_dynamic-slice_fusion.30
  981.5 4.3 collective-permute-done.129
  994.2 2.6 collective-permute-start.132
  1004.1 8.5 collective-permute-done.103
  1014.2 4.0 collective-permute-done.94
  1019.3 4.0 collective-permute-done.98
  1024.5 3.2 collective-permute-done.95
  1029.0 2.9 collective-permute-done.99
  1033.3 2.7 collective-permute-done.96
  1037.2 2.7 collective-permute-done.100
  1039.9 2.7 collective-permute-start.97
  1044.6 2.7 collective-permute-start.101
  1054.8 6.8 collective-permute-done.89
  1063.7 5.6 collective-permute-done.90
  1078.4 3.2 collective-permute-done.92
  1082.8 4.3 collective-permute-done.80
  1092.7 3.1 add_convert_fusion.1
  1097.8 2.6 add_convert_fusion.2
  1103.9 2.6 collective-permute-start.82
  1106.6 2.6 collective-permute-done.82
  1111.3 3.4 collective-permute-done.86
  1114.7 2.9 collective-permute-start.83
  1119.8 3.4 collective-permute-start.87
  1123.2 6.1 collective-permute-done.87
  (875 shorter events, 370.4 us)
Async XLA Ops:
  4.0 15.3 %collective-permute-start.12 = (bf16[1,1,1,1,1,29,128]{6,5,4,3,2,1,0:T(8,128)(2,1)S(1)}, bf16[1,1,1,1,1,29,128]{6,5,4,3,2,1,0:T(8,128)(2,1)S(1)}, u32[]{:S(2)}, u32[]{:S(2)}) collective-permute-start(bf16[1,1,1,1,1,29,128]{6,5,4,3,2,1,0:T(8,128)(2,1)S(1)} %get-tuple-element.164), channel_id=1, source_target_pairs={{0,2},{1,3},{2,0},{3,1},{4,6},{5,7},{6,4},{7,5},{8,10},{9,11},{10,... | collective-permute-start | bytes 22280 | tf_op jit(solution)/shard_map/ppermute | solution.py:54
  8.0 24.9 %collective-permute-start.6 = (bf16[1,24,1152]{2,1,0:T(8,128)(2,1)S(1)}, bf16[1,24,1152]{2,1,0:T(8,128)(2,1)S(1)}, u32[]{:S(2)}, u32[]{:S(2)}) collective-permute-start(bf16[1,24,1152]{2,1,0:T(8,128)(2,1)S(1)} %get-tuple-element.130), channel_id=1, source_target_pairs={{0,16},{1,17},{2,18},{3,19},{4,20},{5,21},{6,22},{7,23},{8,24},{9,... | collective-permute-start | bytes 165896 | tf_op jit(solution)/shard_map/ppermute | solution.py:54
  10.6 22.5 %collective-permute-start = (bf16[1,24,1152]{2,1,0:T(8,128)(2,1)S(1)}, bf16[1,24,1152]{2,1,0:T(8,128)(2,1)S(1)}, u32[]{:S(2)}, u32[]{:S(2)}) collective-permute-start(bf16[1,24,1152]{2,1,0:T(8,128)(2,1)S(1)} %get-tuple-element.131), channel_id=1, source_target_pairs={{0,16},{1,17},{2,18},{3,19},{4,20},{5,21},{6,22},{7,23},{8,24},{9,... | collective-permute-start | bytes 165896 | tf_op jit(solution)/shard_map/ppermute | solution.py:54
  11.8 10.1 collective-permute-start.17
  19.3 25.5 %collective-permute-start.35 = (bf16[1,24,1536]{2,1,0:T(8,128)(2,1)S(1)}, bf16[1,24,1536]{2,1,0:T(8,128)(2,1)S(1)}, u32[]{:S(2)}, u32[]{:S(2)}) collective-permute-start(bf16[1,24,1536]{2,1,0:T(8,128)(2,1)S(1)} %get-tuple-element.128), channel_id=1, source_target_pairs={{0,16},{1,17},{2,18},{3,19},{4,20},{5,21},{6,22},{7,23},{8,24},{9,... | collective-permute-start | bytes 221192 | tf_op jit(solution)/shard_map/ppermute | solution.py:54
  21.9 24.5 %collective-permute-start.29 = (bf16[1,24,1536]{2,1,0:T(8,128)(2,1)S(1)}, bf16[1,24,1536]{2,1,0:T(8,128)(2,1)S(1)}, u32[]{:S(2)}, u32[]{:S(2)}) collective-permute-start(bf16[1,24,1536]{2,1,0:T(8,128)(2,1)S(1)} %get-tuple-element.129), channel_id=1, source_target_pairs={{0,16},{1,17},{2,18},{3,19},{4,20},{5,21},{6,22},{7,23},{8,24},{9,... | collective-permute-start | bytes 221192 | tf_op jit(solution)/shard_map/ppermute | solution.py:54
  30.1 16.6 %collective-permute-start.41 = (bf16[1,96,384]{2,1,0:T(8,128)(2,1)S(1)}, bf16[1,96,384]{2,1,0:T(8,128)(2,1)S(1)}, u32[]{:S(2)}, u32[]{:S(2)}) collective-permute-start(bf16[1,96,384]{2,1,0:T(8,128)(2,1)S(1)} %get-tuple-element.127), channel_id=1, source_target_pairs={{0,16},{1,17},{2,18},{3,19},{4,20},{5,21},{6,22},{7,23},{8,24},{9,... | collective-permute-start | bytes 221192 | tf_op jit(solution)/shard_map/ppermute | solution.py:54
  32.9 15.4 %collective-permute-start.47 = (bf16[1,96,384]{2,1,0:T(8,128)(2,1)S(1)}, bf16[1,96,384]{2,1,0:T(8,128)(2,1)S(1)}, u32[]{:S(2)}, u32[]{:S(2)}) collective-permute-start(bf16[1,96,384]{2,1,0:T(8,128)(2,1)S(1)} %get-tuple-element.126), channel_id=1, source_target_pairs={{0,16},{1,17},{2,18},{3,19},{4,20},{5,21},{6,22},{7,23},{8,24},{9,... | collective-permute-start | bytes 221192 | tf_op jit(solution)/shard_map/ppermute | solution.py:54
  42.1 10.2 collective-permute-start.55
  44.8 17.3 %collective-permute-start.63 = (bf16[1,1,1,120,768]{4,3,2,1,0:T(8,128)(2,1)S(1)}, bf16[1,1,1,120,768]{4,3,2,1,0:T(8,128)(2,1)S(1)}, u32[]{:S(2)}, u32[]{:S(2)}) collective-permute-start(bf16[1,1,1,120,768]{4,3,2,1,0:T(8,128)(2,1)S(1)} %get-tuple-element.125), channel_id=1, source_target_pairs={{0,4},{1,5},{2,6},{3,7},{4,0},{5,1},{6,2},{7,3},{8,12},{9,13},{10,... | collective-permute-start | bytes 552968 | tf_op jit(solution)/shard_map/ppermute | solution.py:54
  46.7 11.8 %collective-permute-start.7 = (bf16[2,24,1152]{2,1,0:T(8,128)(2,1)S(1)}, bf16[2,24,1152]{2,1,0:T(8,128)(2,1)S(1)}, u32[]{:S(2)}, u32[]{:S(2)}) collective-permute-start(bf16[2,24,1152]{2,1,0:T(8,128)(2,1)S(1)} %pad_maximum_fusion.25), channel_id=1, source_target_pairs={{0,8},{1,9},{2,10},{3,11},{4,12},{5,13},{6,14},{7,15},{8,0},{9,1},... | collective-permute-start | bytes 331784 | tf_op jit(solution)/shard_map/ppermute | solution.py:54
  48.3 12.5 %collective-permute-start.1 = (bf16[2,24,1152]{2,1,0:T(8,128)(2,1)S(1)}, bf16[2,24,1152]{2,1,0:T(8,128)(2,1)S(1)}, u32[]{:S(2)}, u32[]{:S(2)}) collective-permute-start(bf16[2,24,1152]{2,1,0:T(8,128)(2,1)S(1)} %pad_maximum_fusion.24), channel_id=1, source_target_pairs={{0,8},{1,9},{2,10},{3,11},{4,12},{5,13},{6,14},{7,15},{8,0},{9,1},... | collective-permute-start | bytes 331784 | tf_op jit(solution)/shard_map/ppermute | solution.py:54
  63.0 14.0 %collective-permute-start.56 = (bf16[2,1,24,1344]{3,2,1,0:T(8,128)(2,1)}, bf16[2,1,24,1344]{3,2,1,0:T(8,128)(2,1)}, u32[]{:S(2)}, u32[]{:S(2)}) collective-permute-start(bf16[2,1,24,1344]{3,2,1,0:T(8,128)(2,1)} %get-tuple-element.115), channel_id=1, source_target_pairs={{0,8},{1,9},{2,10},{3,11},{4,12},{5,13},{6,14},{7,15},{8,0},{9,1},... | collective-permute-start | bytes 387080 | tf_op jit(solution)/shard_map/ppermute | solution.py:54
  65.2 15.9 %collective-permute-start.21 = (bf16[8,24,384]{2,1,0:T(8,128)(2,1)S(1)}, bf16[8,24,384]{2,1,0:T(8,128)(2,1)}, u32[]{:S(2)}, u32[]{:S(2)}) collective-permute-start(bf16[8,24,384]{2,1,0:T(8,128)(2,1)S(1)} %pad_maximum_fusion.17.refs_0_), channel_id=1, source_target_pairs={{0,4},{1,5},{2,6},{3,7},{4,0},{5,1},{6,2},{7,3},{8,12},{9,13},{10,... | collective-permute-start | bytes 442376 | tf_op jit(solution)/shard_map/ppermute | solution.py:54
  66.3 20.2 %collective-permute-start.20 = (bf16[8,24,384]{2,1,0:T(8,128)(2,1)S(1)}, bf16[8,24,384]{2,1,0:T(8,128)(2,1)}, u32[]{:S(2)}, u32[]{:S(2)}) collective-permute-start(bf16[8,24,384]{2,1,0:T(8,128)(2,1)S(1)} %pad_maximum_fusion.17.refs_0_), channel_id=1, source_target_pairs={{0,1},{1,0},{2,3},{3,2},{4,5},{5,4},{6,7},{7,6},{8,9},{9,8},{10,11... | collective-permute-start | bytes 442376 | tf_op jit(solution)/shard_map/ppermute | solution.py:54
  67.1 14.1 %collective-permute-start.27 = (bf16[8,24,384]{2,1,0:T(8,128)(2,1)S(1)}, bf16[8,24,384]{2,1,0:T(8,128)(2,1)}, u32[]{:S(2)}, u32[]{:S(2)}) collective-permute-start(bf16[8,24,384]{2,1,0:T(8,128)(2,1)S(1)} %pad_maximum_fusion.18.refs_4_), channel_id=1, source_target_pairs={{0,2},{1,3},{2,0},{3,1},{4,6},{5,7},{6,4},{7,5},{8,10},{9,11},{10,... | collective-permute-start | bytes 442376 | tf_op jit(solution)/shard_map/ppermute | solution.py:54
  68.4 11.2 collective-permute-start.8
  79.6 48.7 %collective-permute-start.57 = (bf16[4,1,1,1,24,1344]{5,4,3,2,1,0:T(8,128)(2,1)S(1)}, bf16[4,1,1,1,24,1344]{5,4,3,2,1,0:T(8,128)(2,1)S(1)}, u32[]{:S(2)}, u32[]{:S(2)}) collective-permute-start(bf16[4,1,1,1,24,1344]{5,4,3,2,1,0:T(8,128)(2,1)S(1)} %bitcast.293), channel_id=1, source_target_pairs={{0,2},{1,3},{2,0},{3,1},{4,6},{5,7},{6,4},{7,5},{8,10},{9,11},{10,... | collective-permute-start | bytes 774152 | tf_op jit(solution)/shard_map/ppermute | solution.py:54
  86.5 43.5 %collective-permute-start.37 = (bf16[4,24,1536]{2,1,0:T(8,128)(2,1)}, bf16[4,24,1536]{2,1,0:T(8,128)(2,1)}, u32[]{:S(2)}, u32[]{:S(2)}) collective-permute-start(bf16[4,24,1536]{2,1,0:T(8,128)(2,1)} %pad_maximum_fusion.11), channel_id=1, source_target_pairs={{0,4},{1,5},{2,6},{3,7},{4,0},{5,1},{6,2},{7,3},{8,12},{9,13},{10,... | collective-permute-start | bytes 884744 | tf_op jit(solution)/shard_map/ppermute | solution.py:54
  86.9 43.5 %collective-permute-start.31 = (bf16[4,24,1536]{2,1,0:T(8,128)(2,1)}, bf16[4,24,1536]{2,1,0:T(8,128)(2,1)}, u32[]{:S(2)}, u32[]{:S(2)}) collective-permute-start(bf16[4,24,1536]{2,1,0:T(8,128)(2,1)} %pad_maximum_fusion.10), channel_id=1, source_target_pairs={{0,2},{1,3},{2,0},{3,1},{4,6},{5,7},{6,4},{7,5},{8,10},{9,11},{10,... | collective-permute-start | bytes 884744 | tf_op jit(solution)/shard_map/ppermute | solution.py:54
  89.1 46.7 %collective-permute-start.43 = (bf16[4,96,384]{2,1,0:T(8,128)(2,1)}, bf16[4,96,384]{2,1,0:T(8,128)(2,1)S(1)}, u32[]{:S(2)}, u32[]{:S(2)}) collective-permute-start(bf16[4,96,384]{2,1,0:T(8,128)(2,1)} %pad_maximum_fusion.12), channel_id=1, source_target_pairs={{0,2},{1,3},{2,0},{3,1},{4,6},{5,7},{6,4},{7,5},{8,10},{9,11},{10,... | collective-permute-start | bytes 884744 | tf_op jit(solution)/shard_map/ppermute | solution.py:54
  89.7 46.0 %collective-permute-start.49 = (bf16[4,96,384]{2,1,0:T(8,128)(2,1)}, bf16[4,96,384]{2,1,0:T(8,128)(2,1)}, u32[]{:S(2)}, u32[]{:S(2)}) collective-permute-start(bf16[4,96,384]{2,1,0:T(8,128)(2,1)} %pad_maximum_fusion.13), channel_id=1, source_target_pairs={{0,4},{1,5},{2,6},{3,7},{4,0},{5,1},{6,2},{7,3},{8,12},{9,13},{10,... | collective-permute-start | bytes 884744 | tf_op jit(solution)/shard_map/ppermute | solution.py:54
  128.3 11.8 %collective-permute-start.10 = (bf16[8,24,1152]{2,1,0:T(8,128)(2,1)S(1)}, bf16[8,24,1152]{2,1,0:T(8,128)(2,1)S(1)}, u32[]{:S(2)}, u32[]{:S(2)}) collective-permute-start(bf16[8,24,1152]{2,1,0:T(8,128)(2,1)S(1)} %pad_maximum_fusion.8.refs_4_), channel_id=1, source_target_pairs={{0,2},{1,3},{2,0},{3,1},{4,6},{5,7},{6,4},{7,5},{8,10},{9,11},{10,... | collective-permute-start | bytes 1327112 | tf_op jit(solution)/shard_map/ppermute | solution.py:54
  130.0 13.2 %collective-permute-start.4 = (bf16[8,24,1152]{2,1,0:T(8,128)(2,1)S(1)}, bf16[8,24,1152]{2,1,0:T(8,128)(2,1)S(1)}, u32[]{:S(2)}, u32[]{:S(2)}) collective-permute-start(bf16[8,24,1152]{2,1,0:T(8,128)(2,1)S(1)} %pad_maximum_fusion.7.refs_0_), channel_id=1, source_target_pairs={{0,4},{1,5},{2,6},{3,7},{4,0},{5,1},{6,2},{7,3},{8,12},{9,13},{10,... | collective-permute-start | bytes 1327112 | tf_op jit(solution)/shard_map/ppermute | solution.py:54
  130.4 22.4 %collective-permute-start.58 = (bf16[4,1,2,1,24,1344]{5,4,3,2,1,0:T(8,128)(2,1)S(1)}, bf16[4,1,2,1,24,1344]{5,4,3,2,1,0:T(8,128)(2,1)S(1)}, u32[]{:S(2)}, u32[]{:S(2)}) collective-permute-start(bf16[4,1,2,1,24,1344]{5,4,3,2,1,0:T(8,128)(2,1)S(1)} %maximum_select_fusion.5), channel_id=1, source_target_pairs={{0,4},{1,5},{2,6},{3,7},{4,0},{5,1},{6,2},{7,3},{8,12},{9,13},{10,... | collective-permute-start | bytes 1548296 | tf_op jit(solution)/shard_map/ppermute | solution.py:54
  135.7 19.1 %collective-permute-start.3 = (bf16[8,24,1152]{2,1,0:T(8,128)(2,1)S(1)}, bf16[8,24,1152]{2,1,0:T(8,128)(2,1)S(1)}, u32[]{:S(2)}, u32[]{:S(2)}) collective-permute-start(bf16[8,24,1152]{2,1,0:T(8,128)(2,1)S(1)} %pad_maximum_fusion.7.refs_0_), channel_id=1, source_target_pairs={{0,1},{1,0},{2,3},{3,2},{4,5},{5,4},{6,7},{7,6},{8,9},{9,8},{10,11... | collective-permute-start | bytes 1327112 | tf_op jit(solution)/shard_map/ppermute | solution.py:54
  135.8 19.1 %collective-permute-start.9 = (bf16[8,24,1152]{2,1,0:T(8,128)(2,1)S(1)}, bf16[8,24,1152]{2,1,0:T(8,128)(2,1)S(1)}, u32[]{:S(2)}, u32[]{:S(2)}) collective-permute-start(bf16[8,24,1152]{2,1,0:T(8,128)(2,1)S(1)} %pad_maximum_fusion.8.refs_4_), channel_id=1, source_target_pairs={{0,1},{1,0},{2,3},{3,2},{4,5},{5,4},{6,7},{7,6},{8,9},{9,8},{10,11... | collective-permute-start | bytes 1327112 | tf_op jit(solution)/shard_map/ppermute | solution.py:54
  140.1 15.3 %collective-permute-start.11 = (bf16[8,24,1152]{2,1,0:T(8,128)(2,1)S(1)}, bf16[8,24,1152]{2,1,0:T(8,128)(2,1)S(1)}, u32[]{:S(2)}, u32[]{:S(2)}) collective-permute-start(bf16[8,24,1152]{2,1,0:T(8,128)(2,1)S(1)} %collective-permute-done.10.refs_6_), channel_id=1, source_target_pairs={{0,1},{1,0},{2,3},{3,2},{4,5},{5,4},{6,7},{7,6},{8,9},{9,8},{10,11... | collective-permute-start | bytes 1327112 | tf_op jit(solution)/shard_map/ppermute | solution.py:54
  143.1 12.5 %collective-permute-start.5 = (bf16[8,24,1152]{2,1,0:T(8,128)(2,1)S(1)}, bf16[8,24,1152]{2,1,0:T(8,128)(2,1)S(1)}, u32[]{:S(2)}, u32[]{:S(2)}) collective-permute-start(bf16[8,24,1152]{2,1,0:T(8,128)(2,1)S(1)} %collective-permute-done.4.refs_2_), channel_id=1, source_target_pairs={{0,1},{1,0},{2,3},{3,2},{4,5},{5,4},{6,7},{7,6},{8,9},{9,8},{10,11... | collective-permute-start | bytes 1327112 | tf_op jit(solution)/shard_map/ppermute | solution.py:54
  152.8 162.4 %collective-permute-start.39 = (bf16[8,24,1536]{2,1,0:T(8,128)(2,1)}, bf16[8,24,1536]{2,1,0:T(8,128)(2,1)}, u32[]{:S(2)}, u32[]{:S(2)}) collective-permute-start(bf16[8,24,1536]{2,1,0:T(8,128)(2,1)} %pad_maximum_fusion.2.refs_4_), channel_id=1, source_target_pairs={{0,2},{1,3},{2,0},{3,1},{4,6},{5,7},{6,4},{7,5},{8,10},{9,11},{10,... | collective-permute-start | bytes 1769480 | tf_op jit(solution)/shard_map/ppermute | solution.py:54
  154.9 161.5 %collective-permute-start.38 = (bf16[8,24,1536]{2,1,0:T(8,128)(2,1)}, bf16[8,24,1536]{2,1,0:T(8,128)(2,1)}, u32[]{:S(2)}, u32[]{:S(2)}) collective-permute-start(bf16[8,24,1536]{2,1,0:T(8,128)(2,1)} %pad_maximum_fusion.2.refs_4_), channel_id=1, source_target_pairs={{0,1},{1,0},{2,3},{3,2},{4,5},{5,4},{6,7},{7,6},{8,9},{9,8},{10,11... | collective-permute-start | bytes 1769480 | tf_op jit(solution)/shard_map/ppermute | solution.py:54
  154.9 161.4 %collective-permute-start.33 = (bf16[8,24,1536]{2,1,0:T(8,128)(2,1)}, bf16[8,24,1536]{2,1,0:T(8,128)(2,1)}, u32[]{:S(2)}, u32[]{:S(2)}) collective-permute-start(bf16[8,24,1536]{2,1,0:T(8,128)(2,1)} %pad_maximum_fusion.1.refs_0_), channel_id=1, source_target_pairs={{0,4},{1,5},{2,6},{3,7},{4,0},{5,1},{6,2},{7,3},{8,12},{9,13},{10,... | collective-permute-start | bytes 1769480 | tf_op jit(solution)/shard_map/ppermute | solution.py:54
  155.4 162.0 %collective-permute-start.32 = (bf16[8,24,1536]{2,1,0:T(8,128)(2,1)}, bf16[8,24,1536]{2,1,0:T(8,128)(2,1)}, u32[]{:S(2)}, u32[]{:S(2)}) collective-permute-start(bf16[8,24,1536]{2,1,0:T(8,128)(2,1)} %pad_maximum_fusion.1.refs_0_), channel_id=1, source_target_pairs={{0,1},{1,0},{2,3},{3,2},{4,5},{5,4},{6,7},{7,6},{8,9},{9,8},{10,11... | collective-permute-start | bytes 1769480 | tf_op jit(solution)/shard_map/ppermute | solution.py:54
  156.9 161.5 %collective-permute-start.45 = (bf16[8,96,384]{2,1,0:T(8,128)(2,1)}, bf16[8,96,384]{2,1,0:T(8,128)(2,1)}, u32[]{:S(2)}, u32[]{:S(2)}) collective-permute-start(bf16[8,96,384]{2,1,0:T(8,128)(2,1)} %pad_maximum_fusion.3.refs_0_), channel_id=1, source_target_pairs={{0,4},{1,5},{2,6},{3,7},{4,0},{5,1},{6,2},{7,3},{8,12},{9,13},{10,... | collective-permute-start | bytes 1769480 | tf_op jit(solution)/shard_map/ppermute | solution.py:54
  315.2 16.6 %collective-permute-start.51 = (bf16[8,96,384]{2,1,0:T(8,128)(2,1)}, bf16[8,96,384]{2,1,0:T(8,128)(2,1)}, u32[]{:S(2)}, u32[]{:S(2)}) collective-permute-start(bf16[8,96,384]{2,1,0:T(8,128)(2,1)} %pad_maximum_fusion.4.refs_4_), channel_id=1, source_target_pairs={{0,2},{1,3},{2,0},{3,1},{4,6},{5,7},{6,4},{7,5},{8,10},{9,11},{10,... | collective-permute-start | bytes 1769480 | tf_op jit(solution)/shard_map/ppermute | solution.py:54
  316.4 15.4 %collective-permute-start.40 = (bf16[8,24,1536]{2,1,0:T(8,128)(2,1)}, bf16[8,24,1536]{2,1,0:T(8,128)(2,1)}, u32[]{:S(2)}, u32[]{:S(2)}) collective-permute-start(bf16[8,24,1536]{2,1,0:T(8,128)(2,1)} %collective-permute-done.39.refs_6_), channel_id=1, source_target_pairs={{0,1},{1,0},{2,3},{3,2},{4,5},{5,4},{6,7},{7,6},{8,9},{9,8},{10,11... | collective-permute-start | bytes 1769480 | tf_op jit(solution)/shard_map/ppermute | solution.py:54
  316.4 15.9 %collective-permute-start.34 = (bf16[8,24,1536]{2,1,0:T(8,128)(2,1)}, bf16[8,24,1536]{2,1,0:T(8,128)(2,1)}, u32[]{:S(2)}, u32[]{:S(2)}) collective-permute-start(bf16[8,24,1536]{2,1,0:T(8,128)(2,1)} %collective-permute-done.33.refs_2_), channel_id=1, source_target_pairs={{0,1},{1,0},{2,3},{3,2},{4,5},{5,4},{6,7},{7,6},{8,9},{9,8},{10,11... | collective-permute-start | bytes 1769480 | tf_op jit(solution)/shard_map/ppermute | solution.py:54
  317.4 328.4 %collective-permute-start.64 = (bf16[2,1,1,120,768]{4,3,2,1,0:T(8,128)(2,1)}, bf16[2,1,1,120,768]{4,3,2,1,0:T(8,128)(2,1)}, u32[]{:S(2)}, u32[]{:S(2)}) collective-permute-start(bf16[2,1,1,120,768]{4,3,2,1,0:T(8,128)(2,1)} %maximum_select_fusion.7), channel_id=1, source_target_pairs={{0,2},{1,3},{2,0},{3,1},{4,6},{5,7},{6,4},{7,5},{8,10},{9,11},{10,... | collective-permute-start | bytes 1105928 | tf_op jit(solution)/shard_map/ppermute | solution.py:54
  318.4 170.3 %collective-permute-start.44 = (bf16[8,96,384]{2,1,0:T(8,128)(2,1)}, bf16[8,96,384]{2,1,0:T(8,128)(2,1)}, u32[]{:S(2)}, u32[]{:S(2)}) collective-permute-start(bf16[8,96,384]{2,1,0:T(8,128)(2,1)} %pad_maximum_fusion.3.refs_0_), channel_id=1, source_target_pairs={{0,1},{1,0},{2,3},{3,2},{4,5},{5,4},{6,7},{7,6},{8,9},{9,8},{10,11... | collective-permute-start | bytes 1769480 | tf_op jit(solution)/shard_map/ppermute | solution.py:54
  331.8 157.4 %collective-permute-start.50 = (bf16[8,96,384]{2,1,0:T(8,128)(2,1)}, bf16[8,96,384]{2,1,0:T(8,128)(2,1)}, u32[]{:S(2)}, u32[]{:S(2)}) collective-permute-start(bf16[8,96,384]{2,1,0:T(8,128)(2,1)} %pad_maximum_fusion.4.refs_4_), channel_id=1, source_target_pairs={{0,1},{1,0},{2,3},{3,2},{4,5},{5,4},{6,7},{7,6},{8,9},{9,8},{10,11... | collective-permute-start | bytes 1769480 | tf_op jit(solution)/shard_map/ppermute | solution.py:54
  331.8 157.4 %collective-permute-start.46 = (bf16[8,96,384]{2,1,0:T(8,128)(2,1)}, bf16[8,96,384]{2,1,0:T(8,128)(2,1)}, u32[]{:S(2)}, u32[]{:S(2)}) collective-permute-start(bf16[8,96,384]{2,1,0:T(8,128)(2,1)} %collective-permute-done.45.refs_2_), channel_id=1, source_target_pairs={{0,1},{1,0},{2,3},{3,2},{4,5},{5,4},{6,7},{7,6},{8,9},{9,8},{10,11... | collective-permute-start | bytes 1769480 | tf_op jit(solution)/shard_map/ppermute | solution.py:54
  332.3 156.9 %collective-permute-start.52 = (bf16[8,96,384]{2,1,0:T(8,128)(2,1)}, bf16[8,96,384]{2,1,0:T(8,128)(2,1)}, u32[]{:S(2)}, u32[]{:S(2)}) collective-permute-start(bf16[8,96,384]{2,1,0:T(8,128)(2,1)} %collective-permute-done.51.refs_6_), channel_id=1, source_target_pairs={{0,1},{1,0},{2,3},{3,2},{4,5},{5,4},{6,7},{7,6},{8,9},{9,8},{10,11... | collective-permute-start | bytes 1769480 | tf_op jit(solution)/shard_map/ppermute | solution.py:54
  488.7 161.6 %collective-permute-start.59 = (bf16[4,2,2,1,24,1344]{5,4,3,2,1,0:T(8,128)(2,1)}, bf16[4,2,2,1,24,1344]{5,4,3,2,1,0:T(8,128)(2,1)}, u32[]{:S(2)}, u32[]{:S(2)}) collective-permute-start(bf16[4,2,2,1,24,1344]{5,4,3,2,1,0:T(8,128)(2,1)} %maximum_select_fusion.2), channel_id=1, source_target_pairs={{0,1},{1,0},{2,3},{3,2},{4,5},{5,4},{6,7},{7,6},{8,9},{9,8},{10,11... | collective-permute-start | bytes 3096584 | tf_op jit(solution)/shard_map/ppermute | solution.py:54
  647.0 14.8 %collective-permute-start.65 = (bf16[2,2,1,120,768]{4,3,2,1,0:T(8,128)(2,1)S(1)}, bf16[2,2,1,120,768]{4,3,2,1,0:T(8,128)(2,1)S(1)}, u32[]{:S(2)}, u32[]{:S(2)}) collective-permute-start(bf16[2,2,1,120,768]{4,3,2,1,0:T(8,128)(2,1)S(1)} %maximum_select_fusion.3), channel_id=1, source_target_pairs={{0,1},{1,0},{2,3},{3,2},{4,5},{5,4},{6,7},{7,6},{8,9},{9,8},{10,11... | collective-permute-start | bytes 2211848 | tf_op jit(solution)/shard_map/ppermute | solution.py:54
  679.9 27.3 %collective-permute-start.70 = (bf16[8,768]{1,0:T(8,128)(2,1)}, bf16[8,768]{1,0:T(8,128)(2,1)}, u32[]{:S(2)}, u32[]{:S(2)}) collective-permute-start(bf16[8,768]{1,0:T(8,128)(2,1)} %bitcast.254), channel_id=1, source_target_pairs={{0,8},{1,9},{2,10},{3,11},{4,12},{5,13},{6,14},{7,15},{8,0},{9,1},... | collective-permute-start | bytes 36872 | tf_op jit(solution)/shard_map/ppermute | solution.py:54
  684.7 15.3 %collective-permute-start.67 = (f32[32,768]{1,0:T(8,128)}, f32[32,768]{1,0:T(8,128)}, u32[]{:S(2)}, u32[]{:S(2)}) collective-permute-start(f32[32,768]{1,0:T(8,128)} %add.619), channel_id=1, source_target_pairs={{0,16},{1,17},{2,18},{3,19},{4,20},{5,21},{6,22},{7,23},{8,24},{9,... | collective-permute-start | bytes 294920 | tf_op jit(solution)/shard_map/ppermute | solution.py:54
  739.6 18.4 %collective-permute-start.73 = (f32[32,768]{1,0:T(8,128)}, f32[32,768]{1,0:T(8,128)}, u32[]{:S(2)}, u32[]{:S(2)}) collective-permute-start(f32[32,768]{1,0:T(8,128)} %add.646), channel_id=1, source_target_pairs={{0,16},{1,17},{2,18},{3,19},{4,20},{5,21},{6,22},{7,23},{8,24},{9,... | collective-permute-start | bytes 294920 | tf_op jit(solution)/shard_map/ppermute | solution.py:54
  796.1 194.2 %collective-permute-start.102 = (bf16[2,2,1,120,768]{4,3,2,1,0:T(8,128)(2,1)}, bf16[2,2,1,120,768]{4,3,2,1,0:T(8,128)(2,1)}, u32[]{:S(2)}, u32[]{:S(2)}) collective-permute-start(bf16[2,2,1,120,768]{4,3,2,1,0:T(8,128)(2,1)} %fusion.24), channel_id=1, source_target_pairs={{0,1},{1,0},{2,3},{3,2},{4,5},{5,4},{6,7},{7,6},{8,9},{9,8},{10,11... | collective-permute-start | bytes 2211848 | tf_op jit(solution)/shard_map/ppermute | solution.py:54
  799.8 18.0 %collective-permute-start.77 = (f32[1,2,8,768]{3,2,1,0:T(8,128)}, f32[1,2,8,768]{3,2,1,0:T(8,128)}, u32[]{:S(2)}, u32[]{:S(2)}) collective-permute-start(f32[1,2,8,768]{3,2,1,0:T(8,128)} %constant_dynamic-slice_fusion.71), channel_id=1, source_target_pairs={{0,16},{1,17},{2,18},{3,19},{4,20},{5,21},{6,22},{7,23},{8,24},{9,... | collective-permute-start | bytes 147464 | tf_op jit(solution)/shard_map/ppermute | solution.py:54
  824.5 226.1 %collective-permute-start.88 = (bf16[4,2,2,1,24,1344]{5,4,3,2,1,0:T(8,128)(2,1)}, bf16[4,2,2,1,24,1344]{5,4,3,2,1,0:T(8,128)(2,1)}, u32[]{:S(2)}, u32[]{:S(2)}) collective-permute-start(bf16[4,2,2,1,24,1344]{5,4,3,2,1,0:T(8,128)(2,1)} %constant_dynamic-slice_fusion.59), channel_id=1, source_target_pairs={{0,1},{1,0},{2,3},{3,2},{4,5},{5,4},{6,7},{7,6},{8,9},{9,8},{10,11... | collective-permute-start | bytes 3096584 | tf_op jit(solution)/shard_map/ppermute | solution.py:54
  963.2 16.7 %collective-permute-start.128 = (f32[2,2,2,2,1,3360]{5,4,3,2,1,0:T(1,128)S(1)}, f32[2,2,2,2,1,3360]{5,4,3,2,1,0:T(1,128)S(1)}, u32[]{:S(2)}, u32[]{:S(2)}) collective-permute-start(f32[2,2,2,2,1,3360]{5,4,3,2,1,0:T(1,128)S(1)} %constant_dynamic-slice_fusion.6), channel_id=1, source_target_pairs={{0,1},{1,0},{2,3},{3,2},{4,5},{5,4},{6,7},{7,6},{8,9},{9,8},{10,11... | collective-permute-start | bytes 645128 | tf_op jit(solution)/shard_map/ppermute | solution.py:54
  967.6 125.0 %collective-permute-start.114 = (bf16[2,2,2,2,1,96,768]{6,5,4,3,2,1,0:T(8,128)(2,1)}, bf16[2,2,2,2,1,96,768]{6,5,4,3,2,1,0:T(8,128)(2,1)}, u32[]{:S(2)}, u32[]{:S(2)}) collective-permute-start(bf16[2,2,2,2,1,96,768]{6,5,4,3,2,1,0:T(8,128)(2,1)} %constant_dynamic-slice_fusion.30), channel_id=1, source_target_pairs={{0,1},{1,0},{2,3},{3,2},{4,5},{5,4},{6,7},{7,6},{8,9},{9,8},{10,11... | collective-permute-start | bytes 7077896 | tf_op jit(solution)/shard_map/ppermute | solution.py:54
  979.8 117.9 %collective-permute-start.105 = (bf16[2,2,2,2,1,24,3072]{6,5,4,3,2,1,0:T(8,128)(2,1)}, bf16[2,2,2,2,1,24,3072]{6,5,4,3,2,1,0:T(8,128)(2,1)}, u32[]{:S(2)}, u32[]{:S(2)}) collective-permute-start(bf16[2,2,2,2,1,24,3072]{6,5,4,3,2,1,0:T(8,128)(2,1)} %constant_dynamic-slice_fusion.39), channel_id=1, source_target_pairs={{0,1},{1,0},{2,3},{3,2},{4,5},{5,4},{6,7},{7,6},{8,9},{9,8},{10,11... | collective-permute-start | bytes 7077896 | tf_op jit(solution)/shard_map/ppermute | solution.py:54
  990.2 11.5 collective-permute-start.93
  998.9 73.0 %collective-permute-start.79 = (bf16[2,2,2,2,1,24,2304]{6,5,4,3,2,1,0:T(8,128)(2,1)}, bf16[2,2,2,2,1,24,2304]{6,5,4,3,2,1,0:T(8,128)(2,1)}, u32[]{:S(2)}, u32[]{:S(2)}) collective-permute-start(bf16[2,2,2,2,1,24,2304]{6,5,4,3,2,1,0:T(8,128)(2,1)} %constant_dynamic-slice_fusion.68), channel_id=1, source_target_pairs={{0,1},{1,0},{2,3},{3,2},{4,5},{5,4},{6,7},{7,6},{8,9},{9,8},{10,11... | collective-permute-start | bytes 5308424 | tf_op jit(solution)/shard_map/ppermute | solution.py:54
  1001.7 11.0 collective-permute-start.103
  1074.9 12.3 %collective-permute-start.80 = (bf16[2,2,1,2,1,24,1152]{6,5,4,3,2,1,0:T(8,128)(2,1)}, bf16[2,2,1,2,1,24,1152]{6,5,4,3,2,1,0:T(8,128)(2,1)S(1)}, u32[]{:S(2)}, u32[]{:S(2)}) collective-permute-start(bf16[2,2,1,2,1,24,1152]{6,5,4,3,2,1,0:T(8,128)(2,1)} %constant_dynamic-slice_fusion.67), channel_id=1, source_target_pairs={{0,4},{1,5},{2,6},{3,7},{4,0},{5,1},{6,2},{7,3},{8,12},{9,13},{10,... | collective-permute-start | bytes 1327112 | tf_op jit(solution)/shard_map/ppermute | solution.py:54
  1077.4 12.3 %collective-permute-start.84 = (bf16[2,2,2,1,1,24,1152]{6,5,4,3,2,1,0:T(8,128)(2,1)}, bf16[2,2,2,1,1,24,1152]{6,5,4,3,2,1,0:T(8,128)(2,1)}, u32[]{:S(2)}, u32[]{:S(2)}) collective-permute-start(bf16[2,2,2,1,1,24,1152]{6,5,4,3,2,1,0:T(8,128)(2,1)} %constant_dynamic-slice_fusion.63), channel_id=1, source_target_pairs={{0,2},{1,3},{2,0},{3,1},{4,6},{5,7},{6,4},{7,5},{8,10},{9,11},{10,... | collective-permute-start | bytes 1327112 | tf_op jit(solution)/shard_map/ppermute | solution.py:54
  1087.3 15.5 %collective-permute-start.81 = (bf16[2,2,1,1,1,24,1152]{6,5,4,3,2,1,0:T(8,128)(2,1)S(1)}, bf16[2,2,1,1,1,24,1152]{6,5,4,3,2,1,0:T(8,128)(2,1)S(1)}, u32[]{:S(2)}, u32[]{:S(2)}) collective-permute-start(bf16[2,2,1,1,1,24,1152]{6,5,4,3,2,1,0:T(8,128)(2,1)S(1)} %constant_dynamic-slice_fusion.66), channel_id=1, source_target_pairs={{0,2},{1,3},{2,0},{3,1},{4,6},{5,7},{6,4},{7,5},{8,10},{9,11},{10,... | collective-permute-start | bytes 663560 | tf_op jit(solution)/shard_map/ppermute | solution.py:54
  1091.1 12.8 %collective-permute-start.85 = (bf16[2,2,1,1,1,24,1152]{6,5,4,3,2,1,0:T(8,128)(2,1)S(1)}, bf16[2,2,1,1,1,24,1152]{6,5,4,3,2,1,0:T(8,128)(2,1)S(1)}, u32[]{:S(2)}, u32[]{:S(2)}) collective-permute-start(bf16[2,2,1,1,1,24,1152]{6,5,4,3,2,1,0:T(8,128)(2,1)S(1)} %constant_dynamic-slice_fusion.62), channel_id=1, source_target_pairs={{0,4},{1,5},{2,6},{3,7},{4,0},{5,1},{6,2},{7,3},{8,12},{9,13},{10,... | collective-permute-start | bytes 663560 | tf_op jit(solution)/shard_map/ppermute | solution.py:54
  1096.2 34.0 %collective-permute-start.115 = (bf16[2,2,1,2,1,96,384]{6,5,4,3,2,1,0:T(8,128)(2,1)S(1)}, bf16[2,2,1,2,1,96,384]{6,5,4,3,2,1,0:T(8,128)(2,1)S(1)}, u32[]{:S(2)}, u32[]{:S(2)}) collective-permute-start(bf16[2,2,1,2,1,96,384]{6,5,4,3,2,1,0:T(8,128)(2,1)S(1)} %constant_dynamic-slice_fusion.29), channel_id=1, source_target_pairs={{0,4},{1,5},{2,6},{3,7},{4,0},{5,1},{6,2},{7,3},{8,12},{9,13},{10,... | collective-permute-start | bytes 1769480 | tf_op jit(solution)/shard_map/ppermute | solution.py:54
  1096.8 34.8 %collective-permute-start.119 = (bf16[2,2,2,1,1,96,384]{6,5,4,3,2,1,0:T(8,128)(2,1)S(1)}, bf16[2,2,2,1,1,96,384]{6,5,4,3,2,1,0:T(8,128)(2,1)S(1)}, u32[]{:S(2)}, u32[]{:S(2)}) collective-permute-start(bf16[2,2,2,1,1,96,384]{6,5,4,3,2,1,0:T(8,128)(2,1)S(1)} %constant_dynamic-slice_fusion.25), channel_id=1, source_target_pairs={{0,2},{1,3},{2,0},{3,1},{4,6},{5,7},{6,4},{7,5},{8,10},{9,11},{10,... | collective-permute-start | bytes 1769480 | tf_op jit(solution)/shard_map/ppermute | solution.py:54
  1100.6 31.3 %collective-permute-start.106 = (bf16[2,2,1,2,1,24,1536]{6,5,4,3,2,1,0:T(8,128)(2,1)S(1)}, bf16[2,2,1,2,1,24,1536]{6,5,4,3,2,1,0:T(8,128)(2,1)S(1)}, u32[]{:S(2)}, u32[]{:S(2)}) collective-permute-start(bf16[2,2,1,2,1,24,1536]{6,5,4,3,2,1,0:T(8,128)(2,1)S(1)} %constant_dynamic-slice_fusion.38), channel_id=1, source_target_pairs={{0,4},{1,5},{2,6},{3,7},{4,0},{5,1},{6,2},{7,3},{8,12},{9,13},{10,... | collective-permute-start | bytes 1769480 | tf_op jit(solution)/shard_map/ppermute | solution.py:54
  1102.8 30.3 %collective-permute-start.110 = (bf16[2,2,2,1,1,24,1536]{6,5,4,3,2,1,0:T(8,128)(2,1)S(1)}, bf16[2,2,2,1,1,24,1536]{6,5,4,3,2,1,0:T(8,128)(2,1)S(1)}, u32[]{:S(2)}, u32[]{:S(2)}) collective-permute-start(bf16[2,2,2,1,1,24,1536]{6,5,4,3,2,1,0:T(8,128)(2,1)S(1)} %constant_dynamic-slice_fusion.34), channel_id=1, source_target_pairs={{0,2},{1,3},{2,0},{3,1},{4,6},{5,7},{6,4},{7,5},{8,10},{9,11},{10,... | collective-permute-start | bytes 1769480 | tf_op jit(solution)/shard_map/ppermute | solution.py:54
  (175 other events, 5246.1 us)

commit v2 on v1

v2 whole, which is shorter than its diff:
```python
from functools import partial

import jax
import jax.numpy as jnp
from jax import lax
from jax.experimental import pallas as pl
from jax.experimental.pallas import tpu as pltpu
from jax.sharding import PartitionSpec as P

HDIM = 64
SEG = 128
TP = 4
AXES = ("ctx", "wa")
F32 = jnp.float32
BF16 = jnp.bfloat16
SCALE = HDIM ** (-0.5)


def dot(a, b, dims=((1,), (0,))):
    return lax.dot_general(a, b, (dims, ((), ())), preferred_element_type=F32)


def normalize(values):
    center = values - jnp.mean(values, axis=-1, keepdims=True)
    spread = jnp.mean(center * center, axis=-1, keepdims=True)
    inverse = lax.rsqrt(spread + 1e-05)
    return center * inverse, inverse


def normalize_back(grad, normal, inverse):
    return inverse * (
        grad
        - jnp.mean(grad, axis=-1, keepdims=True)
        - normal * jnp.mean(grad * normal, axis=-1, keepdims=True)
    )


def gelu_pair(values):
    phi = 0.5 * (1.0 + lax.erf(values * 0.7071067811865476))
    density = jnp.exp(-0.5 * values * values) * 0.3989422804014327
    return values * phi, phi + values * density


class Net:
    def __init__(self, count):
        self.count = count
        self.bits = count.bit_length() - 1
        self.me = lax.axis_index(AXES)

    def bit(self, b):
        return (self.me >> b) & 1

    def hop(self, value, b):
        return lax.ppermute(value, AXES, [(i, i ^ (1 << b)) for i in range(self.count)])

    def grow(self, value, b, axis):
        other = self.hop(value, b)
        return jnp.where(
            self.bit(b) == 0,
            jnp.concatenate([value, other], axis),
            jnp.concatenate([other, value], axis),
        )

    def pick(self, value, which, axis):
        return lax.dynamic_slice_in_dim(value, which, 1, axis)


def tie(*values):
    return lax.optimization_barrier(values)


def place_blocks(net, parts, blocks, shapes):
    arrays = [part[0] for part in parts]

    def body(me_ref, *refs):
        sources = refs[: len(parts)]
        targets = refs[len(parts) : len(parts) + len(shapes)]
        sem = refs[-1]
        me = me_ref[0]
        for source, (array, masks, half) in zip(sources, parts):
            for j, mask in enumerate(masks):
                for row, rows, lane, lanes, which, to_row, to_lane in blocks(half):
                    pltpu.make_async_copy(
                        source.at[j, pl.ds(row, rows), pl.ds(lane, lanes)],
                        targets[which].at[me ^ mask, pl.ds(to_row, rows), pl.ds(to_lane, lanes)],
                        sem,
                    ).start()
        for target in targets:
            pltpu.make_async_copy(target, target, sem).wait()

    return pl.pallas_call(
        body,
        out_shape=[jax.ShapeDtypeStruct(shape, BF16) for shape in shapes],
        in_specs=[pl.BlockSpec(memory_space=pltpu.SMEM)]
        + [pl.BlockSpec(memory_space=pl.ANY)] * len(parts),
        out_specs=[pl.BlockSpec(memory_space=pltpu.VMEM)] * len(shapes),
        scratch_shapes=[pltpu.SemaphoreType.DMA],
        name="place_blocks",
    )(net.me.reshape(1), *arrays)


def link_orders(net):
    mid = list(range(1, net.bits - 2))
    return mid, mid[::-1]


class Task:
    def __init__(self, steps):
        self.steps, self.flight, self.result = steps, None, None
        self.advance(None)

    def advance(self, arrived):
        try:
            self.flight = list(self.steps.send(arrived))
        except StopIteration as stop:
            self.flight, self.result = [], stop.value

    def get(self):
        while self.flight:
            self.advance(self.flight)
        return self.result


def window(values, tasks):
    done = tie(*values, *[f for task in tasks for f in task.flight])
    at = len(values)
    for task in tasks:
        size = len(task.flight)
        if size:
            task.advance(list(done[at : at + size]))
        at += size
    return done[: len(values)]


def gather_steps(net, have, high):
    have, masks = have[None], [0]
    for b in high:
        (other,) = yield [net.hop(have, b)]
        have = jnp.concatenate([have, other], 0)
        masks = masks + [m ^ (1 << b) for m in masks]
    cut = have.shape[2] // 2
    halves = [have[:, :, :cut], have[:, :, cut:]]
    orders = link_orders(net)
    lists = [masks, masks]
    for step in range(len(orders[0]) - 1):
        others = yield [net.hop(h, o[step]) for h, o in zip(halves, orders)]
        halves = [jnp.concatenate([h, o], 0) for h, o in zip(halves, others)]
        lists = [l + [m ^ (1 << o[step]) for m in l] for l, o in zip(lists, orders)]
    last = [o[-1] for o in orders]
    late = yield [net.hop(h, b) for h, b in zip(halves, last)]
    core = yield [net.hop(h, 0) for pair in zip(halves, late) for h in pair]
    parts = []
    for n in (0, 1):
        late_list = [m ^ (1 << last[n]) for m in lists[n]]
        parts.append((halves[n], lists[n], n))
        parts.append((core[2 * n], [m ^ 1 for m in lists[n]], n))
        parts.append((late[n], late_list, n))
        parts.append((core[2 * n + 1], [m ^ 1 for m in late_list], n))
    return parts


def stack_columns(width, *shares):
    pieces = []
    for share in shares:
        for at in range(0, share.shape[1], width):
            pieces.append(share[:, at : at + width])
    return jnp.concatenate(pieces, 0)


def flat_rows(out):
    return out.reshape(-1, out.shape[2])


def pack_small(table, small):
    small = jnp.pad(small, ((0, 0), (0, 128 - small.shape[1])))
    return jnp.concatenate([v[i : i + 8] for v in (table, small) for i in (0, 8, 16)], 1)


def gather_first(net, w_qkv, table, small, packed):
    rows, width = w_qkv.shape[0], w_qkv.shape[1] // 3
    half = width // 2
    if packed is None:
        cube = lax.all_gather(w_qkv, AXES, axis=0, tiled=True).reshape(width, 3, 2, half)
        return (
            cube[:, :, 0].reshape(width, -1),
            cube[:, :, 1].reshape(width, -1),
            lax.all_gather(table, AXES, axis=0, tiled=True),
            lax.all_gather(small, AXES, axis=0),
        )
    parts = yield from gather_steps(net, packed, (net.bits - 1, net.bits - 2))
    left, right, table, small = place_blocks(
        net,
        parts,
        lambda h: [(i * rows, rows, 0, half, h, 0, i * half) for i in range(3)]
        + [(3 * rows, 8, i * 128, 128, 2 + h, i * 8, 0) for i in range(3)],
        [(net.count, rows, 3 * half)] * 2 + [(net.count, 24, 128)] * 2,
    )
    return flat_rows(left), flat_rows(right), flat_rows(table), small[:, :, :rows]


def gather_rest(net, w_out, w_up, w_down, packed):
    rows, width = w_out.shape
    if packed is None:
        return [lax.all_gather(w, AXES, axis=0, tiled=True) for w in (w_out, w_up, w_down)]
    parts = yield from gather_steps(net, packed, (net.bits - 1, net.bits - 2))
    columns = w_up.shape[1] // width
    half = width // 2
    out, up, down = place_blocks(
        net,
        parts,
        lambda h: [(0, rows, 0, half, 0, 0, h * half)]
        + [((i + 1) * rows, rows, 0, half, 1, 0, i * width + h * half) for i in range(columns)]
        + [((columns + 1) * rows, w_down.shape[0], 0, half, 2, 0, h * half)],
        [(net.count,) + w.shape for w in (w_out, w_up, w_down)],
    )
    return flat_rows(out), flat_rows(up), flat_rows(down)


def settle(keep, other, dtype=BF16):
    return (keep.astype(F32) + other.astype(F32)).astype(dtype)


def reduce_steps(net, grads, order):
    axis = lambda b: net.bits - 1 - b
    cubes = [g.reshape((2,) * net.bits + (g.shape[0] // net.count, g.shape[1])) for g in grads]
    widths = [g.shape[1] for g in grads]
    join = lambda values: jnp.concatenate(values, -1) if len(values) > 1 else values[0]
    arrived = yield [net.hop(net.pick(c, 1 - net.bit(0), axis(0)), 0) for c in cubes]
    pairs = [(net.pick(c, net.bit(0), axis(0)), f) for c, f in zip(cubes, arrived)]
    for n, b in enumerate(order):
        side = lambda which: join(
            [settle(net.pick(k, which, axis(b)), net.pick(f, which, axis(b))) for k, f in pairs]
        )
        sent, kept = side(1 - net.bit(b)), side(net.bit(b))
        (other,) = yield [net.hop(sent, b)]
        pairs = [(kept, other)]
    whole = settle(*pairs[0], F32)
    whole = whole.reshape(whole.shape[-2:])
    out, at = [], 0
    for w in widths:
        out.append(whole[:, at : at + w])
        at += w
    return out


def total_steps(net, value):
    for b in [0] + list(range(1, net.bits)):
        (other,) = yield [net.hop(value, b)]
        value = value + other
    return value


def ordered(net, value, other, b, axis):
    return jnp.where(
        net.bit(b) == 0,
        jnp.concatenate([value, other], axis),
        jnp.concatenate([other, value], axis),
    )


def trade_pair(net, value, b, axis):
    return net.hop(net.pick(value, 1 - net.bit(b), axis), b), net.pick(value, net.bit(b), axis)


def dot_nt(a, b):
    return dot(a, b, ((1,), (1,)))


def dot_tn(a, b):
    return dot(a, b, ((0,), (0,)))


def pick_lanes(mask, values):
    return jnp.where(mask, values, jnp.zeros_like(values))


def head_masks(rows):
    lane = lax.broadcasted_iota(jnp.int32, (rows, 2 * HDIM), 1)
    return lane < HDIM, lane >= HDIM


def chance_of(keys, queries):
    scores = dot_nt(keys, queries) * SCALE
    raised = jnp.exp(scores - jnp.max(scores, axis=0, keepdims=True))
    return raised * (1.0 / jnp.sum(raised, axis=0, keepdims=True))


def attend_forward_body(heads, qkv_ref, out_ref):
    width = heads * HDIM
    for at in range(0, width, 2 * HDIM):
        queries, keys, values = [qkv_ref[:, n * width + at : n * width + at + 128] for n in range(3)]
        total = 0.0
        for mask in head_masks(SEG):
            chance = chance_of(pick_lanes(mask, keys), queries).astype(BF16)
            total = total + dot_tn(pick_lanes(mask, values), chance)
        out_ref[:, at : at + 128] = total.T.astype(BF16)


def attend_backward_body(heads, qkv_ref, grad_ref, out_ref, sums_ref):
    width = heads * HDIM
    for at in range(0, width, 2 * HDIM):
        queries, keys, values = [qkv_ref[:, n * width + at : n * width + at + 128] for n in range(3)]
        grad = grad_ref[:, at : at + 128]
        totals = [0.0, 0.0, 0.0]
        for mask in head_masks(SEG):
            own_keys = pick_lanes(mask, keys)
            chance = chance_of(own_keys, queries)
            slope = dot_nt(pick_lanes(mask, values), grad)
            slope = slope - jnp.sum(slope * chance, axis=0, keepdims=True)
            tilt = (chance * slope).astype(BF16)
            totals[0] = totals[0] + dot_tn(tilt, own_keys)
            totals[1] = totals[1] + dot(tilt, pick_lanes(mask, queries))
            totals[2] = totals[2] + dot(chance.astype(BF16), pick_lanes(mask, grad))
        for n, (total, scale) in enumerate(zip(totals, (SCALE, SCALE, 1.0))):
            low = (total * scale).astype(BF16)
            out_ref[:, n * width + at : n * width + at + 128] = low
            sums_ref[0, :, n * width + at : n * width + at + 128] = jnp.sum(
                low.astype(F32), axis=0, keepdims=True
            )


def segment_attend(qkv, half, context=None):
    rows, width = qkv.shape[0], qkv.shape[1] // 3

    def body(*refs):
        attend_forward_body(width // HDIM, refs[0], refs[-1])

    return pl.pallas_call(
        body,
        out_shape=jax.ShapeDtypeStruct((rows, 2 * width), BF16),
        grid=(rows // SEG,),
        in_specs=[pl.BlockSpec((SEG, 3 * width), lambda i: (i, 0))]
        + [pl.BlockSpec(memory_space=pl.ANY)] * half,
        out_specs=pl.BlockSpec((SEG, width), lambda i: (i, half)),
        input_output_aliases={1: 0} if half else {},
        name="segment_attend",
    )(*([qkv, context] if half else [qkv]))


def segment_attend_back(qkv, grad, half):
    rows, width = qkv.shape[0], qkv.shape[1] // 3
    return pl.pallas_call(
        partial(attend_backward_body, width // HDIM),
        out_shape=(
            jax.ShapeDtypeStruct((rows, 3 * width), BF16),
            jax.ShapeDtypeStruct((rows // SEG, 1, 3 * width), F32),
        ),
        grid=(rows // SEG,),
        in_specs=[
            pl.BlockSpec((SEG, 3 * width), lambda i: (i, 0)),
            pl.BlockSpec((SEG, width), lambda i: (i, half)),
        ],
        out_specs=(
            pl.BlockSpec((SEG, 3 * width), lambda i: (i, 0)),
            pl.BlockSpec((1, 1, 3 * width), lambda i: (i, 0, 0)),
        ),
        name="segment_attend_back",
    )(qkv, grad)


def column_sums(values):
    return jnp.sum(values.astype(F32), axis=0)


def cross_weight_steps(net, w_qkv, w_out, w_up, w_down):
    rows, width = w_out.shape
    hi, lo = net.bits - 1, net.bits - 2
    part = width // TP
    planes = net.count // TP
    cube = w_qkv.reshape(rows, 3, TP, part)
    ups = w_up.reshape(rows, TP, -1)
    hidden = ups.shape[2]
    assert hidden == width
    kvq = jnp.concatenate([cube[:, 1], cube[:, 2], cube[:, 0], jnp.zeros_like(cube[:, 0])], 2)
    cols = jnp.stack([ups, kvq]).transpose(2, 0, 1, 3).reshape(2, 2, 2 * rows, width)
    for b, axis in ((hi, 0), (lo, 1)):
        flight, keep = trade_pair(net, cols, b, axis)
        (other,) = yield [flight]
        cols = ordered(net, keep, other, b, axis)
    have = jnp.concatenate([cols.reshape(-1, width), w_out, w_down], 0)
    if rows % 8:
        value = have[None]
        for b in range(net.bits - 2):
            (other,) = yield [net.hop(value, b)]
            value = ordered(net, value, other, b, 0)
        cols = value[:, : 8 * rows].reshape(planes, TP, 2, rows, width).transpose(1, 0, 3, 2, 4)
        return (
            cols.reshape(width, 2 * width),
            value[:, 8 * rows : 9 * rows].reshape(part, width),
            value[:, 9 * rows :].reshape(hidden, width),
        )
    parts = yield from gather_steps(net, have, ())
    parts = [(array, [m & (planes - 1) for m in masks], h) for array, masks, h in parts]
    half = width // 2
    plane = Net.__new__(Net)
    plane.me = net.me & (planes - 1)
    outs = place_blocks(
        plane,
        parts,
        lambda h: [
            ((2 * t + k) * rows, rows, 0, half, t, 0, k * width + h * half)
            for t in range(TP)
            for k in (0, 1)
        ]
        + [
            (8 * rows, rows, 0, half, TP, 0, h * half),
            (9 * rows, 4 * rows, 0, half, TP + 1, 0, h * half),
        ],
        [(planes, rows, 2 * width)] * TP + [(planes, rows, width), (planes, 4 * rows, width)],
    )
    return (
        jnp.concatenate([flat_rows(o) for o in outs[:TP]], 0),
        flat_rows(outs[TP]),
        flat_rows(outs[TP + 1]),
    )


def cross_grad_steps(net, ups, rest, grad_out, grad_down, order):
    hi, lo = net.bits - 1, net.bits - 2
    plane = net.bits - 2
    planes = net.count // TP
    width = ups.shape[0]
    rows = width // net.count
    part = width // TP
    pair = jnp.stack([ups.reshape(TP, planes, rows, width), rest.reshape(TP, planes, rows, width)])
    whole = jnp.concatenate(
        [
            pair.transpose(2, 1, 0, 3, 4).reshape(planes, 8 * rows, width),
            grad_out.reshape(planes, rows, width),
            grad_down.reshape(planes, 4 * rows, width),
        ],
        1,
    ).reshape((2,) * plane + (13 * rows, width))
    axis = lambda b: plane - 1 - b
    (other,) = yield [net.hop(net.pick(whole, 1 - net.bit(0), axis(0)), 0)]
    kept = net.pick(whole, net.bit(0), axis(0))
    for b in order:
        side = lambda which: settle(net.pick(kept, which, axis(b)), net.pick(other, which, axis(b)))
        sent, kept = side(1 - net.bit(b)), side(net.bit(b))
        (other,) = yield [net.hop(sent, b)]
    whole = settle(kept, other).reshape(13 * rows, width)
    cols = whole[: 8 * rows].reshape(2, 2, 2 * rows, width)
    for b, at in ((hi, 0), (lo, 1)):
        flight, keep = trade_pair(net, cols, b, at)
        (back,) = yield [flight]
        cols = ordered(net, keep, back, b, at)
    whole, cols = yield [whole, cols]
    cols = cols.reshape(TP, 2, rows, width).transpose(1, 2, 0, 3).astype(F32)
    deep = whole[8 * rows :].astype(F32)
    pieces = [cols[1, :, :, n * part : (n + 1) * part].reshape(rows, width) for n in (2, 0, 1)]
    return (
        jnp.concatenate(pieces, 1),
        deep[:rows],
        cols[0].reshape(rows, -1),
        deep[rows:],
        cols[1, :, 0, 3 * part :],
    )


def lanes_between(values, first, last):
    lane = lax.broadcasted_iota(jnp.int32, values.shape, values.ndim - 1)
    return jnp.where((lane >= first) & (lane < last), values, jnp.zeros_like(values))


def stack_heads(values, heads, first):
    return jnp.concatenate(
        [lanes_between(values, first + h * HDIM, first + (h + 1) * HDIM) for h in range(heads)], 0
    )


def merge_heads(values, heads, first):
    rows = values.shape[0] // heads
    return sum(
        lanes_between(values[h * rows : (h + 1) * rows], first + h * HDIM, first + (h + 1) * HDIM)
        for h in range(heads)
    )


def fused(body, outs, *args, name):
    return pl.pallas_call(
        body, out_shape=[jax.ShapeDtypeStruct(shape, dtype) for shape, dtype in outs], name=name
    )(*args)


def cross_encoder(net, cross_in, grad_own, weights, params, allowed, onehot):
    cols, w_out, w_down = weights
    own, width = cross_in.shape
    part, hidden = w_out.shape[0], w_down.shape[0]
    plane = net.bits - 2
    hi, lo = net.bits - 1, net.bits - 2
    member = net.me >> lo
    up = list(range(1, plane))
    heads = part // HDIM
    biases, gains, up_bias = params
    row = lambda n: biases[n : n + 1]
    slab = lambda vector, size: lax.dynamic_slice_in_dim(vector, member * size, size, 1)
    bias_kv = jnp.concatenate([jnp.zeros((1, part), F32), slab(row(1), part)], 1)
    bias_q = slab(row(0), part)
    bias_up = slab(up_bias.reshape(1, -1), hidden)
    both = jnp.concatenate([cross_in, grad_own], 0)[None]
    both = net.grow(net.grow(both, lo, 0), hi, 0)
    count = TP * own
    full, wide, flat = (count, width), (count, 2 * part), (count, part)

    def project(x_ref, cols_ref, bias_kv_ref, bias_q_ref, hidden_ref, grad_ref, low_ref, kv_ref, q_ref):
        values = jnp.concatenate([x_ref[t, :own, :] for t in range(TP)], 0)
        hidden_ref[...] = values
        grad_ref[...] = jnp.concatenate([x_ref[t, own:, :] for t in range(TP)], 0)
        low = values.astype(BF16)
        low_ref[...] = low
        kv = dot(low, cols_ref[:, hidden : hidden + 2 * part]) + bias_kv_ref[...]
        kv_ref[...] = kv.astype(BF16)
        q_ref[...] = (dot(low, cols_ref[:, hidden + 2 * part : hidden + 3 * part]) + bias_q_ref[...]).astype(BF16)

    hidden_all, grad_all, hidden_low, kv, queries = fused(
        project,
        [(full, F32), (full, F32), (full, BF16), (wide, BF16), (flat, BF16)],
        both, cols, bias_kv, bias_q,
        name="cross_project",
    )
    have = kv
    for b in up:
        have = jnp.concatenate([have, net.hop(have, b)], 0)
    late = net.hop(have, 0)
    seen = 2 * have.shape[0]

    def attend(q_ref, have_ref, late_ref, allowed_ref, out_w_ref, chance_ref, context_ref, part_ref):
        kv = jnp.concatenate([have_ref[...], late_ref[...]], 0)
        q = q_ref[...]
        spread = stack_heads(jnp.concatenate([q, jnp.zeros_like(q)], 1), heads, 0)
        scores = dot_nt(spread, kv) * SCALE
        scores = jnp.where(jnp.concatenate([allowed_ref[...]] * heads, 0) > 0.5, scores, -1e30)
        raised = jnp.exp(scores - jnp.max(scores, axis=1, keepdims=True))
        chance = raised * (1.0 / jnp.sum(raised, axis=1, keepdims=True))
        chance_ref[...] = chance
        context = merge_heads(dot(chance.astype(BF16), kv), heads, part)[:, part:].astype(BF16)
        context_ref[...] = context
        part_ref[...] = dot(context, out_w_ref[...]).astype(BF16)

    chance, context, partial_sum = fused(
        attend,
        [((heads * count, seen), F32), (flat, BF16), (full, BF16)],
        queries, have, late, allowed, w_out,
        name="cross_attend",
    )
    half_sum = settle(partial_sum, net.hop(partial_sum, lo))
    other_sum = net.hop(half_sum, hi)

    def feed(
        x_ref, a_ref, b_ref, bias_ref, gain_ref, cols_ref, bias_up_ref, down_ref,
        normed_ref, normal_ref, inverse_ref, low_ref, active_ref, slope_ref, part_ref,
    ):
        mixed = x_ref[...] + (a_ref[...].astype(F32) + b_ref[...].astype(F32)) + bias_ref[2:3, :]
        normal, inverse = normalize(mixed)
        normed = normal * gain_ref[0:1, :] + bias_ref[3:4, :]
        low = normed.astype(BF16)
        active, slope = gelu_pair(dot(low, cols_ref[:, :hidden]) + bias_up_ref[...])
        active = active.astype(BF16)
        normed_ref[...] = normed
        normal_ref[...] = normal
        inverse_ref[...] = inverse
        low_ref[...] = low
        active_ref[...] = active
        slope_ref[...] = slope
        part_ref[...] = dot(active, down_ref[...]).astype(BF16)

    normed, normal1, inverse1, normed_low, active, slope, partial_sum = fused(
        feed,
        [
            (full, F32), (full, F32), ((count, 1), F32), (full, BF16),
            ((count, hidden), BF16), ((count, hidden), F32), (full, BF16),
        ],
        hidden_all, half_sum, other_sum, biases, gains, cols, bias_up, w_down,
        name="cross_feed",
    )
    half_sum = settle(partial_sum, net.hop(partial_sum, lo))
    other_sum = net.hop(half_sum, hi)

    def turn(
        normed_ref, a_ref, b_ref, bias_ref, gain_ref, grad_ref, down_ref, slope_ref, cols_ref,
        result_ref, normal_ref, second_ref, ffn_ref, before_ref, part_ref,
    ):
        second = normed_ref[...] + (a_ref[...].astype(F32) + b_ref[...].astype(F32)) + bias_ref[4:5, :]
        normal, inverse = normalize(second)
        gain = gain_ref[1:2, :]
        result_ref[...] = normal * gain + bias_ref[5:6, :]
        normal_ref[...] = normal
        grad_second = normalize_back(grad_ref[...] * gain, normal, inverse)
        second_ref[...] = grad_second
        ffn = grad_second.astype(BF16)
        ffn_ref[...] = ffn
        before = (dot_nt(ffn, down_ref[...]) * slope_ref[...]).astype(BF16)
        before_ref[...] = before
        part_ref[...] = dot_nt(before, cols_ref[:, :hidden]).astype(BF16)

    result, normal2, grad_second, grad_ffn, grad_before, partial_sum = fused(
        turn,
        [
            (full, F32), (full, F32), (full, F32), (full, BF16),
            ((count, hidden), BF16), (full, BF16),
        ],
        normed, half_sum, other_sum, biases, gains, grad_all, w_down, slope, cols,
        name="cross_turn",
    )
    half_sum = settle(partial_sum, net.hop(partial_sum, lo))
    other_sum = net.hop(half_sum, hi)

    def attend_back(
        second_ref, a_ref, b_ref, normal_ref, inverse_ref, gain_ref, out_w_ref, chance_ref,
        q_ref, have_ref, late_ref,
        normed_ref, mixed_ref, attn_ref, grad_q_ref, keep_ref, send_ref,
    ):
        grad_normed = second_ref[...] + (a_ref[...].astype(F32) + b_ref[...].astype(F32))
        normed_ref[...] = grad_normed
        grad_mixed = normalize_back(
            grad_normed * gain_ref[0:1, :], normal_ref[...], inverse_ref[...]
        )
        mixed_ref[...] = grad_mixed
        attn = grad_mixed.astype(BF16)
        attn_ref[...] = attn
        grad = dot_nt(attn, out_w_ref[...]).astype(BF16)
        grads = stack_heads(jnp.concatenate([jnp.zeros_like(grad), grad], 1), heads, part)
        q = q_ref[...]
        spread = stack_heads(jnp.concatenate([q, jnp.zeros_like(q)], 1), heads, 0)
        kv = jnp.concatenate([have_ref[...], late_ref[...]], 0)
        chance = chance_ref[...]
        slopes = dot_nt(grads, kv)
        slopes = slopes - jnp.sum(slopes * chance, axis=1, keepdims=True)
        tilt = (chance * slopes).astype(BF16)
        grad_q = merge_heads(dot(tilt, kv), heads, 0)[:, :part] * SCALE
        grad_q_ref[...] = grad_q.astype(BF16)
        grad_kv = dot_tn(tilt, spread) * SCALE + dot_tn(chance.astype(BF16), grads)
        keep_ref[...] = grad_kv[: seen // 2]
        send_ref[...] = grad_kv[seen // 2 :]

    grad_normed, grad_mixed, grad_attn, grad_q, keep, send = fused(
        attend_back,
        [
            (full, F32), (full, F32), (full, BF16), (flat, BF16),
            ((seen // 2, 2 * part), F32), ((seen // 2, 2 * part), F32),
        ],
        grad_second, half_sum, other_sum, normal1, inverse1, gains, w_out, chance,
        queries, have, late,
        name="cross_attend_back",
    )
    other = net.hop(send, 0)
    for b in up[::-1]:
        size = keep.shape[0] // 2
        total = keep + other
        keep, other = total[:size], net.hop(total[size:], b)

    def project_back(grad_q_ref, keep_ref, other_ref, cols_ref, grad_ref, back_ref):
        grad_kv = (keep_ref[...] + other_ref[...]).astype(BF16)
        grad_q = grad_q_ref[...]
        grad_ref[...] = jnp.concatenate([grad_kv, grad_q], 1)
        back = dot_nt(grad_kv, cols_ref[:, hidden : hidden + 2 * part]) + dot_nt(
            grad_q, cols_ref[:, hidden + 2 * part : hidden + 3 * part]
        )
        back_ref[...] = back.astype(BF16)

    grad_kvq, back = fused(
        project_back,
        [((count, 3 * part), BF16), (full, BF16)],
        grad_q, keep, other, cols,
        name="cross_project_back",
    )
    half_sum = settle(back, net.hop(back, lo))
    grad_in = grad_mixed + settle(half_sum, net.hop(half_sum, hi), F32)
    mine = lambda values: lax.dynamic_slice_in_dim(values, member * own, own, 0)

    def weight_grads(
        low_ref, grad_ref, normed_ref, before_ref, context_ref, attn_ref, active_ref, ffn_ref,
        in_ref, onehot_ref, up_ref, rest_ref, out_ref, down_ref,
    ):
        up_ref[...] = dot_tn(normed_ref[...], before_ref[...]).astype(BF16)
        table = dot_tn(in_ref[...].astype(BF16), onehot_ref[...])
        rest_ref[...] = jnp.concatenate(
            [
                dot_tn(low_ref[...], grad_ref[...]),
                table,
                jnp.zeros((width, part - table.shape[1]), F32),
            ],
            1,
        ).astype(BF16)
        out_ref[...] = dot_tn(context_ref[...], attn_ref[...]).astype(BF16)
        down_ref[...] = dot_tn(active_ref[...], ffn_ref[...]).astype(BF16)

    grads = fused(
        weight_grads,
        [
            ((width, hidden), BF16),
            ((width, width), BF16),
            (w_out.shape, BF16),
            (w_down.shape, BF16),
        ],
        hidden_low, grad_kvq, normed_low, grad_before, context, grad_attn, active, grad_ffn,
        grad_in, onehot,
        name="cross_weight_grads",
    )

    def small_sums(
        member_ref, grad_ref, attn_ref, normed_ref, ffn_ref, result_grad_ref, normal1_ref,
        normal2_ref, before_ref, out_ref,
    ):
        member = member_ref[0]
        rows = lax.broadcasted_iota(jnp.int32, full, 0) // own == member
        ours = lambda values: jnp.sum(jnp.where(rows, values, 0.0), axis=0, keepdims=True)
        every = lambda values: jnp.sum(values.astype(F32), axis=0, keepdims=True)

        def spread(values):
            return jnp.concatenate([jnp.where(member == j, values, 0.0) for j in range(TP)], 1)

        sums = every(grad_ref[...])
        grad_normed, grad_result = normed_ref[...], result_grad_ref[...]
        out_ref[...] = jnp.zeros_like(out_ref)
        out_ref[0:1, :] = spread(sums[:, 2 * part :])
        out_ref[1:2, :] = spread(sums[:, part : 2 * part])
        out_ref[2:3, :] = ours(attn_ref[...].astype(F32))
        out_ref[3:4, :] = ours(grad_normed)
        out_ref[4:5, :] = ours(ffn_ref[...].astype(F32))
        out_ref[5:6, :] = ours(grad_result)
        out_ref[6:7, :] = ours(grad_normed * normal1_ref[...])
        out_ref[7:8, :] = ours(grad_result * normal2_ref[...])
        up_sums = every(before_ref[...])
        per = hidden // width
        for j in range(TP):
            for k in range(per):
                at = 8 + j * per + k
                out_ref[at : at + 1, :] = jnp.where(
                    member == j, up_sums[:, k * width : (k + 1) * width], 0.0
                )

    lines = 8 + hidden * TP // width
    small = pl.pallas_call(
        small_sums,
        out_shape=jax.ShapeDtypeStruct((lines, width), F32),
        in_specs=[pl.BlockSpec(memory_space=pltpu.SMEM)]
        + [pl.BlockSpec(memory_space=pltpu.VMEM)] * 8,
        name="cross_small_sums",
    )(member.reshape(1), grad_kvq, grad_attn, grad_normed, grad_ffn, grad_all, normal1, normal2,
      grad_before)
    return mine(result), mine(grad_in), grads, small


def places_of(ids, slots, seq_ids, table_rows):
    all_slots = jnp.arange(seq_ids.shape[0], dtype=jnp.int32)
    earlier = (seq_ids[None, :] == ids[:, None]) & (all_slots[None, :] < slots[:, None])
    places = jnp.sum(earlier.astype(jnp.int32), axis=1)
    rows = jnp.arange(table_rows, dtype=jnp.int32)
    return (places[:, None] == rows[None, :]).astype(BF16)


def shards(
    count, tokens, seq_ids, w_qkv, w_out, w_up, w_down, biases, up_bias, norm_gains, pos_table, cotangent
):
    net = Net(count)
    rows_here, width = tokens.shape
    segs_here = rows_here // SEG
    share, hidden = biases.shape[2], up_bias.shape[1]
    half = width // 2
    lo, hi = net.bits - 2, net.bits - 1
    planes = count // TP

    order = list(range(1, net.bits - 2)) + [0]
    masks = [0]
    for b in order:
        masks = masks + [m | 1 << b for m in masks]
    slots = jnp.arange(seq_ids.shape[0], dtype=jnp.int32).reshape(TP, planes, segs_here)
    key_slots = jnp.take(slots, (net.me & (planes - 1)) ^ jnp.array(masks, jnp.int32), axis=1)
    row_slots = key_slots[:, 0].reshape(-1)
    key_ids = seq_ids[key_slots.transpose(1, 0, 2).reshape(-1)]
    row_ids = seq_ids[row_slots]
    allowed = (row_ids[:, None] == key_ids[None, :]).astype(F32)
    onehot = places_of(row_ids, row_slots, seq_ids, pos_table.shape[0])

    grad_rows = cotangent.reshape(segs_here, SEG, width)
    table = pos_table.T
    small = jnp.concatenate(
        [v.reshape(-1, share) for v in (biases, norm_gains, up_bias)], 0
    )
    if share % 8:
        first_packed = packed = None
    else:
        first_packed = jnp.concatenate(
            [stack_columns(width, w_qkv[0]), pack_small(table, small)], 0
        )
        packed = jnp.concatenate([stack_columns(width, w_out[0], w_up[0]), w_down[0]], 0)
    cross_shares = (w_qkv[1], w_out[1], w_up[1], w_down[1])

    get_qkv = Task(gather_first(net, w_qkv[0], table, small, first_packed))
    packed, *cross_shares = window([packed, *cross_shares], [get_qkv]) if packed is not None else (
        packed, *cross_shares
    )
    get_rest = Task(gather_rest(net, w_out[0], w_up[0], w_down[0], packed))
    cross_shares = window([*cross_shares], [get_qkv])
    window([], [get_rest])
    cross_shares = window([*cross_shares], [get_qkv])
    get_cross = Task(cross_weight_steps(net, *cross_shares))
    (tokens,) = window([tokens], [get_qkv])
    *weights_qkv, table, small = get_qkv.get()
    small = small.astype(F32)
    narrow = small[:, :16].transpose(1, 0, 2).reshape(16, width)
    long = small[:, 16:].reshape(count, 2, -1).transpose(1, 0, 2).reshape(2, 1, -1)
    biases0, gains0, up_bias0 = narrow[:6], narrow[12:14], long[0, 0]
    params1 = narrow[6:12], narrow[14:], long[1]

    qkv, context = [], None
    for n, weight in enumerate(weights_qkv):
        shift = jnp.concatenate(
            [
                biases0[0, n * half : (n + 1) * half],
                jnp.zeros((half,), F32),
                biases0[1, n * half : (n + 1) * half],
            ]
        )
        qkv.append((dot(tokens, weight) + shift).astype(BF16))
        context = segment_attend(qkv[n], n, context)
        context, tokens = window([context, tokens], [get_rest, get_cross])
    (context,) = window([context], [get_rest, get_cross])
    w_out0, w_up0, w_down0 = get_rest.get()

    mixed = tokens.astype(F32) + dot(context, w_out0) + biases0[2]
    normal1, inverse1 = normalize(mixed)
    normed = normal1 * gains0[0] + biases0[3]
    normed_low = normed.astype(BF16)
    active, slope = gelu_pair(dot(normed_low, w_up0) + up_bias0)
    active, slope = active.astype(BF16), slope.astype(BF16)
    active, slope = window([active, slope], [get_cross])
    second = normed + dot(active, w_down0) + biases0[4]
    normal2, inverse2 = normalize(second)
    blocked = (normal2 * gains0[1] + biases0[5]).reshape(segs_here, SEG, width)

    firsts = blocked[:, 0, :]
    own_onehot = lax.dynamic_slice_in_dim(onehot, (net.me >> lo) * segs_here, segs_here, 0)
    cross_in = firsts + dot_nt(own_onehot, table)
    result1, grad_cross, grads1, small1 = cross_encoder(
        net,
        cross_in,
        grad_rows[:, 0, :].astype(F32),
        get_cross.get(),
        params1,
        allowed,
        onehot,
    )
    is_first = lax.broadcasted_iota(jnp.int32, (1, SEG, 1), 1) == 0
    layer_out = jnp.where(is_first, result1[:, None, :], blocked)
    layer_out = layer_out.reshape(rows_here, width).astype(BF16)

    ways, back_ways = link_orders(net)
    grad = jnp.where(is_first, grad_cross[:, None, :], grad_rows.astype(F32))
    grad = grad.reshape(rows_here, width)
    red_cross = Task(cross_grad_steps(net, *grads1, ways))
    grad_second = normalize_back(grad * gains0[1], normal2, inverse2)
    grad_ffn = grad_second.astype(BF16)
    grad_down = dot_tn(active, grad_ffn).astype(BF16)
    grad_down, grad_ffn = window([grad_down, grad_ffn], [red_cross])
    red_down = Task(reduce_steps(net, [grad_down], back_ways + [lo, hi]))
    grad_before = (dot_nt(grad_ffn, w_down0) * slope.astype(F32)).astype(BF16)
    (grad_before,) = window([grad_before], [red_down])
    grad_up = dot_tn(normed_low, grad_before).astype(BF16)
    grad_up, grad_before = window([grad_up, grad_before], [])
    red_up = Task(reduce_steps(net, [grad_up], ways + [lo, hi]))
    grad_normed = grad_second + dot_nt(grad_before, w_up0)
    (grad_normed,) = window([grad_normed], [red_cross, red_up])
    grad_mixed = normalize_back(grad_normed * gains0[0], normal1, inverse1)
    grad_attn = grad_mixed.astype(BF16)
    grad_context = dot_nt(grad_attn, w_out0).astype(BF16)
    grad_out = dot_tn(context, grad_attn).astype(BF16)
    grad_context, grad_out = window([grad_context, grad_out], [])
    back_left, sums_left = segment_attend_back(qkv[0], grad_context, 0)
    back_left, grad_context = window([back_left, grad_context], [red_down, red_cross])
    grad_left = dot_tn(tokens, back_left).astype(BF16)
    grad_left, grad_context, grad_out = window([grad_left, grad_context, grad_out], [])
    red_left = Task(reduce_steps(net, [grad_left, grad_out], ways + [lo, hi]))
    back_right, sums_right = segment_attend_back(qkv[1], grad_context, 1)
    (back_right,) = window([back_right], [red_up, red_left, red_cross])
    grad_right = dot_tn(tokens, back_right).astype(BF16)
    grad_right, back_right = window([grad_right, back_right], [])
    red_right = Task(reduce_steps(net, [grad_right], back_ways + [lo, hi]))
    grad_tokens = grad_mixed + dot_nt(back_left, weights_qkv[0]) + dot_nt(back_right, weights_qkv[1])
    (grad_tokens, sums_left, sums_right) = window(
        [grad_tokens.astype(BF16), sums_left, sums_right], [red_down, red_right, red_cross]
    )

    sums = [jnp.sum(v, axis=(0, 1)).reshape(3, half) for v in (sums_left, sums_right)]
    small0 = jnp.concatenate(
        [
            jnp.stack(
                [
                    jnp.concatenate([v[0] for v in sums]),
                    jnp.concatenate([v[2] for v in sums]),
                    column_sums(grad_attn),
                    column_sums(grad_normed),
                    column_sums(grad_ffn),
                    column_sums(grad),
                    column_sums(grad_normed * normal1),
                    column_sums(grad * normal2),
                ]
            ),
            column_sums(grad_before).reshape(-1, width),
        ]
    )
    red_small = Task(total_steps(net, jnp.stack([small0, small1])))
    window([], [red_up, red_left, red_small])
    window([], [red_down, red_right, red_small])
    window([], [red_up, red_left, red_small])
    window([], [red_down, red_right, red_small])
    window([], [red_up, red_left, red_small])
    window([], [red_right])
    for _ in range(net.bits):
        window([], [red_down, red_up, red_left, red_right, red_small])

    small = red_small.get()
    narrow = lax.dynamic_slice_in_dim(small[:, :8], net.me * share, share, 2)
    long = lax.dynamic_slice_in_dim(small[:, 8:].reshape(2, -1), net.me * hidden, hidden, 1)
    (grad_down0,) = red_down.get()
    (grad_up0,) = red_up.get()
    grad_left0, grad_out0 = red_left.get()
    halves = [r.reshape(-1, 3, half) for r in (grad_left0, red_right.get()[0])]
    grad_qkv0 = jnp.stack(halves, 2).reshape(share, -1)
    shares1 = red_cross.get()
    return (
        layer_out,
        grad_tokens,
        jnp.stack([grad_qkv0, shares1[0]]),
        jnp.stack([grad_out0, shares1[1]]),
        jnp.stack([grad_up0, shares1[2]]),
        jnp.stack([grad_down0, shares1[3]]),
        narrow[:, :6],
        long,
        narrow[:, 6:],
        shares1[4][:, : pos_table.shape[0]].T,
    )


def solution(mesh):
    count = mesh.shape["ctx"] * mesh.shape["wa"]
    in_specs = (
        P(AXES, None),
        P(),
        P(None, AXES, None),
        P(None, AXES, None),
        P(None, AXES, None),
        P(None, AXES, None),
        P(None, None, AXES),
        P(None, AXES),
        P(None, None, AXES),
        P(None, AXES),
        P(AXES, None),
    )
    out_specs = (
        P(AXES, None),
        P(AXES, None),
        P(None, AXES, None),
        P(None, AXES, None),
        P(None, AXES, None),
        P(None, AXES, None),
        P(None, None, AXES),
        P(None, AXES),
        P(None, None, AXES),
        P(None, AXES),
    )
    return jax.shard_map(
        partial(shards, count), mesh=mesh, in_specs=in_specs, out_specs=out_specs, check_vma=False
    )
```

time: 1170 us -> 504 us (0.43)
  Pallas kernels: 518 us -> 84.3 us
  local copies, waits for them, and re-layouts: 134 us -> 60.9 us
  starting transfers between devices: 141 us -> 68.8 us
  matrix products: 116 us -> 80.3 us
  waiting for transfers between devices: 152 us -> 122 us
  other arithmetic: 91.3 us -> 78.9 us
    pallas_call x5 -> x13, Pallas kernels: 469 us -> 60.1 us  [the longest x7 21.9 us: fused(): pl.pallas_call(body, out_shape=[jax.ShapeDtypeStruct(shape, dtype) for sh...]
    ppermute x133 -> x77, starting transfers between devices: 141 us -> 68.8 us  [hop(): lax.ppermute(value, AXES, [(i, i ^ 1 << b) for i in range(self.count)])]
    ppermute x133 -> x77, waiting for transfers between devices: 152 us -> 122 us  [hop(): lax.ppermute(value, AXES, [(i, i ^ 1 << b) for i in range(self.count)])]
    dot_general x25 -> x16, matrix products: 106 us -> 80.3 us  [dot(): return lax.dot_general(a, b, (dims, ((), ())), preferred_element_type=F32)]
    pallas_call x1 -> x2, Pallas kernels: 48.4 us -> 24.2 us  [segment_attend_back(): pl.pallas_call(partial(attend_backward_body, width // HDIM), out_shape=(j...]
    concatenate x14 -> x6, local copies, waits for them, and re-layouts: 20.4 us -> 1.72 us  [the longest x1 0.92 us: shards(): jnp.concatenate([stack_columns(width, w_out[0], w_up[0]), w_down[0]], 0)]
    slice x54 -> x36, local copies, waits for them, and re-layouts: 27.1 us -> 11.5 us  [the longest x4 3.56 us: cross_grad_steps(): cols[1, :, :, n * part:(n + 1) * part].reshape(rows, width)]
    another operation x37 -> x18, local copies, waits for them, and re-layouts: 18.6 us -> 3.7 us  [the longest x8 2.96 us: shards(): jnp.stack([jnp.concatenate([v[0] for v in sums]), jnp.concatenate([v[2] f...]
  transfers between devices with their start and end apart: 133 -> 77, of which waited for: 52 -> 32; matrix products, arithmetic and copies ran while one was open for 25% -> 34% of each run, Pallas kernels for 45% -> 12%
where the time goes in v2:
time: 504 us; the launch traced here: 498 us
  waiting for transfers between devices  122 us (24%)
  Pallas kernels  84.3 us (17%)
  matrix products  80.3 us (16%)
  other arithmetic  78.9 us (16%)
  starting transfers between devices  68.8 us (14%)
  local copies, waits for them, and re-layouts  60.9 us (12%)
    ppermute x77, waiting for transfers between devices, hop(): lax.ppermute(value, AXES, [(i, i ^ 1 << b) for i in range(self.count)])  122 us
    dot_general x16, matrix products, dot(): return lax.dot_general(a, b, (dims, ((), ())), preferred_element_type=F32)  80.3 us
    ppermute x77, starting transfers between devices, hop(): lax.ppermute(value, AXES, [(i, i ^ 1 << b) for i in range(self.count)])  68.8 us
    convert_element_type x24, other arithmetic, settle(): return (keep.astype(F32) + other.astype(F32)).astype(dtype)  31.1 us
    pallas_call x2, Pallas kernels, segment_attend_back(): pl.pallas_call(partial(attend_backward_body, width // HDIM), out_shape=(j...  24.2 us
    pallas_call x7, Pallas kernels, fused(): pl.pallas_call(body, out_shape=[jax.ShapeDtypeStruct(shape, dtype) for sh...  21.9 us
    pallas_call x2, Pallas kernels, segment_attend(): pl.pallas_call(body, out_shape=jax.ShapeDtypeStruct((rows, 2 * width), BF...  19.3 us
    unnamed x194, local copies, waits for them, and re-layouts  18.2 us
  transfers between devices with their start and end apart: 77, of which 32 were waited for; matrix products, arithmetic and copies ran while one was open for 34% of the time, Pallas kernels for 12%

profile of v2, /device:TPU:0, one launch (start us, length us, event | category | flops | bytes accessed | tf_op | source)
XLA Modules:
  0.0 497.7 jit_solution(2661428203095833505)
XLA Ops:
  5.9 4.1 collective-permute-start
  17.4 5.8 %collective-permute-done.1 = bf16[2,80,768]{2,1,0:T(8,128)(2,1)S(1)} collective-permute-done((bf16[2,80,768]{2,1,0:T(8,128)(2,1)S(1)}, bf16[2,80,768]{2,1,0:T(8,128)(2,1)S(1)}, u32[]{:S(2)}, u32[]{:S(2)}) %collective-permute-start.1) | collective-permute-done | bytes 245792 | tf_op jit(solution)/shard_map/ppermute | solution.py:54
  26.5 3.1 collective-permute-start.10
  33.4 10.1 %collective-permute-done.10 = bf16[1,216,768]{2,1,0:T(8,128)(2,1)S(1)} collective-permute-done((bf16[1,216,768]{2,1,0:T(8,128)(2,1)S(1)}, bf16[1,216,768]{2,1,0:T(8,128)(2,1)S(1)}, u32[]{:S(2)}, u32[]{:S(2)}) %collective-permute-start.10) | collective-permute-done | bytes 331808 | tf_op jit(solution)/shard_map/ppermute | solution.py:54
  46.7 3.4 collective-permute-start.12
  50.1 4.6 place_blocks.3
  56.7 5.6 %add_convert_fusion.1.refs_0_.qkv_ref = bf16[1024,1152]{1,0:T(8,128)(2,1)} fusion(bf16[1024,768]{1,0:T(8,128)(2,1)} %param.12, bf16[768,1152]{1,0:T(8,128)(2,1)} %bitcast.229, f32[1152]{0:T(1024)S(1)} %get-tuple-element.410), kind=kOutput, calls=%fused_computation.16 | convolution fusion | flops 1814298624 | bytes 5706240 | tf_op jit(solution)/shard_map/dot_general | solution.py:20
  62.3 9.8 %segment_attend.2.refs_1_ = bf16[1024,768]{1,0:T(8,128)(2,1)} custom-call(bf16[1024,1152]{1,0:T(8,128)(2,1)} %add_convert_fusion.1.refs_0_.qkv_ref), custom_call_target="tpu_custom_call" | custom-call | tf_op jit(solution)/shard_map/segment_attend/pallas_call | solution.py:328
  75.9 3.6 add_convert_fusion.refs_0_.qkv_ref
  79.5 9.5 %segment_attend.3 = bf16[1024,768]{1,0:T(8,128)(2,1)} custom-call(bf16[1024,1152]{1,0:T(8,128)(2,1)} %add_convert_fusion.refs_0_.qkv_ref, bf16[1024,768]{1,0:T(8,128)(2,1)} %segment_attend.2.refs_1_), custom_call_target="tpu_custom_call", output_to_operand_aliasing={{}: (1, {})} | custom-call | tf_op jit(solution)/shard_map/segment_attend/pallas_call | solution.py:328
  91.8 2.8 pad_maximum_fusion.4.refs_4_
  102.8 28.1 %collective-permute-done.19 = bf16[1,312,384]{2,1,0:T(8,128)(2,1)S(1)} collective-permute-done((bf16[1,312,384]{2,1,0:T(8,128)(2,1)S(1)}, bf16[1,312,384]{2,1,0:T(8,128)(2,1)S(1)}, u32[]{:S(2)}, u32[]{:S(2)}) %collective-permute-start.19) | collective-permute-done | bytes 239648 | tf_op jit(solution)/shard_map/ppermute | solution.py:54
  141.9 8.2 %place_blocks.4 = (bf16[32,24,768]{2,1,0:T(8,128)(2,1)}, bf16[32,24,3072]{2,1,0:T(8,128)(2,1)}, bf16[32,96,768]{2,1,0:T(8,128)(2,1)}) custom-call(s32[1]{0:T(128)} %bitcast.12.me_ref, bf16[8,216,384]{2,1,0:T(8,128)(2,1)} %copy-done.10, bf16[8,216,384]{2,1,0:T(8,128)(2,1)} %collective-permute-done.20.refs_1_, ...), custom_call_target="tpu_custom_call" | custom-call | tf_op jit(solution)/shard_map/place_blocks/pallas_call | solution.py:91
  150.2 3.4 fusion.30
  154.3 14.2 %fusion.4 = (bf16[1024,3072]{1,0:T(8,128)(2,1)}, bf16[1024,3072]{1,0:T(8,128)(2,1)S(1)}) fusion(f32[3072]{0:T(1024)S(1)} %add.552, bf16[768,3072]{1,0:T(8,128)(2,1)S(1)} %bitcast.222, f32[1024,768]{1,0:T(8,128)S(1)} %get-tuple-element.343, f32[768]{0:T(1024)S(1)} %add.549, f32[768]{0:T(1024)S(1)} %mul.155, f32[1024]{0:T(1024)S(1)} %add_rsqrt_fusion.1, ...), kind=kOutput, calls=%fused_computation.8 | convolution fusion | flops 4873519104 | bytes 20473856 | tf_op jit(solution)/shard_map/dot_general | solution.py:20
  169.2 6.1 %fusion.41 = (f32[1024]{0:T(1024)S(1)}, f32[1024,768]{1,0:T(8,128)S(1)}) fusion(f32[768]{0:T(1024)S(1)} %copy-done.67, bf16[1024,3072]{1,0:T(8,128)(2,1)S(1)} %get-tuple-element.186, bf16[3072,768]{1,0:T(8,128)(2,1)S(1)} %bitcast.226, f32[768]{0:T(1024)} %copy-done.65, f32[768]{0:T(1024)S(1)} %mul.155, f32[1024]{0:T(1024)S(1)} %add_rsqrt_fusion.1, ...), kind=kOutput, calls=%fused_computation.265 | convolution fusion | flops 4837342208 | bytes 17323008 | tf_op jit(solution)/shard_map/dot_general | solution.py:20
  179.9 2.6 gather_fusion.2
  185.6 2.4 collective-permute-start.27
  190.0 3.3 collective-permute-done.27
  193.9 4.1 place_blocks.5
  198.0 3.2 pad_maximum_fusion.1.cols_ref
  201.2 2.5 cross_project.1
  209.2 3.4 collective-permute-done.33
  215.3 2.5 cross_attend.1
  219.2 3.1 collective-permute-done.35
  229.2 3.5 cross_feed.1
  232.8 4.2 collective-permute-done.37
  238.6 4.3 collective-permute-done.38.b_ref
  243.5 4.0 cross_turn.1
  247.6 4.3 collective-permute-done.39
  253.7 4.2 collective-permute-done.40.b_ref
  258.5 2.9 cross_attend_back.1
  264.7 4.2 collective-permute-done.42
  271.1 2.6 collective-permute-done.43.other_ref
  274.3 2.8 cross_project_back.1
  277.1 4.2 collective-permute-done.44
  283.1 4.2 collective-permute-done.45
  287.3 3.2 multiply_reduce_fusion
  290.5 3.7 cross_weight_grads.1
  297.9 2.3 copy-done.5
  300.2 2.4 fusion.29
  303.7 5.5 %convolution_convert_fusion.1 = bf16[3072,768]{1,0:T(8,128)(2,1)S(1)} fusion(bf16[1024,3072]{1,0:T(8,128)(2,1)S(1)} %bitcast.234, bf16[1024,768]{1,0:T(8,128)(2,1)S(1)} %get-tuple-element.228), kind=kOutput, calls=%fused_computation.14 | convolution fusion | flops 4834197504 | bytes 12582912 | tf_op jit(solution)/shard_map/dot_general | solution.py:20
  313.1 8.5 %multiply_convert_fusion = bf16[1024,3072]{1,0:T(8,128)(2,1)S(1)} fusion(bf16[1024,3072]{1,0:T(8,128)(2,1)} %get-tuple-element.229, bf16[1024,768]{1,0:T(8,128)(2,1)} %copy-done.9, bf16[3072,768]{1,0:T(8,128)(2,1)} %bitcast.223), kind=kOutput, calls=%fused_computation.10 | convolution fusion | flops 4841275392 | bytes 18874368 | tf_op jit(solution)/shard_map/dot_general | solution.py:20
  321.7 6.3 %convolution_convert_fusion = bf16[768,3072]{1,0:T(8,128)(2,1)S(1)} fusion(bf16[1024,3072]{1,0:T(8,128)(2,1)S(1)} %multiply_convert_fusion, f32[1024,768]{1,0:T(8,128)S(1)} %copy-done.2, f32[768]{0:T(1024)S(1)} %copy-done.66, f32[768]{0:T(1024)S(1)} %copy-done.55, f32[1024]{0:T(1024)S(1)} %copy-done.57, f32[1024]{0:T(1024)S(1)} %copy-done.46), kind=kOutput, calls=%fused_computation.13 | convolution fusion | flops 4838129664 | bytes 14170112 | tf_op jit(solution)/shard_map/dot_general | solution.py:20
  338.2 3.1 add_convert_fusion.7
  342.9 4.1 add_convert_fusion.4
  348.5 9.2 %convolution_add_fusion = f32[1024,768]{1,0:T(8,128)S(1)} fusion(f32[1024,768]{1,0:T(8,128)} %get-tuple-element.339, bf16[1024,3072]{1,0:T(8,128)(2,1)} %copy-done.6, bf16[768,3072]{1,0:T(8,128)(2,1)} %bitcast.219), kind=kOutput, calls=%fused_computation.53 | convolution fusion | flops 4832624640 | bytes 17301504 | tf_op jit(solution)/shard_map/dot_general | solution.py:20
  357.8 6.9 %collective-permute-done.48 = bf16[2,1,1,312,768]{4,3,2,1,0:T(8,128)(2,1)S(1)} collective-permute-done((bf16[2,1,1,312,768]{4,3,2,1,0:T(8,128)(2,1)}, bf16[2,1,1,312,768]{4,3,2,1,0:T(8,128)(2,1)S(1)}, u32[]{:S(2)}, u32[]{:S(2)}) %collective-permute-start.48) | collective-permute-done | bytes 958496 | tf_op jit(solution)/shard_map/ppermute | solution.py:54
  369.1 2.5 convolution_convert_fusion.5
  371.6 2.6 convolution_convert_fusion.4.grad_ref
  376.0 12.2 %segment_attend_back.2 = (bf16[1024,1152]{1,0:T(8,128)(2,1)}, f32[8,1,1152]{2,1,0:T(1,128)}) custom-call(bf16[1024,1152]{1,0:T(8,128)(2,1)} %add_convert_fusion.1.refs_0_.qkv_ref, bf16[1024,768]{1,0:T(8,128)(2,1)} %convolution_convert_fusion.4.grad_ref), custom_call_target="tpu_custom_call" | custom-call | tf_op jit(solution)/shard_map/segment_attend_back/pallas_call | solution.py:342
  388.2 4.5 add_convert_fusion.3
  394.3 3.9 fusion.42
  398.2 2.2 convolution_convert_fusion.3
  403.9 2.3 add_convert_fusion.9
  407.0 12.0 %segment_attend_back.3 = (bf16[1024,1152]{1,0:T(8,128)(2,1)}, f32[8,1,1152]{2,1,0:T(1,128)}) custom-call(bf16[1024,1152]{1,0:T(8,128)(2,1)} %add_convert_fusion.refs_0_.qkv_ref, bf16[1024,768]{1,0:T(8,128)(2,1)} %convolution_convert_fusion.4.grad_ref), custom_call_target="tpu_custom_call" | custom-call | tf_op jit(solution)/shard_map/segment_attend_back/pallas_call | solution.py:342
  428.0 2.5 add_convert_fusion.10
  431.8 2.3 convolution_convert_fusion.2
  436.7 3.4 add_convert_fusion.2
  449.6 4.8 collective-permute-done.60
  467.6 2.9 collective-permute-done.63
  475.8 4.1 collective-permute-done.72
  480.2 2.5 collective-permute-start.75
  483.5 2.2 collective-permute-done.69
  (537 shorter events, 177.6 us)
Async XLA Ops:
  5.9 10.1 %collective-permute-start = (bf16[1,80,768]{2,1,0:T(8,128)(2,1)S(1)}, bf16[1,80,768]{2,1,0:T(8,128)(2,1)S(1)}, u32[]{:S(2)}, u32[]{:S(2)}) collective-permute-start(bf16[1,80,768]{2,1,0:T(8,128)(2,1)S(1)} %maximum_bitcast_fusion.4), channel_id=1, source_target_pairs={{0,16},{1,17},{2,18},{3,19},{4,20},{5,21},{6,22},{7,23},{8,24},{9,... | collective-permute-start | bytes 368648 | tf_op jit(solution)/shard_map/ppermute | solution.py:54
  16.0 7.2 %collective-permute-start.1 = (bf16[2,80,768]{2,1,0:T(8,128)(2,1)S(1)}, bf16[2,80,768]{2,1,0:T(8,128)(2,1)S(1)}, u32[]{:S(2)}, u32[]{:S(2)}) collective-permute-start(bf16[2,80,768]{2,1,0:T(8,128)(2,1)S(1)} %pad_maximum_fusion.17), channel_id=1, source_target_pairs={{0,8},{1,9},{2,10},{3,11},{4,12},{5,13},{6,14},{7,15},{8,0},{9,1},... | collective-permute-start | bytes 737288 | tf_op jit(solution)/shard_map/ppermute | solution.py:54
  23.3 6.3 %collective-permute-start.3 = (bf16[4,80,384]{2,1,0:T(8,128)(2,1)S(1)}, bf16[4,80,384]{2,1,0:T(8,128)(2,1)S(1)}, u32[]{:S(2)}, u32[]{:S(2)}) collective-permute-start(bf16[4,80,384]{2,1,0:T(8,128)(2,1)S(1)} %get-tuple-element.377), channel_id=1, source_target_pairs={{0,4},{1,5},{2,6},{3,7},{4,0},{5,1},{6,2},{7,3},{8,12},{9,13},{10,... | collective-permute-start | bytes 737288 | tf_op jit(solution)/shard_map/ppermute | solution.py:54
  24.9 6.2 %collective-permute-start.2 = (bf16[4,80,384]{2,1,0:T(8,128)(2,1)S(1)}, bf16[4,80,384]{2,1,0:T(8,128)(2,1)S(1)}, u32[]{:S(2)}, u32[]{:S(2)}) collective-permute-start(bf16[4,80,384]{2,1,0:T(8,128)(2,1)S(1)} %get-tuple-element.378), channel_id=1, source_target_pairs={{0,2},{1,3},{2,0},{3,1},{4,6},{5,7},{6,4},{7,5},{8,10},{9,11},{10,... | collective-permute-start | bytes 737288 | tf_op jit(solution)/shard_map/ppermute | solution.py:54
  26.5 17.1 %collective-permute-start.10 = (bf16[1,216,768]{2,1,0:T(8,128)(2,1)S(1)}, bf16[1,216,768]{2,1,0:T(8,128)(2,1)S(1)}, u32[]{:S(2)}, u32[]{:S(2)}) collective-permute-start(bf16[1,216,768]{2,1,0:T(8,128)(2,1)S(1)} %bitcast.184), channel_id=1, source_target_pairs={{0,16},{1,17},{2,18},{3,19},{4,20},{5,21},{6,22},{7,23},{8,24},{9,... | collective-permute-start | bytes 995336 | tf_op jit(solution)/shard_map/ppermute | solution.py:54
  31.2 13.9 %collective-permute-start.5 = (bf16[8,80,384]{2,1,0:T(8,128)(2,1)S(1)}, bf16[8,80,384]{2,1,0:T(8,128)(2,1)}, u32[]{:S(2)}, u32[]{:S(2)}) collective-permute-start(bf16[8,80,384]{2,1,0:T(8,128)(2,1)S(1)} %pad_maximum_fusion.11.refs_4_), channel_id=1, source_target_pairs={{0,2},{1,3},{2,0},{3,1},{4,6},{5,7},{6,4},{7,5},{8,10},{9,11},{10,... | collective-permute-start | bytes 1474568 | tf_op jit(solution)/shard_map/ppermute | solution.py:54
  32.8 12.3 %collective-permute-start.4 = (bf16[8,80,384]{2,1,0:T(8,128)(2,1)S(1)}, bf16[8,80,384]{2,1,0:T(8,128)(2,1)}, u32[]{:S(2)}, u32[]{:S(2)}) collective-permute-start(bf16[8,80,384]{2,1,0:T(8,128)(2,1)S(1)} %pad_maximum_fusion.10.refs_0_), channel_id=1, source_target_pairs={{0,4},{1,5},{2,6},{3,7},{4,0},{5,1},{6,2},{7,3},{8,12},{9,13},{10,... | collective-permute-start | bytes 1474568 | tf_op jit(solution)/shard_map/ppermute | solution.py:54
  43.6 28.5 %collective-permute-start.11 = (bf16[2,216,768]{2,1,0:T(8,128)(2,1)S(1)}, bf16[2,216,768]{2,1,0:T(8,128)(2,1)S(1)}, u32[]{:S(2)}, u32[]{:S(2)}) collective-permute-start(bf16[2,216,768]{2,1,0:T(8,128)(2,1)S(1)} %pad_maximum_fusion.6), channel_id=1, source_target_pairs={{0,8},{1,9},{2,10},{3,11},{4,12},{5,13},{6,14},{7,15},{8,0},{9,1},... | collective-permute-start | bytes 1990664 | tf_op jit(solution)/shard_map/ppermute | solution.py:54
  44.4 5.7 %collective-permute-start.6 = (bf16[8,80,384]{2,1,0:T(8,128)(2,1)S(1)}, bf16[8,80,384]{2,1,0:T(8,128)(2,1)}, u32[]{:S(2)}, u32[]{:S(2)}) collective-permute-start(bf16[8,80,384]{2,1,0:T(8,128)(2,1)S(1)} %pad_maximum_fusion.10.refs_0_), channel_id=1, source_target_pairs={{0,1},{1,0},{2,3},{3,2},{4,5},{5,4},{6,7},{7,6},{8,9},{9,8},{10,11... | collective-permute-start | bytes 1474568 | tf_op jit(solution)/shard_map/ppermute | solution.py:54
  45.1 4.9 collective-permute-start.7
  46.7 25.4 %collective-permute-start.12 = (bf16[1,2,48,768]{3,2,1,0:T(8,128)(2,1)}, bf16[1,2,48,768]{3,2,1,0:T(8,128)(2,1)}, u32[]{:S(2)}, u32[]{:S(2)}) collective-permute-start(bf16[1,2,48,768]{3,2,1,0:T(8,128)(2,1)} %get-tuple-element.390), channel_id=1, source_target_pairs={{0,16},{1,17},{2,18},{3,19},{4,20},{5,21},{6,22},{7,23},{8,24},{9,... | collective-permute-start | bytes 442376 | tf_op jit(solution)/shard_map/ppermute | solution.py:54
  72.4 16.7 %collective-permute-start.14 = (bf16[4,216,384]{2,1,0:T(8,128)(2,1)S(1)}, bf16[4,216,384]{2,1,0:T(8,128)(2,1)S(1)}, u32[]{:S(2)}, u32[]{:S(2)}) collective-permute-start(bf16[4,216,384]{2,1,0:T(8,128)(2,1)S(1)} %get-tuple-element.364), channel_id=1, source_target_pairs={{0,4},{1,5},{2,6},{3,7},{4,0},{5,1},{6,2},{7,3},{8,12},{9,13},{10,... | collective-permute-start | bytes 1990664 | tf_op jit(solution)/shard_map/ppermute | solution.py:54
  73.0 17.6 %collective-permute-start.13 = (bf16[4,216,384]{2,1,0:T(8,128)(2,1)S(1)}, bf16[4,216,384]{2,1,0:T(8,128)(2,1)}, u32[]{:S(2)}, u32[]{:S(2)}) collective-permute-start(bf16[4,216,384]{2,1,0:T(8,128)(2,1)S(1)} %get-tuple-element.365), channel_id=1, source_target_pairs={{0,2},{1,3},{2,0},{3,1},{4,6},{5,7},{6,4},{7,5},{8,10},{9,11},{10,... | collective-permute-start | bytes 1990664 | tf_op jit(solution)/shard_map/ppermute | solution.py:54
  75.2 13.8 %collective-permute-start.15 = (bf16[2,1,48,768]{3,2,1,0:T(8,128)(2,1)S(1)}, bf16[2,1,48,768]{3,2,1,0:T(8,128)(2,1)S(1)}, u32[]{:S(2)}, u32[]{:S(2)}) collective-permute-start(bf16[2,1,48,768]{3,2,1,0:T(8,128)(2,1)S(1)} %get-tuple-element.388), channel_id=1, source_target_pairs={{0,8},{1,9},{2,10},{3,11},{4,12},{5,13},{6,14},{7,15},{8,0},{9,1},... | collective-permute-start | bytes 442376 | tf_op jit(solution)/shard_map/ppermute | solution.py:54
  94.6 36.3 %collective-permute-start.17 = (bf16[8,216,384]{2,1,0:T(8,128)(2,1)}, bf16[8,216,384]{2,1,0:T(8,128)(2,1)}, u32[]{:S(2)}, u32[]{:S(2)}) collective-permute-start(bf16[8,216,384]{2,1,0:T(8,128)(2,1)} %pad_maximum_fusion.4.refs_4_), channel_id=1, source_target_pairs={{0,2},{1,3},{2,0},{3,1},{4,6},{5,7},{6,4},{7,5},{8,10},{9,11},{10,... | collective-permute-start | bytes 3981320 | tf_op jit(solution)/shard_map/ppermute | solution.py:54
  96.1 34.8 %collective-permute-start.16 = (bf16[8,216,384]{2,1,0:T(8,128)(2,1)S(1)}, bf16[8,216,384]{2,1,0:T(8,128)(2,1)}, u32[]{:S(2)}, u32[]{:S(2)}) collective-permute-start(bf16[8,216,384]{2,1,0:T(8,128)(2,1)S(1)} %pad_maximum_fusion.3.refs_0_), channel_id=1, source_target_pairs={{0,4},{1,5},{2,6},{3,7},{4,0},{5,1},{6,2},{7,3},{8,12},{9,13},{10,... | collective-permute-start | bytes 3981320 | tf_op jit(solution)/shard_map/ppermute | solution.py:54
  100.3 30.6 %collective-permute-start.19 = (bf16[1,312,384]{2,1,0:T(8,128)(2,1)S(1)}, bf16[1,312,384]{2,1,0:T(8,128)(2,1)S(1)}, u32[]{:S(2)}, u32[]{:S(2)}) collective-permute-start(bf16[1,312,384]{2,1,0:T(8,128)(2,1)S(1)} %get-tuple-element.379), channel_id=1, source_target_pairs={{0,4},{1,5},{2,6},{3,7},{4,0},{5,1},{6,2},{7,3},{8,12},{9,13},{10,... | collective-permute-start | bytes 718856 | tf_op jit(solution)/shard_map/ppermute | solution.py:54
  100.9 30.0 %collective-permute-start.18 = (bf16[1,312,384]{2,1,0:T(8,128)(2,1)S(1)}, bf16[1,312,384]{2,1,0:T(8,128)(2,1)S(1)}, u32[]{:S(2)}, u32[]{:S(2)}) collective-permute-start(bf16[1,312,384]{2,1,0:T(8,128)(2,1)S(1)} %get-tuple-element.380), channel_id=1, source_target_pairs={{0,2},{1,3},{2,0},{3,1},{4,6},{5,7},{6,4},{7,5},{8,10},{9,11},{10,... | collective-permute-start | bytes 718856 | tf_op jit(solution)/shard_map/ppermute | solution.py:54
  102.8 37.1 %collective-permute-start.22 = (bf16[8,216,384]{2,1,0:T(8,128)(2,1)}, bf16[8,216,384]{2,1,0:T(8,128)(2,1)}, u32[]{:S(2)}, u32[]{:S(2)}) collective-permute-start(bf16[8,216,384]{2,1,0:T(8,128)(2,1)} %pad_maximum_fusion.4.refs_4_), channel_id=1, source_target_pairs={{0,1},{1,0},{2,3},{3,2},{4,5},{5,4},{6,7},{7,6},{8,9},{9,8},{10,11... | collective-permute-start | bytes 3981320 | tf_op jit(solution)/shard_map/ppermute | solution.py:54
  130.9 9.6 %collective-permute-start.20 = (bf16[8,216,384]{2,1,0:T(8,128)(2,1)S(1)}, bf16[8,216,384]{2,1,0:T(8,128)(2,1)}, u32[]{:S(2)}, u32[]{:S(2)}) collective-permute-start(bf16[8,216,384]{2,1,0:T(8,128)(2,1)S(1)} %pad_maximum_fusion.3.refs_0_), channel_id=1, source_target_pairs={{0,1},{1,0},{2,3},{3,2},{4,5},{5,4},{6,7},{7,6},{8,9},{9,8},{10,11... | collective-permute-start | bytes 3981320 | tf_op jit(solution)/shard_map/ppermute | solution.py:54
  130.9 9.6 %collective-permute-start.21 = (bf16[8,216,384]{2,1,0:T(8,128)(2,1)}, bf16[8,216,384]{2,1,0:T(8,128)(2,1)}, u32[]{:S(2)}, u32[]{:S(2)}) collective-permute-start(bf16[8,216,384]{2,1,0:T(8,128)(2,1)} %collective-permute-done.16.refs_2_), channel_id=1, source_target_pairs={{0,1},{1,0},{2,3},{3,2},{4,5},{5,4},{6,7},{7,6},{8,9},{9,8},{10,11... | collective-permute-start | bytes 3981320 | tf_op jit(solution)/shard_map/ppermute | solution.py:54
  131.5 10.5 %collective-permute-start.23 = (bf16[8,216,384]{2,1,0:T(8,128)(2,1)}, bf16[8,216,384]{2,1,0:T(8,128)(2,1)}, u32[]{:S(2)}, u32[]{:S(2)}) collective-permute-start(bf16[8,216,384]{2,1,0:T(8,128)(2,1)} %collective-permute-done.17.refs_6_), channel_id=1, source_target_pairs={{0,1},{1,0},{2,3},{3,2},{4,5},{5,4},{6,7},{7,6},{8,9},{9,8},{10,11... | collective-permute-start | bytes 3981320 | tf_op jit(solution)/shard_map/ppermute | solution.py:54
  138.6 55.3 %collective-permute-start.30 = (bf16[2,312,384]{2,1,0:T(8,128)(2,1)}, bf16[2,312,384]{2,1,0:T(8,128)(2,1)}, u32[]{:S(2)}, u32[]{:S(2)}) collective-permute-start(bf16[2,312,384]{2,1,0:T(8,128)(2,1)} %pad_maximum_fusion.13.refs_4_), channel_id=1, source_target_pairs={{0,1},{1,0},{2,3},{3,2},{4,5},{5,4},{6,7},{7,6},{8,9},{9,8},{10,11... | collective-permute-start | bytes 1437704 | tf_op jit(solution)/shard_map/ppermute | solution.py:54
  139.9 28.7 %collective-permute-start.25 = (bf16[2,312,384]{2,1,0:T(8,128)(2,1)}, bf16[2,312,384]{2,1,0:T(8,128)(2,1)}, u32[]{:S(2)}, u32[]{:S(2)}) collective-permute-start(bf16[2,312,384]{2,1,0:T(8,128)(2,1)} %pad_maximum_fusion.13.refs_4_), channel_id=1, source_target_pairs={{0,2},{1,3},{2,0},{3,1},{4,6},{5,7},{6,4},{7,5},{8,10},{9,11},{10,... | collective-permute-start | bytes 1437704 | tf_op jit(solution)/shard_map/ppermute | solution.py:54
  140.5 53.4 %collective-permute-start.28 = (bf16[2,312,384]{2,1,0:T(8,128)(2,1)}, bf16[2,312,384]{2,1,0:T(8,128)(2,1)}, u32[]{:S(2)}, u32[]{:S(2)}) collective-permute-start(bf16[2,312,384]{2,1,0:T(8,128)(2,1)} %pad_maximum_fusion.12.refs_0_), channel_id=1, source_target_pairs={{0,1},{1,0},{2,3},{3,2},{4,5},{5,4},{6,7},{7,6},{8,9},{9,8},{10,11... | collective-permute-start | bytes 1437704 | tf_op jit(solution)/shard_map/ppermute | solution.py:54
  140.5 28.0 %collective-permute-start.24 = (bf16[2,312,384]{2,1,0:T(8,128)(2,1)}, bf16[2,312,384]{2,1,0:T(8,128)(2,1)}, u32[]{:S(2)}, u32[]{:S(2)}) collective-permute-start(bf16[2,312,384]{2,1,0:T(8,128)(2,1)} %pad_maximum_fusion.12.refs_0_), channel_id=1, source_target_pairs={{0,4},{1,5},{2,6},{3,7},{4,0},{5,1},{6,2},{7,3},{8,12},{9,13},{10,... | collective-permute-start | bytes 1437704 | tf_op jit(solution)/shard_map/ppermute | solution.py:54
  168.6 25.4 %collective-permute-start.29 = (bf16[2,312,384]{2,1,0:T(8,128)(2,1)}, bf16[2,312,384]{2,1,0:T(8,128)(2,1)}, u32[]{:S(2)}, u32[]{:S(2)}) collective-permute-start(bf16[2,312,384]{2,1,0:T(8,128)(2,1)} %collective-permute-done.24.refs_2_), channel_id=1, source_target_pairs={{0,1},{1,0},{2,3},{3,2},{4,5},{5,4},{6,7},{7,6},{8,9},{9,8},{10,11... | collective-permute-start | bytes 1437704 | tf_op jit(solution)/shard_map/ppermute | solution.py:54
  168.8 25.2 %collective-permute-start.31 = (bf16[2,312,384]{2,1,0:T(8,128)(2,1)}, bf16[2,312,384]{2,1,0:T(8,128)(2,1)}, u32[]{:S(2)}, u32[]{:S(2)}) collective-permute-start(bf16[2,312,384]{2,1,0:T(8,128)(2,1)} %collective-permute-done.25.refs_6_), channel_id=1, source_target_pairs={{0,1},{1,0},{2,3},{3,2},{4,5},{5,4},{6,7},{7,6},{8,9},{9,8},{10,11... | collective-permute-start | bytes 1437704 | tf_op jit(solution)/shard_map/ppermute | solution.py:54
  178.4 6.3 %collective-permute-start.26 = (f32[1,16,768]{2,1,0:T(8,128)}, f32[1,16,768]{2,1,0:T(8,128)}, u32[]{:S(2)}, u32[]{:S(2)}) collective-permute-start(f32[1,16,768]{2,1,0:T(8,128)} %maximum_bitcast_fusion.5), channel_id=1, source_target_pairs={{0,8},{1,9},{2,10},{3,11},{4,12},{5,13},{6,14},{7,15},{8,0},{9,1},... | collective-permute-start | bytes 147464 | tf_op jit(solution)/shard_map/ppermute | solution.py:54
  185.6 7.6 %collective-permute-start.27 = (f32[2,16,768]{2,1,0:T(8,128)S(1)}, f32[2,16,768]{2,1,0:T(8,128)S(1)}, u32[]{:S(2)}, u32[]{:S(2)}) collective-permute-start(f32[2,16,768]{2,1,0:T(8,128)S(1)} %maximum_select_fusion.5), channel_id=1, source_target_pairs={{0,16},{1,17},{2,18},{3,19},{4,20},{5,21},{6,22},{7,23},{8,24},{9,... | collective-permute-start | bytes 294920 | tf_op jit(solution)/shard_map/ppermute | solution.py:54
  223.7 5.6 %collective-permute-start.36 = (bf16[32,768]{1,0:T(8,128)(2,1)}, bf16[32,768]{1,0:T(8,128)(2,1)}, u32[]{:S(2)}, u32[]{:S(2)}) collective-permute-start(bf16[32,768]{1,0:T(8,128)(2,1)} %add_convert_fusion.45.a_ref), channel_id=1, source_target_pairs={{0,16},{1,17},{2,18},{3,19},{4,20},{5,21},{6,22},{7,23},{8,24},{9,... | collective-permute-start | bytes 147464 | tf_op jit(solution)/shard_map/ppermute | solution.py:54
  237.8 5.1 %collective-permute-start.38 = (bf16[32,768]{1,0:T(8,128)(2,1)S(1)}, bf16[32,768]{1,0:T(8,128)(2,1)S(1)}, u32[]{:S(2)}, u32[]{:S(2)}) collective-permute-start(bf16[32,768]{1,0:T(8,128)(2,1)S(1)} %add_convert_fusion.44.a_ref), channel_id=1, source_target_pairs={{0,16},{1,17},{2,18},{3,19},{4,20},{5,21},{6,22},{7,23},{8,24},{9,... | collective-permute-start | bytes 147464 | tf_op jit(solution)/shard_map/ppermute | solution.py:54
  252.7 5.2 %collective-permute-start.40 = (bf16[32,768]{1,0:T(8,128)(2,1)S(1)}, bf16[32,768]{1,0:T(8,128)(2,1)S(1)}, u32[]{:S(2)}, u32[]{:S(2)}) collective-permute-start(bf16[32,768]{1,0:T(8,128)(2,1)S(1)} %add_convert_fusion.43.a_ref), channel_id=1, source_target_pairs={{0,16},{1,17},{2,18},{3,19},{4,20},{5,21},{6,22},{7,23},{8,24},{9,... | collective-permute-start | bytes 147464 | tf_op jit(solution)/shard_map/ppermute | solution.py:54
  264.0 4.9 collective-permute-start.42
  282.2 5.1 %collective-permute-start.45 = (bf16[32,768]{1,0:T(8,128)(2,1)S(1)}, bf16[32,768]{1,0:T(8,128)(2,1)S(1)}, u32[]{:S(2)}, u32[]{:S(2)}) collective-permute-start(bf16[32,768]{1,0:T(8,128)(2,1)S(1)} %add_convert_fusion.42), channel_id=1, source_target_pairs={{0,16},{1,17},{2,18},{3,19},{4,20},{5,21},{6,22},{7,23},{8,24},{9,... | collective-permute-start | bytes 147464 | tf_op jit(solution)/shard_map/ppermute | solution.py:54
  297.8 11.4 %collective-permute-start.46 = (bf16[2,2,1,312,768]{4,3,2,1,0:T(8,128)(2,1)S(1)}, bf16[2,2,1,312,768]{4,3,2,1,0:T(8,128)(2,1)S(1)}, u32[]{:S(2)}, u32[]{:S(2)}) collective-permute-start(bf16[2,2,1,312,768]{4,3,2,1,0:T(8,128)(2,1)S(1)} %constant_dynamic-slice_fusion.12), channel_id=1, source_target_pairs={{0,1},{1,0},{2,3},{3,2},{4,5},{5,4},{6,7},{7,6},{8,9},{9,8},{10,11... | collective-permute-start | bytes 5750792 | tf_op jit(solution)/shard_map/ppermute | solution.py:54
  313.0 8.6 %collective-permute-start.47 = (bf16[2,2,2,2,1,96,768]{6,5,4,3,2,1,0:T(8,128)(2,1)}, bf16[2,2,2,2,1,96,768]{6,5,4,3,2,1,0:T(8,128)(2,1)}, u32[]{:S(2)}, u32[]{:S(2)}) collective-permute-start(bf16[2,2,2,2,1,96,768]{6,5,4,3,2,1,0:T(8,128)(2,1)} %constant_dynamic-slice_fusion.11), channel_id=1, source_target_pairs={{0,1},{1,0},{2,3},{3,2},{4,5},{5,4},{6,7},{7,6},{8,9},{9,8},{10,11... | collective-permute-start | bytes 7077896 | tf_op jit(solution)/shard_map/ppermute | solution.py:54
  329.8 34.9 %collective-permute-start.49 = (bf16[2,2,2,2,1,24,3072]{6,5,4,3,2,1,0:T(8,128)(2,1)}, bf16[2,2,2,2,1,24,3072]{6,5,4,3,2,1,0:T(8,128)(2,1)}, u32[]{:S(2)}, u32[]{:S(2)}) collective-permute-start(bf16[2,2,2,2,1,24,3072]{6,5,4,3,2,1,0:T(8,128)(2,1)} %constant_dynamic-slice_fusion.10), channel_id=1, source_target_pairs={{0,1},{1,0},{2,3},{3,2},{4,5},{5,4},{6,7},{7,6},{8,9},{9,8},{10,11... | collective-permute-start | bytes 7077896 | tf_op jit(solution)/shard_map/ppermute | solution.py:54
  341.4 23.3 %collective-permute-start.48 = (bf16[2,1,1,312,768]{4,3,2,1,0:T(8,128)(2,1)}, bf16[2,1,1,312,768]{4,3,2,1,0:T(8,128)(2,1)S(1)}, u32[]{:S(2)}, u32[]{:S(2)}) collective-permute-start(bf16[2,1,1,312,768]{4,3,2,1,0:T(8,128)(2,1)} %get-tuple-element.351), channel_id=1, source_target_pairs={{0,2},{1,3},{2,0},{3,1},{4,6},{5,7},{6,4},{7,5},{8,10},{9,11},{10,... | collective-permute-start | bytes 2875400 | tf_op jit(solution)/shard_map/ppermute | solution.py:54
  346.9 47.3 %collective-permute-start.50 = (bf16[2,2,1,2,1,96,768]{6,5,4,3,2,1,0:T(8,128)(2,1)}, bf16[2,2,1,2,1,96,768]{6,5,4,3,2,1,0:T(8,128)(2,1)}, u32[]{:S(2)}, u32[]{:S(2)}) collective-permute-start(bf16[2,2,1,2,1,96,768]{6,5,4,3,2,1,0:T(8,128)(2,1)} %get-tuple-element.349), channel_id=1, source_target_pairs={{0,4},{1,5},{2,6},{3,7},{4,0},{5,1},{6,2},{7,3},{8,12},{9,13},{10,... | collective-permute-start | bytes 3538952 | tf_op jit(solution)/shard_map/ppermute | solution.py:54
  367.4 26.9 %collective-permute-start.51 = (bf16[1,1,1,312,768]{4,3,2,1,0:T(8,128)(2,1)}, bf16[1,1,1,312,768]{4,3,2,1,0:T(8,128)(2,1)}, u32[]{:S(2)}, u32[]{:S(2)}) collective-permute-start(bf16[1,1,1,312,768]{4,3,2,1,0:T(8,128)(2,1)} %add_convert_fusion.15), channel_id=1, source_target_pairs={{0,4},{1,5},{2,6},{3,7},{4,0},{5,1},{6,2},{7,3},{8,12},{9,13},{10,... | collective-permute-start | bytes 1437704 | tf_op jit(solution)/shard_map/ppermute | solution.py:54
  392.7 29.2 %collective-permute-start.52 = (bf16[2,2,2,1,1,24,3072]{6,5,4,3,2,1,0:T(8,128)(2,1)}, bf16[2,2,2,1,1,24,3072]{6,5,4,3,2,1,0:T(8,128)(2,1)}, u32[]{:S(2)}, u32[]{:S(2)}) collective-permute-start(bf16[2,2,2,1,1,24,3072]{6,5,4,3,2,1,0:T(8,128)(2,1)} %get-tuple-element.347), channel_id=1, source_target_pairs={{0,2},{1,3},{2,0},{3,1},{4,6},{5,7},{6,4},{7,5},{8,10},{9,11},{10,... | collective-permute-start | bytes 3538952 | tf_op jit(solution)/shard_map/ppermute | solution.py:54
  402.1 19.7 %collective-permute-start.55 = (bf16[1,2,48,768]{3,2,1,0:T(8,128)(2,1)S(1)}, bf16[1,2,48,768]{3,2,1,0:T(8,128)(2,1)S(1)}, u32[]{:S(2)}, u32[]{:S(2)}) collective-permute-start(bf16[1,2,48,768]{3,2,1,0:T(8,128)(2,1)S(1)} %get-tuple-element.386), channel_id=1, source_target_pairs={{0,16},{1,17},{2,18},{3,19},{4,20},{5,21},{6,22},{7,23},{8,24},{9,... | collective-permute-start | bytes 442376 | tf_op jit(solution)/shard_map/ppermute | solution.py:54
  403.9 18.1 %collective-permute-start.53 = (bf16[2,2,2,2,1,24,1152]{6,5,4,3,2,1,0:T(8,128)(2,1)}, bf16[2,2,2,2,1,24,1152]{6,5,4,3,2,1,0:T(8,128)(2,1)}, u32[]{:S(2)}, u32[]{:S(2)}) collective-permute-start(bf16[2,2,2,2,1,24,1152]{6,5,4,3,2,1,0:T(8,128)(2,1)} %constant_dynamic-slice_fusion.8), channel_id=1, source_target_pairs={{0,1},{1,0},{2,3},{3,2},{4,5},{5,4},{6,7},{7,6},{8,9},{9,8},{10,11... | collective-permute-start | bytes 2654216 | tf_op jit(solution)/shard_map/ppermute | solution.py:54
  406.2 33.9 %collective-permute-start.56 = (bf16[2,2,1,1,1,96,768]{6,5,4,3,2,1,0:T(8,128)(2,1)}, bf16[2,2,1,1,1,96,768]{6,5,4,3,2,1,0:T(8,128)(2,1)}, u32[]{:S(2)}, u32[]{:S(2)}) collective-permute-start(bf16[2,2,1,1,1,96,768]{6,5,4,3,2,1,0:T(8,128)(2,1)} %get-tuple-element.357), channel_id=1, source_target_pairs={{0,2},{1,3},{2,0},{3,1},{4,6},{5,7},{6,4},{7,5},{8,10},{9,11},{10,... | collective-permute-start | bytes 1769480 | tf_op jit(solution)/shard_map/ppermute | solution.py:54
  425.9 14.2 %collective-permute-start.58 = (bf16[2,1,48,768]{3,2,1,0:T(8,128)(2,1)S(1)}, bf16[2,1,48,768]{3,2,1,0:T(8,128)(2,1)S(1)}, u32[]{:S(2)}, u32[]{:S(2)}) collective-permute-start(bf16[2,1,48,768]{3,2,1,0:T(8,128)(2,1)S(1)} %get-tuple-element.384), channel_id=1, source_target_pairs={{0,8},{1,9},{2,10},{3,11},{4,12},{5,13},{6,14},{7,15},{8,0},{9,1},... | collective-permute-start | bytes 442376 | tf_op jit(solution)/shard_map/ppermute | solution.py:54
  430.5 19.1 %collective-permute-start.59 = (bf16[2,2,1,1,1,24,3072]{6,5,4,3,2,1,0:T(8,128)(2,1)}, bf16[2,2,1,1,1,24,3072]{6,5,4,3,2,1,0:T(8,128)(2,1)}, u32[]{:S(2)}, u32[]{:S(2)}) collective-permute-start(bf16[2,2,1,1,1,24,3072]{6,5,4,3,2,1,0:T(8,128)(2,1)} %get-tuple-element.359), channel_id=1, source_target_pairs={{0,4},{1,5},{2,6},{3,7},{4,0},{5,1},{6,2},{7,3},{8,12},{9,13},{10,... | collective-permute-start | bytes 1769480 | tf_op jit(solution)/shard_map/ppermute | solution.py:54
  434.2 6.0 %collective-permute-start.57 = (bf16[2,2,2,2,1,24,1152]{6,5,4,3,2,1,0:T(8,128)(2,1)S(1)}, bf16[2,2,2,2,1,24,1152]{6,5,4,3,2,1,0:T(8,128)(2,1)S(1)}, u32[]{:S(2)}, u32[]{:S(2)}) collective-permute-start(bf16[2,2,2,2,1,24,1152]{6,5,4,3,2,1,0:T(8,128)(2,1)S(1)} %constant_dynamic-slice_fusion.4), channel_id=1, source_target_pairs={{0,1},{1,0},{2,3},{3,2},{4,5},{5,4},{6,7},{7,6},{8,9},{9,8},{10,11... | collective-permute-start | bytes 2654216 | tf_op jit(solution)/shard_map/ppermute | solution.py:54
  435.2 19.2 %collective-permute-start.60 = (bf16[2,2,2,1,1,24,1920]{6,5,4,3,2,1,0:T(8,128)(2,1)}, bf16[2,2,2,1,1,24,1920]{6,5,4,3,2,1,0:T(8,128)(2,1)}, u32[]{:S(2)}, u32[]{:S(2)}) collective-permute-start(bf16[2,2,2,1,1,24,1920]{6,5,4,3,2,1,0:T(8,128)(2,1)} %pad_maximum_fusion.5), channel_id=1, source_target_pairs={{0,2},{1,3},{2,0},{3,1},{4,6},{5,7},{6,4},{7,5},{8,10},{9,11},{10,... | collective-permute-start | bytes 2211848 | tf_op jit(solution)/shard_map/ppermute | solution.py:54
  443.1 11.3 %collective-permute-start.61 = (f32[2,12,768]{2,1,0:T(8,128)}, f32[2,12,768]{2,1,0:T(8,128)}, u32[]{:S(2)}, u32[]{:S(2)}) collective-permute-start(f32[2,12,768]{2,1,0:T(8,128)} %pad_maximum_fusion.19), channel_id=1, source_target_pairs={{0,1},{1,0},{2,3},{3,2},{4,5},{5,4},{6,7},{7,6},{8,9},{9,8},{10,11... | collective-permute-start | bytes 221192 | tf_op jit(solution)/shard_map/ppermute | solution.py:54
  448.3 11.7 %collective-permute-start.64 = (bf16[2,1,1,1,1,96,768]{6,5,4,3,2,1,0:T(8,128)(2,1)}, bf16[2,1,1,1,1,96,768]{6,5,4,3,2,1,0:T(8,128)(2,1)S(1)}, u32[]{:S(2)}, u32[]{:S(2)}) collective-permute-start(bf16[2,1,1,1,1,96,768]{6,5,4,3,2,1,0:T(8,128)(2,1)} %get-tuple-element.367), channel_id=1, source_target_pairs={{0,8},{1,9},{2,10},{3,11},{4,12},{5,13},{6,14},{7,15},{8,0},{9,1},... | collective-permute-start | bytes 884744 | tf_op jit(solution)/shard_map/ppermute | solution.py:54
  448.4 12.6 %collective-permute-start.65 = (bf16[2,2,1,2,1,24,1152]{6,5,4,3,2,1,0:T(8,128)(2,1)}, bf16[2,2,1,2,1,24,1152]{6,5,4,3,2,1,0:T(8,128)(2,1)S(1)}, u32[]{:S(2)}, u32[]{:S(2)}) collective-permute-start(bf16[2,2,1,2,1,24,1152]{6,5,4,3,2,1,0:T(8,128)(2,1)} %get-tuple-element.353), channel_id=1, source_target_pairs={{0,4},{1,5},{2,6},{3,7},{4,0},{5,1},{6,2},{7,3},{8,12},{9,13},{10,... | collective-permute-start | bytes 1327112 | tf_op jit(solution)/shard_map/ppermute | solution.py:54
  458.1 9.5 %collective-permute-start.62 = (bf16[2,1,1,1,1,24,3072]{6,5,4,3,2,1,0:T(8,128)(2,1)S(1)}, bf16[2,1,1,1,1,24,3072]{6,5,4,3,2,1,0:T(8,128)(2,1)S(1)}, u32[]{:S(2)}, u32[]{:S(2)}) collective-permute-start(bf16[2,1,1,1,1,24,3072]{6,5,4,3,2,1,0:T(8,128)(2,1)S(1)} %get-tuple-element.369), channel_id=1, source_target_pairs={{0,8},{1,9},{2,10},{3,11},{4,12},{5,13},{6,14},{7,15},{8,0},{9,1},... | collective-permute-start | bytes 884744 | tf_op jit(solution)/shard_map/ppermute | solution.py:54
  459.5 11.0 %collective-permute-start.63 = (bf16[2,2,1,1,1,24,1920]{6,5,4,3,2,1,0:T(8,128)(2,1)S(1)}, bf16[2,2,1,1,1,24,1920]{6,5,4,3,2,1,0:T(8,128)(2,1)S(1)}, u32[]{:S(2)}, u32[]{:S(2)}) collective-permute-start(bf16[2,2,1,1,1,24,1920]{6,5,4,3,2,1,0:T(8,128)(2,1)S(1)} %get-tuple-element.363), channel_id=1, source_target_pairs={{0,4},{1,5},{2,6},{3,7},{4,0},{5,1},{6,2},{7,3},{8,12},{9,13},{10,... | collective-permute-start | bytes 1105928 | tf_op jit(solution)/shard_map/ppermute | solution.py:54
  462.0 9.6 %collective-permute-start.67 = (f32[2,12,768]{2,1,0:T(8,128)S(1)}, f32[2,12,768]{2,1,0:T(8,128)S(1)}, u32[]{:S(2)}, u32[]{:S(2)}) collective-permute-start(f32[2,12,768]{2,1,0:T(8,128)S(1)} %fusion.70), channel_id=1, source_target_pairs={{0,4},{1,5},{2,6},{3,7},{4,0},{5,1},{6,2},{7,3},{8,12},{9,13},{10,... | collective-permute-start | bytes 221192 | tf_op jit(solution)/shard_map/ppermute | solution.py:54
  462.6 17.3 %collective-permute-start.70 = (bf16[1,1,1,1,1,96,768]{6,5,4,3,2,1,0:T(8,128)(2,1)S(1)}, bf16[1,1,1,1,1,96,768]{6,5,4,3,2,1,0:T(8,128)(2,1)S(1)}, u32[]{:S(2)}, u32[]{:S(2)}) collective-permute-start(bf16[1,1,1,1,1,96,768]{6,5,4,3,2,1,0:T(8,128)(2,1)S(1)} %add_convert_fusion.34), channel_id=1, source_target_pairs={{0,16},{1,17},{2,18},{3,19},{4,20},{5,21},{6,22},{7,23},{8,24},{9,... | collective-permute-start | bytes 442376 | tf_op jit(solution)/shard_map/ppermute | solution.py:54
  464.9 15.0 %collective-permute-start.71 = (bf16[2,2,1,1,1,24,1152]{6,5,4,3,2,1,0:T(8,128)(2,1)S(1)}, bf16[2,2,1,1,1,24,1152]{6,5,4,3,2,1,0:T(8,128)(2,1)S(1)}, u32[]{:S(2)}, u32[]{:S(2)}) collective-permute-start(bf16[2,2,1,1,1,24,1152]{6,5,4,3,2,1,0:T(8,128)(2,1)S(1)} %get-tuple-element.371), channel_id=1, source_target_pairs={{0,2},{1,3},{2,0},{3,1},{4,6},{5,7},{6,4},{7,5},{8,10},{9,11},{10,... | collective-permute-start | bytes 663560 | tf_op jit(solution)/shard_map/ppermute | solution.py:54
  471.6 8.3 %collective-permute-start.72 = (f32[2,12,768]{2,1,0:T(8,128)S(1)}, f32[2,12,768]{2,1,0:T(8,128)S(1)}, u32[]{:S(2)}, u32[]{:S(2)}) collective-permute-start(f32[2,12,768]{2,1,0:T(8,128)S(1)} %add.620), channel_id=1, source_target_pairs={{0,8},{1,9},{2,10},{3,11},{4,12},{5,13},{6,14},{7,15},{8,0},{9,1},... | collective-permute-start | bytes 221192 | tf_op jit(solution)/shard_map/ppermute | solution.py:54
  473.4 10.2 %collective-permute-start.68 = (bf16[1,1,1,1,1,24,3072]{6,5,4,3,2,1,0:T(8,128)(2,1)S(1)}, bf16[1,1,1,1,1,24,3072]{6,5,4,3,2,1,0:T(8,128)(2,1)S(1)}, u32[]{:S(2)}, u32[]{:S(2)}) collective-permute-start(bf16[1,1,1,1,1,24,3072]{6,5,4,3,2,1,0:T(8,128)(2,1)S(1)} %add_convert_fusion.35), channel_id=1, source_target_pairs={{0,16},{1,17},{2,18},{3,19},{4,20},{5,21},{6,22},{7,23},{8,24},{9,... | collective-permute-start | bytes 442376 | tf_op jit(solution)/shard_map/ppermute | solution.py:54
  474.0 11.8 %collective-permute-start.69 = (bf16[2,1,1,1,1,24,1920]{6,5,4,3,2,1,0:T(8,128)(2,1)S(1)}, bf16[2,1,1,1,1,24,1920]{6,5,4,3,2,1,0:T(8,128)(2,1)S(1)}, u32[]{:S(2)}, u32[]{:S(2)}) collective-permute-start(bf16[2,1,1,1,1,24,1920]{6,5,4,3,2,1,0:T(8,128)(2,1)S(1)} %get-tuple-element.373), channel_id=1, source_target_pairs={{0,8},{1,9},{2,10},{3,11},{4,12},{5,13},{6,14},{7,15},{8,0},{9,1},... | collective-permute-start | bytes 552968 | tf_op jit(solution)/shard_map/ppermute | solution.py:54
  480.0 7.0 %collective-permute-start.73 = (f32[2,12,768]{2,1,0:T(8,128)S(1)}, f32[2,12,768]{2,1,0:T(8,128)S(1)}, u32[]{:S(2)}, u32[]{:S(2)}) collective-permute-start(f32[2,12,768]{2,1,0:T(8,128)S(1)} %add.625), channel_id=1, source_target_pairs={{0,16},{1,17},{2,18},{3,19},{4,20},{5,21},{6,22},{7,23},{8,24},{9,... | collective-permute-start | bytes 221192 | tf_op jit(solution)/shard_map/ppermute | solution.py:54
  480.2 9.8 %collective-permute-start.75 = (bf16[2,1,1,1,1,24,1152]{6,5,4,3,2,1,0:T(8,128)(2,1)S(1)}, bf16[2,1,1,1,1,24,1152]{6,5,4,3,2,1,0:T(8,128)(2,1)S(1)}, u32[]{:S(2)}, u32[]{:S(2)}) collective-permute-start(bf16[2,1,1,1,1,24,1152]{6,5,4,3,2,1,0:T(8,128)(2,1)S(1)} %get-tuple-element.382), channel_id=1, source_target_pairs={{0,8},{1,9},{2,10},{3,11},{4,12},{5,13},{6,14},{7,15},{8,0},{9,1},... | collective-permute-start | bytes 331784 | tf_op jit(solution)/shard_map/ppermute | solution.py:54
  487.1 6.3 %collective-permute-start.74 = (bf16[1,1,1,1,1,24,1920]{6,5,4,3,2,1,0:T(8,128)(2,1)S(1)}, bf16[1,1,1,1,1,24,1920]{6,5,4,3,2,1,0:T(8,128)(2,1)S(1)}, u32[]{:S(2)}, u32[]{:S(2)}) collective-permute-start(bf16[1,1,1,1,1,24,1920]{6,5,4,3,2,1,0:T(8,128)(2,1)S(1)} %add_convert_fusion.38), channel_id=1, source_target_pairs={{0,16},{1,17},{2,18},{3,19},{4,20},{5,21},{6,22},{7,23},{8,24},{9,... | collective-permute-start | bytes 276488 | tf_op jit(solution)/shard_map/ppermute | solution.py:54
  489.9 5.4 %collective-permute-start.76 = (bf16[1,1,1,1,1,24,1152]{6,5,4,3,2,1,0:T(8,128)(2,1)S(1)}, bf16[1,1,1,1,1,24,1152]{6,5,4,3,2,1,0:T(8,128)(2,1)S(1)}, u32[]{:S(2)}, u32[]{:S(2)}) collective-permute-start(bf16[1,1,1,1,1,24,1152]{6,5,4,3,2,1,0:T(8,128)(2,1)S(1)} %add_convert_fusion.41), channel_id=1, source_target_pairs={{0,16},{1,17},{2,18},{3,19},{4,20},{5,21},{6,22},{7,23},{8,24},{9,... | collective-permute-start | bytes 165896 | tf_op jit(solution)/shard_map/ppermute | solution.py:54
  (102 other events, 777.8 us)
